TPU v7x, 256 devices: a whole 4x4x8 slice. The times are simulated.
256 devices in a mesh: seq: 32 (over x, z), mp: 8 (over y, core).
Axes of the slice: x: 4, y: 4, z: 8, core: 2. Of those that a mesh axis runs over, the one named last changes fastest.
Arguments:
- prompt_hidden: bfloat16 [1024, 4096], P('seq', 'mp'), may hold values from -6 to 6
- recompute_hidden: bfloat16 [1024, 4096], P('seq', 'mp'), may hold values from -6 to 6
- key_cache: bfloat16 [32, 1024, 1024], P('seq', None, 'mp')
- value_cache: bfloat16 [32, 1024, 1024], P('seq', None, 'mp'), may hold values from -6 to 6
- norm_gain: float32 [4096], replicated, may hold values from 0.1 to 1.9
- w_query: bfloat16 [4096, 4096], P(None, 'mp'), may hold values from -0.09375 to 0.09375
- key_weight: bfloat16 [4096, 1024], P(None, 'mp'), may hold values from -0.09375 to 0.09375
- value_weight: bfloat16 [4096, 1024], P(None, 'mp'), may hold values from -0.09375 to 0.09375
- w_out: bfloat16 [4096, 4096], P('mp'), may hold values from -0.375 to 0.375
- passage_owner: int32 [32], replicated, may hold values from 0 to 31
- prompt_slot: int32 [32], replicated, may hold values from 0 to 31, each once
- prompt_length: int32 [32], replicated, may hold values from 1 to 32, 768 in all
- recompute_count: int32 [32], replicated, may hold values from 1 to 32, 768 in all
- recompute_index: int32 [32, 32], replicated, may hold values from 0 to 1023, as said below
Outputs:
- prompt_out: bfloat16 [1024, 4096], P('seq', 'mp')
- recompute_out: bfloat16 [1024, 4096], P('seq', 'mp')
Inputs may be any that keep to these rules, and one draw needn't show every extreme that they name: `recompute_index`: within each row the 32 entries are distinct positions of the passage. `prompt_slot`: each request appears once. `passage_owner`: A request's passages stand in its context in the order of their indices.
All inputs are finite; a program needn't handle non-finite values.
Results may differ from a plain program's by a relative error of at most 0.015.
Values may be sent and summed in bfloat16 or wider, within the bound.
A program may use at most 128 MiB of HBM per device.

v0:
```python
import math

import jax
import jax.numpy as jnp
from jax import lax
from jax.sharding import PartitionSpec as P

HEAD_SIZE = 128


NEGATIVE_FLOOR = -1e30


def layout(
    passage_owner,
    prompt_slot,
    prompt_length,
    recompute_count,
    recompute_index,
    passage_length,
    prompt_rows,
):
    seq_count = passage_owner.shape[0]
    recompute_rows = recompute_index.shape[1]
    indices = jnp.arange(seq_count, dtype=jnp.int32)
    same_owner = passage_owner[:, None] == passage_owner[None, :]
    passage_rank = jnp.sum(
        jnp.where(same_owner & (indices[None, :] < indices[:, None]), 1, 0), axis=1
    ).astype(jnp.int32)
    held_count = jnp.sum(
        jnp.where(passage_owner[None, :] == prompt_slot[:, None], 1, 0), axis=1
    ).astype(jnp.int32)
    prompt_index = jnp.arange(prompt_rows, dtype=jnp.int32)
    slot_index = jnp.arange(recompute_rows, dtype=jnp.int32)
    token_index = jnp.arange(passage_length, dtype=jnp.int32)
    prompt_req = jnp.broadcast_to(prompt_slot[:, None], (seq_count, prompt_rows))
    prompt_pos = held_count[:, None] * passage_length + prompt_index[None, :]
    prompt_live = prompt_index[None, :] < prompt_length[:, None]
    recompute_req = jnp.broadcast_to(passage_owner[:, None], (seq_count, recompute_rows))
    recompute_pos = passage_rank[:, None] * passage_length + recompute_index
    recompute_live = slot_index[None, :] < recompute_count[:, None]
    cached_req = jnp.broadcast_to(passage_owner[:, None], (seq_count, passage_length))
    cached_pos = passage_rank[:, None] * passage_length + token_index[None, :]
    cached_live = jnp.ones((seq_count, passage_length), dtype=bool)
    query_req = jnp.concatenate([prompt_req, recompute_req], axis=1)
    query_pos = jnp.concatenate([prompt_pos, recompute_pos], axis=1)
    query_live = jnp.concatenate([prompt_live, recompute_live], axis=1)
    key_req = jnp.concatenate([cached_req, prompt_req], axis=1)
    key_pos = jnp.concatenate([cached_pos, prompt_pos], axis=1)
    key_live = jnp.concatenate([cached_live, prompt_live], axis=1)
    return (query_req, query_pos, query_live, key_req, key_pos, key_live, passage_rank)


def apply_rotation(vectors, positions):
    half_width = vectors.shape[-1] // 2
    exponent = jnp.arange(half_width).astype(jnp.float32) * (2.0 / vectors.shape[-1])
    frequency = jnp.exp(-exponent * math.log(500000.0))
    angles = positions.astype(jnp.float32)[:, None] * frequency[None, :]
    cosines = jnp.cos(angles)[:, None, :]
    sines = jnp.sin(angles)[:, None, :]
    leading = vectors[..., :half_width]
    trailing = vectors[..., half_width:]
    return jnp.concatenate(
        [leading * cosines - trailing * sines, trailing * cosines + leading * sines], axis=-1
    )


def normalize(rows_in, norm_gain):
    values = rows_in.astype(jnp.float32)
    inverse_rms = lax.rsqrt(jnp.mean(values * values, axis=-1, keepdims=True) + 1e-05)
    return (values * inverse_rms * norm_gain).astype(jnp.bfloat16)


def attend(queries_in, query_req, query_pos, keys_in, values_in, key_req, key_pos, key_live):
    head_total = queries_in.shape[1] // HEAD_SIZE
    score_scale = 1.0 / math.sqrt(HEAD_SIZE)
    visible = (
        (query_req[:, None] == key_req[None, :])
        & (key_pos[None, :] <= query_pos[:, None])
        & key_live[None, :]
    )
    outputs = []
    maxima_list = []
    totals_list = []
    for head_index in range(head_total):
        query_part = queries_in[:, head_index * HEAD_SIZE : (head_index + 1) * HEAD_SIZE]
        scores = (
            lax.dot_general(
                query_part, keys_in, (((1,), (1,)), ((), ())), preferred_element_type=jnp.float32
            )
            * score_scale
        )
        scores = jnp.where(visible, scores, NEGATIVE_FLOOR)
        maxima = jnp.max(scores, axis=1)
        weights = jnp.where(visible, jnp.exp(scores - maxima[:, None]), 0.0)
        totals_list.append(jnp.sum(weights, axis=1))
        maxima_list.append(maxima)
        outputs.append(
            jnp.dot(weights.astype(jnp.bfloat16), values_in, preferred_element_type=jnp.float32)
        )
    return (
        jnp.concatenate(outputs, axis=1),
        jnp.stack(maxima_list, axis=1),
        jnp.stack(totals_list, axis=1),
    )


def merge_parts(earlier, later):
    highest = jnp.maximum(earlier[1], later[1])
    earlier_scale = jnp.exp(earlier[1] - highest)
    later_scale = jnp.exp(later[1] - highest)
    accumulated = earlier[0] * jnp.repeat(earlier_scale, HEAD_SIZE, axis=1) + later[0] * jnp.repeat(
        later_scale, HEAD_SIZE, axis=1
    )
    return (accumulated, highest, later[2] * later_scale)


def local(
    prompt_hidden,
    recompute_hidden,
    key_cache,
    value_cache,
    norm_gain,
    w_query,
    key_weight,
    value_weight,
    w_out,
    passage_owner,
    prompt_slot,
    prompt_length,
    recompute_count,
    recompute_index,
):
    prompt_rows = prompt_hidden.shape[0]
    recompute_rows = recompute_hidden.shape[0]
    query_row_stack = prompt_rows + recompute_rows
    passage_length = key_cache.shape[1]
    local_heads = w_query.shape[1] // HEAD_SIZE
    local_groups = key_weight.shape[1] // HEAD_SIZE
    device = lax.axis_index("seq")
    query_req, query_pos, query_live, key_req, key_pos, key_live, passage_rank = layout(
        passage_owner,
        prompt_slot,
        prompt_length,
        recompute_count,
        recompute_index,
        passage_length,
        prompt_rows,
    )
    own_req = lax.dynamic_index_in_dim(query_req, device, 0, keepdims=False)
    own_pos = lax.dynamic_index_in_dim(query_pos, device, 0, keepdims=False)
    own_live = lax.dynamic_index_in_dim(query_live, device, 0, keepdims=False)
    rows_local = jnp.concatenate([prompt_hidden, recompute_hidden], axis=0)
    full_rows = lax.all_gather(rows_local, "mp", axis=1, tiled=True)
    normalized_hidden = normalize(full_rows, norm_gain)
    query_vectors = (
        apply_rotation(
            jnp.dot(normalized_hidden, w_query, preferred_element_type=jnp.float32).reshape(
                query_row_stack, local_heads, HEAD_SIZE
            ),
            own_pos,
        )
        .astype(jnp.bfloat16)
        .reshape(query_row_stack, local_heads * HEAD_SIZE)
    )
    newest_keys = (
        apply_rotation(
            jnp.dot(normalized_hidden, key_weight, preferred_element_type=jnp.float32).reshape(
                query_row_stack, local_groups, HEAD_SIZE
            ),
            own_pos,
        )
        .astype(jnp.bfloat16)
        .reshape(query_row_stack, local_groups * HEAD_SIZE)
    )
    newest_values = jnp.dot(
        normalized_hidden, value_weight, preferred_element_type=jnp.float32
    ).astype(jnp.bfloat16)
    own_rank = lax.dynamic_index_in_dim(passage_rank, device, 0, keepdims=False)
    position_shift = jnp.full((passage_length,), own_rank * passage_length, jnp.int32)
    shifted_keys = (
        apply_rotation(
            key_cache[0].astype(jnp.float32).reshape(passage_length, local_groups, HEAD_SIZE),
            position_shift,
        )
        .astype(jnp.bfloat16)
        .reshape(passage_length, local_groups * HEAD_SIZE)
    )
    index_row = lax.dynamic_index_in_dim(recompute_index, device, 0, keepdims=False)
    count_here = lax.dynamic_index_in_dim(recompute_count, device, 0, keepdims=False)
    chosen = (index_row[:, None] == jnp.arange(passage_length, dtype=jnp.int32)[None, :]) & (
        jnp.arange(recompute_rows, dtype=jnp.int32)[:, None] < count_here
    )
    replaced = jnp.any(chosen, axis=0)[:, None]
    fresh_pair = jnp.concatenate([newest_keys[prompt_rows:], newest_values[prompt_rows:]], axis=1)
    placed = lax.dot_general(
        chosen.astype(jnp.bfloat16),
        fresh_pair,
        (((0,), (0,)), ((), ())),
        preferred_element_type=jnp.float32,
    ).astype(jnp.bfloat16)
    kv_width = newest_keys.shape[1]
    passage_key_rows = jnp.where(replaced, placed[:, :kv_width], shifted_keys)
    passage_value_rows = jnp.where(replaced, placed[:, kv_width:], value_cache[0])
    resident_keys = jnp.concatenate([passage_key_rows, newest_keys[:prompt_rows]], axis=0)
    resident_values = jnp.concatenate([passage_value_rows, newest_values[:prompt_rows]], axis=0)
    flat_req = key_req.reshape(-1)
    flattened_position = key_pos.reshape(-1)
    flat_live = key_live.reshape(-1)
    starting_state = (
        jnp.zeros((query_row_stack, local_heads * HEAD_SIZE), jnp.float32),
        jnp.full((query_row_stack, local_heads), NEGATIVE_FLOOR, jnp.float32),
        jnp.zeros((query_row_stack, local_heads), jnp.float32),
    )
    partial_value = attend(
        query_vectors,
        own_req,
        own_pos,
        lax.all_gather(resident_keys, "seq", axis=0, tiled=True),
        lax.all_gather(resident_values, "seq", axis=0, tiled=True),
        flat_req,
        flattened_position,
        flat_live,
    )
    accumulated, maxima, totals = merge_parts(starting_state, partial_value)
    safe_totals = jnp.where(totals > 0, totals, 1.0)
    attention = jnp.where(
        own_live[:, None], accumulated / jnp.repeat(safe_totals, HEAD_SIZE, axis=1), 0.0
    ).astype(jnp.bfloat16)
    projected = jnp.dot(attention, w_out, preferred_element_type=jnp.float32)
    combined = lax.psum_scatter(projected, "mp", scatter_dimension=1, tiled=True).astype(
        jnp.bfloat16
    )
    return (combined[:prompt_rows], combined[prompt_rows:])


def solution(mesh):
    return jax.shard_map(
        local,
        mesh=mesh,
        in_specs=(
            P("seq", "mp"),
            P("seq", "mp"),
            P("seq", None, "mp"),
            P("seq", None, "mp"),
            P(),
            P(None, "mp"),
            P(None, "mp"),
            P(None, "mp"),
            P("mp", None),
            P(),
            P(),
            P(),
            P(),
            P(),
        ),
        out_specs=(P("seq", "mp"), P("seq", "mp")),
        check_vma=False,
    )
```

profile of v0, /device:TPU:1, one launch (start us, length us, event | category | flops | bytes accessed | tf_op | source)
XLA Modules:
  0.0 307.5 jit_solution(16897663712811716777)
XLA Ops:
  7.2 0.0 copy-start
  7.2 0.0 all-gather.3.cloned.1.call-start
  7.3 0.9 select_reduce_fusion
  8.2 0.6 dynamic_slice.27
  8.8 0.7 fusion.71
  9.5 0.8 broadcast_add_fusion
  10.3 0.1 iota_add_fusion.1
  10.4 0.8 pad_maximum_fusion.2
  11.1 16.2 %all_gather.9 = bf16[64,4096]{1,0:T(8,128)(2,1)S(1)} all-gather(bf16[64,512]{1,0:T(8,128)(2,1)S(1)} %pad_maximum_fusion.2), channel_id=1, replica_groups=mesh['seq'=32,'mp'=8] {'mp'}, dimensions={1}, use_global_device_ids=true | all-gather | bytes 589824 | tf_op jit(solution)/shard_map/all_gather | solution.py:154
  27.3 0.2 fusion.28
  27.5 1.2 dynamic_slice.26
  28.8 0.6 iota_compare_fusion.4
  29.4 1.1 convolution_bitcast_fusion
  30.5 1.6 convolution_convert_fusion.1
  32.8 1.0 bitcast_convert_fusion
  33.8 0.1 fusion.85
  33.9 0.2 fusion.50
  34.1 0.1 fusion.62
  34.2 0.1 fusion.38
  34.3 0.4 convolution_convert_fusion
  34.7 0.2 fusion.31
  34.9 1.3 slice_select_fusion
  36.3 0.7 pad_maximum_fusion
  37.0 0.0 all-gather.3.cloned.1.call-update
  37.0 0.0 all-gather.5.cloned.1.call-start
  37.0 0.8 pad_maximum_fusion.1
  37.8 0.0 all-gather.5.cloned.1.call-update
  37.8 0.0 reduce-scatter.2.cloned.1.call-start
  37.9 3.1 %fusion.83 = f32[64,512]{1,0:T(8,128)S(1)} fusion(bf16[4096,512]{1,0:T(8,128)(2,1)} %param.19, bf16[64,4096]{1,0:T(8,128)(2,1)S(1)} %all_gather.9, f32[4096]{0:T(1024)S(1)} %copy-done.4, f32[64]{0:T(128)S(1)} %add_rsqrt_fusion), kind=kOutput, calls=%fused_computation.140 | convolution fusion | flops 269484032 | bytes 4866304 | tf_op jit(solution)/shard_map/dot_general | solution.py:158
  41.0 0.2 multiply_cosine_fusion.1
  41.2 0.2 subtract_convert_fusion.1
  41.4 0.1 pad_maximum_fusion.3
  41.5 0.1 iota_add_fusion
  41.6 0.1 le.17
  41.8 0.1 iota_compare_fusion.2
  41.9 0.2 and.27
  42.1 0.1 broadcast_in_dim.66
  42.1 0.1 broadcast_in_dim.68
  42.2 0.1 eq.24
  42.4 0.1 broadcast_in_dim.67
  42.4 0.1 fusion.70
  42.5 0.1 fusion.68
  42.6 94.5 %all-gather.3.cloned.1.call-done = bf16[33792,128]{1,0:T(8,128)(2,1)} async-done(((bf16[1056,128]{1,0:T(8,128)(2,1)}), bf16[33792,128]{1,0:T(8,128)(2,1)}) %all-gather.3.cloned.1.call-update) | async-done | bytes 8650768 | tf_op jit(solution)/shard_map/all_gather | solution.py:219
  137.1 10.6 %fusion.90 = (f32[64]{0:T(128)S(1)}, f32[64,33792]{1,0:T(8,128)}) fusion(bf16[33792,128]{1,0:T(8,128)(2,1)} %all-gather.3.cloned.1.call-done, bf16[64,512]{1,0:T(8,128)(2,1)S(1)} %bitcast.78, pred[33792]{0:T(1024)(128)(4,1)S(1)} %and.27, s32[64]{0:T(128)S(1)} %get-tuple-element.9, s32[33792]{0:T(1024)S(1)} %le.17, s32[33792]{0:T(1024)S(1)} %eq.24, ...), kind=kOutput, calls=%fused_computation.145 | convolution fusion | flops 568786880 | bytes 17623296 | tf_op jit(solution)/shard_map/dot_general | solution.py:88
  147.8 6.1 %fusion.91 = (f32[64]{0:T(128)S(1)}, f32[64,33792]{1,0:T(8,128)}) fusion(bf16[33792,128]{1,0:T(8,128)(2,1)S(1)} %copy-done.9, bf16[64,512]{1,0:T(8,128)(2,1)S(1)} %bitcast.79, pred[33792]{0:T(1024)(128)(4,1)S(1)} %and.27, s32[64]{0:T(128)S(1)} %get-tuple-element.9, s32[33792]{0:T(1024)S(1)} %le.17, s32[33792]{0:T(1024)S(1)} %eq.24, s32[64]{0:T(128)S(1)} %fusion.70), kind=kOutput, calls=%fused_computation.146 | convolution fusion | flops 568786880 | bytes 17623296 | tf_op jit(solution)/shard_map/dot_general | solution.py:88
  153.9 6.0 %fusion.92 = (f32[64]{0:T(128)S(1)}, f32[64,33792]{1,0:T(8,128)}) fusion(bf16[33792,128]{1,0:T(8,128)(2,1)S(1)} %copy-done.9, bf16[64,512]{1,0:T(8,128)(2,1)S(1)} %bitcast.80, pred[33792]{0:T(1024)(128)(4,1)S(1)} %and.27, s32[64]{0:T(128)S(1)} %get-tuple-element.9, s32[33792]{0:T(1024)S(1)} %le.17, s32[33792]{0:T(1024)S(1)} %eq.24, s32[64]{0:T(128)S(1)} %fusion.70), kind=kOutput, calls=%fused_computation.147 | convolution fusion | flops 568786880 | bytes 17623296 | tf_op jit(solution)/shard_map/dot_general | solution.py:88
  159.9 6.2 %fusion.89 = (f32[64]{0:T(128)S(1)}, f32[64,33792]{1,0:T(8,128)S(1)}) fusion(bf16[33792,128]{1,0:T(8,128)(2,1)} %all-gather.3.cloned.1.call-done, bf16[64,512]{1,0:T(8,128)(2,1)S(1)} %bitcast.81, pred[33792]{0:T(1024)(128)(4,1)S(1)} %and.27, s32[64]{0:T(128)S(1)} %get-tuple-element.9, s32[33792]{0:T(1024)S(1)} %le.17, s32[33792]{0:T(1024)S(1)} %eq.24, ...), kind=kOutput, calls=%fused_computation.144 | convolution fusion | flops 568786880 | bytes 17623296 | tf_op jit(solution)/shard_map/dot_general | solution.py:88
  166.0 16.5 %fusion.4 = (f32[64]{0:T(128)S(1)}, f32[64]{0:T(128)S(1)}, f32[64]{0:T(128)S(1)}, f32[64]{0:T(128)S(1)}) fusion(f32[64,33792]{1,0:T(8,128)} %get-tuple-element.36, f32[64]{0:T(128)S(1)} %get-tuple-element.35, pred[33792]{0:T(1024)(128)(4,1)S(1)} %and.27, s32[64]{0:T(128)S(1)} %get-tuple-element.9, s32[33792]{0:T(1024)S(1)} %le.17, s32[33792]{0:T(1024)S(1)} %eq.24, ...), kind=kLoop, calls=%fused_computation.13 | loop fusion | flops 34602752 | bytes 34909696 | tf_op jit(solution)/shard_map/reduce_sum | solution.py:96
  182.6 0.1 copy.19
  182.7 0.1 copy.20
  182.8 0.1 copy.21
  182.9 53.5 %all-gather.5.cloned.1.call-done = bf16[33792,128]{1,0:T(8,128)(2,1)} async-done(((bf16[1056,128]{1,0:T(8,128)(2,1)}), bf16[33792,128]{1,0:T(8,128)(2,1)}) %all-gather.5.cloned.1.call-update) | async-done | bytes 8650768 | tf_op jit(solution)/shard_map/all_gather | solution.py:220
  236.4 9.3 %fusion.14 = f32[64,128]{1,0:T(8,128)S(1)} fusion(bf16[33792,128]{1,0:T(8,128)(2,1)} %all-gather.5.cloned.1.call-done, f32[64,33792]{1,0:T(8,128)} %get-tuple-element.32, f32[64]{0:T(128)S(1)} %get-tuple-element.31, s32[33792]{0:T(1024)S(1)} %le.17, s32[33792]{0:T(1024)S(1)} %eq.24, s32[64]{0:T(128)S(1)} %get-tuple-element.9, s32[64]{0:T(128)S(1)} %fusion.70, ...), kind=kOutput, calls=%fused_computation.22 | convolution fusion | flops 568786944 | bytes 17639168 | tf_op jit(solution)/shard_map/dot_general | solution.py:99
  245.8 9.3 %fusion.16 = f32[64,128]{1,0:T(8,128)S(1)} fusion(bf16[33792,128]{1,0:T(8,128)(2,1)} %all-gather.5.cloned.1.call-done, f32[64,33792]{1,0:T(8,128)} %get-tuple-element.34, f32[64]{0:T(128)S(1)} %get-tuple-element.33, s32[33792]{0:T(1024)S(1)} %le.17, s32[33792]{0:T(1024)S(1)} %eq.24, s32[64]{0:T(128)S(1)} %get-tuple-element.9, s32[64]{0:T(128)S(1)} %fusion.70, ...), kind=kOutput, calls=%fused_computation.23 | convolution fusion | flops 568786944 | bytes 17639168 | tf_op jit(solution)/shard_map/dot_general | solution.py:99
  255.2 6.1 %fusion.18 = f32[64,128]{1,0:T(8,128)S(1)} fusion(bf16[33792,128]{1,0:T(8,128)(2,1)} %all-gather.5.cloned.1.call-done, f32[64,33792]{1,0:T(8,128)S(1)} %bitcast.73, f32[64]{0:T(128)S(1)} %get-tuple-element.35, s32[33792]{0:T(1024)S(1)} %le.17, s32[33792]{0:T(1024)S(1)} %eq.24, s32[64]{0:T(128)S(1)} %get-tuple-element.9, s32[64]{0:T(128)S(1)} %fusion.70, ...), kind=kOutput, calls=%fused_computation.24 | convolution fusion | flops 568786944 | bytes 17639168 | tf_op jit(solution)/shard_map/dot_general | solution.py:99
  261.3 6.2 %fusion.12 = f32[64,128]{1,0:T(8,128)S(1)} fusion(bf16[33792,128]{1,0:T(8,128)(2,1)} %all-gather.5.cloned.1.call-done, f32[64,33792]{1,0:T(8,128)S(1)} %bitcast.71, f32[64]{0:T(128)S(1)} %get-tuple-element.29, s32[33792]{0:T(1024)S(1)} %le.17, s32[33792]{0:T(1024)S(1)} %eq.24, s32[64]{0:T(128)S(1)} %get-tuple-element.9, s32[64]{0:T(128)S(1)} %fusion.70, ...), kind=kOutput, calls=%fused_computation.21 | convolution fusion | flops 568786944 | bytes 17639168 | tf_op jit(solution)/shard_map/dot_general | solution.py:99
  267.5 0.1 broadcast_in_dim.75
  267.6 0.1 broadcast_in_dim.140
  267.8 0.1 broadcast_in_dim.142
  267.9 1.9 fusion.39
  269.8 0.0 reduce-scatter.2.cloned.1.call-update
  269.8 29.6 %reduce-scatter.2.cloned.1.call-done = f32[64,512]{1,0:T(8,128)} async-done(((f32[64,4096]{1,0:T(8,128)}), f32[64,512]{1,0:T(8,128)}) %reduce-scatter.2.cloned.1.call-update) | async-done | bytes 131088 | tf_op jit(solution)/shard_map/reduce_scatter | solution.py:231
  299.4 0.9 convert_element_type.110
  300.4 0.6 fusion.87
  (44 shorter events, 0.3 us)
Async XLA Ops:
  7.2 22.3 %copy-start = (bf16[4096,128]{1,0:T(8,128)(2,1)S(1)}, bf16[4096,128]{1,0:T(8,128)(2,1)}, u32[]{:S(2)}) copy-start(bf16[4096,128]{1,0:T(8,128)(2,1)} %param.20) | copy-start | bytes 3145732
  7.2 30.7 %copy-start.4 = (f32[4096]{0:T(1024)S(1)}, f32[4096]{0:T(1024)}, u32[]{:S(2)}) copy-start(f32[4096]{0:T(1024)} %param.18) | copy-start | bytes 49156
  7.2 129.9 %all-gather.3.cloned.1.call-start = ((), (), s32[]{:S(2)}) async-start(), calls=%async_computation.1 | async-start | bytes 8921088 | tf_op jit(solution)/shard_map/all_gather | solution.py:219
  27.3 14.5 %copy-start.7 = (s32[32]{0:T(128)S(1)}, s32[32]{0:T(128)}, u32[]{:S(2)}) copy-start(s32[32]{0:T(128)} %param.26) | copy-start | bytes 388
  27.3 14.5 %copy-start.8 = (s32[32]{0:T(128)S(1)}, s32[32]{0:T(128)}, u32[]{:S(2)}) copy-start(s32[32]{0:T(128)} %param.25) | copy-start | bytes 388
  27.3 14.7 %copy-start.6 = (s32[32]{0:T(128)S(1)}, s32[32]{0:T(128)}, u32[]{:S(2)}) copy-start(s32[32]{0:T(128)} %param.24) | copy-start | bytes 388
  27.3 14.8 %copy-start.5 = (s32[32]{0:T(128)S(1)}, s32[32]{0:T(128)}, u32[]{:S(2)}) copy-start(s32[32]{0:T(128)} %param.23) | copy-start | bytes 388
  37.0 199.4 %all-gather.5.cloned.1.call-start = ((), (), s32[]{:S(2)}) async-start(), calls=%async_computation.2 | async-start | bytes 8921088 | tf_op jit(solution)/shard_map/all_gather | solution.py:220
  37.8 261.6 %reduce-scatter.2.cloned.1.call-start = ((), (), s32[]{:S(2)}) async-start(), calls=%async_computation.3 | async-start | bytes 1179648 | tf_op jit(solution)/shard_map/reduce_scatter | solution.py:231
  137.1 10.6 %copy-start.9 = (bf16[33792,128]{1,0:T(8,128)(2,1)S(1)}, bf16[33792,128]{1,0:T(8,128)(2,1)}, u32[]{:S(2)}) copy-start(bf16[33792,128]{1,0:T(8,128)(2,1)} %all-gather.3.cloned.1.call-done) | copy-start | bytes 25952260
  166.0 16.5 %copy-start.2 = (f32[64,33792]{1,0:T(8,128)}, f32[64,33792]{1,0:T(8,128)S(1)}, u32[]{:S(2)}) copy-start(f32[64,33792]{1,0:T(8,128)S(1)} %get-tuple-element.30) | copy-start | bytes 25952260
  236.4 18.7 %slice-start.3 = ((s8[8650752]{0:T(1024)(128)(4,1)}), s8[4194304]{0:T(1024)(128)(4,1)S(1)}, s32[]{:S(2)}) async-start(s8[8650752]{0:T(1024)(128)(4,1)} %bitcast.72), calls=%async_computation.7 | async-start | bytes 8388608
  236.4 18.7 %slice-start.4 = ((s8[8650752]{0:T(1024)(128)(4,1)}), s8[4194304]{0:T(1024)(128)(4,1)S(1)}, s32[]{:S(2)}) async-start(s8[8650752]{0:T(1024)(128)(4,1)} %bitcast.72), calls=%async_computation.8 | async-start | bytes 8388608
  245.7 9.4 %slice-start.5 = ((s8[8650752]{0:T(1024)(128)(4,1)}), s8[262144]{0:T(1024)(128)(4,1)S(1)}, s32[]{:S(2)}) async-start(s8[8650752]{0:T(1024)(128)(4,1)} %bitcast.72), calls=%async_computation.9 | async-start | bytes 524288
  245.7 15.5 %slice-start = ((s8[8650752]{0:T(1024)(128)(4,1)}), s8[4194304]{0:T(1024)(128)(4,1)S(1)}, s32[]{:S(2)}) async-start(s8[8650752]{0:T(1024)(128)(4,1)} %bitcast.70), calls=%async_computation.4 | async-start | bytes 8388608
  245.8 15.5 %slice-start.1 = ((s8[8650752]{0:T(1024)(128)(4,1)}), s8[4194304]{0:T(1024)(128)(4,1)S(1)}, s32[]{:S(2)}) async-start(s8[8650752]{0:T(1024)(128)(4,1)} %bitcast.70), calls=%async_computation.5 | async-start | bytes 8388608
  255.2 6.1 %slice-start.2 = ((s8[8650752]{0:T(1024)(128)(4,1)}), s8[262144]{0:T(1024)(128)(4,1)S(1)}, s32[]{:S(2)}) async-start(s8[8650752]{0:T(1024)(128)(4,1)} %bitcast.70), calls=%async_computation.6 | async-start | bytes 524288
  261.3 6.6 %copy-start.3 = (bf16[512,4096]{1,0:T(8,128)(2,1)S(1)}, bf16[512,4096]{1,0:T(8,128)(2,1)}, u32[]{:S(2)}) copy-start(bf16[512,4096]{1,0:T(8,128)(2,1)} %param.22) | copy-start | bytes 12582916
  261.3 39.7 %copy-start.1 = (bf16[4096,128]{1,0:T(8,128)(2,1)S(1)}, bf16[4096,128]{1,0:T(8,128)(2,1)}, u32[]{:S(2)}) copy-start(bf16[4096,128]{1,0:T(8,128)(2,1)} %param.20) | copy-start | bytes 3145732
Sparse Core Ops, SparseCore 0:
  37.1 99.9 all-gather.2
  139.7 96.6 all-gather.4
  269.9 29.4 reduce-scatter.1
where the time goes:
time: 310 us; the launch traced here: 308 us
  waiting for transfers between devices  178 us (57%)
  matrix products  67.8 us (22%)
  other arithmetic  26.2 us (8%)
  blocking collectives  16.2 us (5%)
  between operations  14.8 us (5%)
  local copies, waits for them, and re-layouts  4.59 us (1%)
    all_gather x1, waiting for transfers between devices, local(): lax.all_gather(resident_keys, 'seq', axis=0, tiled=True)  94.5 us
    all_gather x1, waiting for transfers between devices, local(): lax.all_gather(resident_values, 'seq', axis=0, tiled=True)  53.5 us
    dot_general x4, matrix products, attend(): jnp.dot(weights.astype(jnp.bfloat16), values_in, preferred_element_type=j...  30.9 us
    reduce_scatter x1, waiting for transfers between devices, local(): lax.psum_scatter(projected, 'mp', scatter_dimension=1, tiled=True)  29.6 us
    dot_general x4, matrix products, attend(): lax.dot_general(query_part, keys_in, (((1,), (1,)), ((), ())), preferred_...  28.9 us
    reduce_sum x1, other arithmetic, attend(): totals_list.append(jnp.sum(weights, axis=1))  16.5 us
    all_gather x1, blocking collectives, local(): full_rows = lax.all_gather(rows_local, 'mp', axis=1, tiled=True)  16.2 us
  transfers between devices with their start and end apart: 3, of which 3 were waited for; matrix products, arithmetic and copies ran while one was open for 17% of the time, Pallas kernels for 0%

commit v1 on v0

v1 whole, which is shorter than its diff:
```python
import functools
import math

import jax
import jax.numpy as jnp
from jax import lax
from jax.experimental import pallas as pl
from jax.experimental.pallas import tpu as pltpu
from jax.sharding import PartitionSpec as P

HEAD_SIZE = 128
NEGATIVE_FLOOR = -1e30


def apply_rotation(vectors, positions):
    half_width = vectors.shape[-1] // 2
    exponent = jnp.arange(half_width).astype(jnp.float32) * (2.0 / vectors.shape[-1])
    frequency = jnp.exp(-exponent * math.log(500000.0))
    angles = positions.astype(jnp.float32)[:, None] * frequency[None, :]
    cosines = jnp.cos(angles)[:, None, :]
    sines = jnp.sin(angles)[:, None, :]
    leading = vectors[..., :half_width]
    trailing = vectors[..., half_width:]
    return jnp.concatenate(
        [leading * cosines - trailing * sines, trailing * cosines + leading * sines], axis=-1
    )


def normalize(rows_in, norm_gain):
    values = rows_in.astype(jnp.float32)
    inverse_rms = lax.rsqrt(jnp.mean(values * values, axis=-1, keepdims=True) + 1e-05)
    return (values * inverse_rms * norm_gain).astype(jnp.bfloat16)


def passage_kernel(flags_ref, q_ref, k_ref, v_ref, lim_ref, acc_ref, st_ref):
    b = pl.program_id(0)
    flag = flags_ref[b]
    rows = q_ref.shape[1]
    keys = k_ref.shape[0]

    @pl.when(flag == 0)
    def _():
        acc_ref[...] = jnp.zeros_like(acc_ref)
        sub = lax.broadcasted_iota(jnp.int32, st_ref.shape, 1)
        st_ref[...] = jnp.where(sub == 0, NEGATIVE_FLOOR, 0.0).astype(jnp.float32)

    @pl.when(flag > 0)
    def _():
        scores = lax.dot_general(
            q_ref[0], k_ref[...], (((1,), (1,)), ((), ())), preferred_element_type=jnp.float32
        ) * (1.0 / math.sqrt(HEAD_SIZE))
        limit = jnp.where(flag == 2, lim_ref[...], keys - 1)
        token = lax.broadcasted_iota(jnp.int32, (rows, keys), 1)
        scores = jnp.where(token <= limit, scores, NEGATIVE_FLOOR)
        maxima = jnp.max(scores, axis=1, keepdims=True)
        weights = jnp.exp(scores - maxima)
        totals = jnp.sum(weights, axis=1, keepdims=True)
        acc_ref[0] = jnp.dot(
            weights.astype(jnp.bfloat16), v_ref[...], preferred_element_type=jnp.float32
        ).astype(acc_ref.dtype)
        m_row = jnp.transpose(jnp.broadcast_to(maxima, (rows, rows)))[0:8]
        l_row = jnp.transpose(jnp.broadcast_to(totals, (rows, rows)))[0:8]
        sub = lax.broadcasted_iota(jnp.int32, (8, rows), 0)
        st_ref[0] = jnp.where(sub == 0, m_row, jnp.where(sub == 1, l_row, 0.0))


def passage_attention(flags, q_blocks, keys, values, lim):
    nb, rows, _ = q_blocks.shape
    n_keys = keys.shape[0]
    grid_spec = pltpu.PrefetchScalarGridSpec(
        num_scalar_prefetch=1,
        grid=(nb,),
        in_specs=[
            pl.BlockSpec((1, rows, HEAD_SIZE), lambda b, f: (b, 0, 0)),
            pl.BlockSpec((n_keys, HEAD_SIZE), lambda b, f: (0, 0)),
            pl.BlockSpec((n_keys, HEAD_SIZE), lambda b, f: (0, 0)),
            pl.BlockSpec((rows, 1), lambda b, f: (0, 0)),
        ],
        out_specs=[
            pl.BlockSpec((1, rows, HEAD_SIZE), lambda b, f: (b, 0, 0)),
            pl.BlockSpec((1, 8, rows), lambda b, f: (b, 0, 0)),
        ],
    )
    return pl.pallas_call(
        passage_kernel,
        grid_spec=grid_spec,
        out_shape=[
            jax.ShapeDtypeStruct((nb, rows, HEAD_SIZE), jnp.bfloat16),
            jax.ShapeDtypeStruct((nb, 8, rows), jnp.float32),
        ],
    )(flags, q_blocks, keys, values, lim)


def local(
    prompt_hidden,
    recompute_hidden,
    key_cache,
    value_cache,
    norm_gain,
    w_query,
    key_weight,
    value_weight,
    w_out,
    passage_owner,
    prompt_slot,
    prompt_length,
    recompute_count,
    recompute_index,
):
    prompt_rows = prompt_hidden.shape[0]
    recompute_rows = recompute_hidden.shape[0]
    query_rows = prompt_rows + recompute_rows
    passage_length = key_cache.shape[1]
    local_heads = w_query.shape[1] // HEAD_SIZE
    n_seq = passage_owner.shape[0]
    me = lax.axis_index("seq")
    scale = 1.0 / math.sqrt(HEAD_SIZE)

    seq_ids = jnp.arange(n_seq, dtype=jnp.int32)
    same_owner = passage_owner[:, None] == passage_owner[None, :]
    passage_rank = jnp.sum(
        jnp.where(same_owner & (seq_ids[None, :] < seq_ids[:, None]), 1, 0), axis=1
    ).astype(jnp.int32)
    held_count = jnp.sum(
        jnp.where(passage_owner[None, :] == prompt_slot[:, None], 1, 0), axis=1
    ).astype(jnp.int32)
    own_rank = passage_rank[me]
    own_owner = passage_owner[me]
    own_held = held_count[me]
    own_index = lax.dynamic_index_in_dim(recompute_index, me, 0, keepdims=False)
    own_length = prompt_length[me]
    own_count = recompute_count[me]

    prompt_pos = own_held * passage_length + jnp.arange(prompt_rows, dtype=jnp.int32)
    recompute_pos = own_rank * passage_length + own_index
    own_pos = jnp.concatenate([prompt_pos, recompute_pos])
    own_live = jnp.concatenate(
        [
            jnp.arange(prompt_rows, dtype=jnp.int32) < own_length,
            jnp.arange(recompute_rows, dtype=jnp.int32) < own_count,
        ]
    )

    rows_local = jnp.concatenate([prompt_hidden, recompute_hidden], axis=0)
    full_rows = lax.all_gather(rows_local, "mp", axis=1, tiled=True)
    normalized_hidden = normalize(full_rows, norm_gain)
    queries = (
        apply_rotation(
            jnp.dot(normalized_hidden, w_query, preferred_element_type=jnp.float32).reshape(
                query_rows, local_heads, HEAD_SIZE
            ),
            own_pos,
        )
        .astype(jnp.bfloat16)
    )
    fresh_keys = (
        apply_rotation(
            jnp.dot(normalized_hidden, key_weight, preferred_element_type=jnp.float32).reshape(
                query_rows, 1, HEAD_SIZE
            ),
            own_pos,
        )
        .astype(jnp.bfloat16)
        .reshape(query_rows, HEAD_SIZE)
    )
    fresh_values = jnp.dot(
        normalized_hidden, value_weight, preferred_element_type=jnp.float32
    ).astype(jnp.bfloat16)

    position_shift = jnp.full((passage_length,), own_rank * passage_length, jnp.int32)
    shifted_keys = (
        apply_rotation(
            key_cache[0].astype(jnp.float32).reshape(passage_length, 1, HEAD_SIZE),
            position_shift,
        )
        .astype(jnp.bfloat16)
        .reshape(passage_length, HEAD_SIZE)
    )
    chosen = (own_index[:, None] == jnp.arange(passage_length, dtype=jnp.int32)[None, :]) & (
        jnp.arange(recompute_rows, dtype=jnp.int32)[:, None] < own_count
    )
    replaced = jnp.any(chosen, axis=0)[:, None]
    fresh_pair = jnp.concatenate([fresh_keys[prompt_rows:], fresh_values[prompt_rows:]], axis=1)
    placed = lax.dot_general(
        chosen.astype(jnp.bfloat16),
        fresh_pair,
        (((0,), (0,)), ((), ())),
        preferred_element_type=jnp.float32,
    ).astype(jnp.bfloat16)
    passage_keys = jnp.where(replaced, placed[:, :HEAD_SIZE], shifted_keys)
    passage_values = jnp.where(replaced, placed[:, HEAD_SIZE:], value_cache[0])

    all_queries = lax.all_gather(queries, "seq", axis=0, tiled=False)
    q_blocks = all_queries.reshape(n_seq * 2, prompt_rows * local_heads, HEAD_SIZE)
    prompt_flag = jnp.where(prompt_slot == own_owner, 1, 0)
    recompute_flag = jnp.where(
        seq_ids == me, 2, jnp.where((passage_owner == own_owner) & (seq_ids > me), 1, 0)
    )
    flags = jnp.stack([prompt_flag, recompute_flag], axis=1).reshape(-1).astype(jnp.int32)
    lim = jnp.repeat(own_index, local_heads).reshape(-1, 1).astype(jnp.int32)
    acc, stats = passage_attention(flags, q_blocks, passage_keys, passage_values, lim)

    acc = acc.reshape(n_seq, query_rows, local_heads * HEAD_SIZE)
    stats = stats[:, 0:2].reshape(n_seq, 2, 2, prompt_rows * local_heads)
    acc_back = lax.all_to_all(acc, "seq", 0, 0, tiled=True)
    stats_back = lax.all_to_all(stats, "seq", 0, 0, tiled=True)
    part_max = jnp.transpose(stats_back[:, :, 0], (0, 1, 2)).reshape(n_seq, query_rows, local_heads)
    part_tot = stats_back[:, :, 1].reshape(n_seq, query_rows, local_heads)
    part_acc = acc_back.reshape(n_seq, query_rows, local_heads, HEAD_SIZE).astype(jnp.float32)

    pq = queries[:prompt_rows].astype(jnp.float32)
    pk = fresh_keys[:prompt_rows].astype(jnp.float32)
    pv = fresh_values[:prompt_rows].astype(jnp.float32)
    ps = jnp.einsum("qhd,kd->qhk", pq, pk) * scale
    jj = jnp.arange(prompt_rows, dtype=jnp.int32)
    pvis = (jj[None, :] <= jj[:, None]) & (jj[None, :] < own_length)
    ps = jnp.where(pvis[:, None, :], ps, NEGATIVE_FLOOR)
    pmax = jnp.max(ps, axis=-1)
    pw = jnp.where(pvis[:, None, :], jnp.exp(ps - pmax[..., None]), 0.0)
    ptot = jnp.sum(pw, axis=-1)
    pacc = jnp.einsum("qhk,kd->qhd", pw.astype(jnp.bfloat16).astype(jnp.float32), pv)
    loc_max = jnp.concatenate(
        [pmax, jnp.full((recompute_rows, local_heads), NEGATIVE_FLOOR, jnp.float32)]
    )
    loc_tot = jnp.concatenate([ptot, jnp.zeros((recompute_rows, local_heads), jnp.float32)])
    loc_acc = jnp.concatenate(
        [pacc, jnp.zeros((recompute_rows, local_heads, HEAD_SIZE), jnp.float32)]
    )

    highest = jnp.maximum(jnp.max(part_max, axis=0), loc_max)
    part_scale = jnp.exp(part_max - highest[None])
    loc_scale = jnp.exp(loc_max - highest)
    accumulated = jnp.sum(part_acc * part_scale[..., None], axis=0) + loc_acc * loc_scale[..., None]
    totals = jnp.sum(part_tot * part_scale, axis=0) + loc_tot * loc_scale
    safe_totals = jnp.where(totals > 0, totals, 1.0)
    attention = jnp.where(
        own_live[:, None, None], accumulated / safe_totals[..., None], 0.0
    ).astype(jnp.bfloat16).reshape(query_rows, local_heads * HEAD_SIZE)
    projected = jnp.dot(attention, w_out, preferred_element_type=jnp.float32)
    combined = lax.psum_scatter(projected, "mp", scatter_dimension=1, tiled=True).astype(
        jnp.bfloat16
    )
    return (combined[:prompt_rows], combined[prompt_rows:])


def solution(mesh):
    return jax.shard_map(
        local,
        mesh=mesh,
        in_specs=(
            P("seq", "mp"),
            P("seq", "mp"),
            P("seq", None, "mp"),
            P("seq", None, "mp"),
            P(),
            P(None, "mp"),
            P(None, "mp"),
            P(None, "mp"),
            P("mp", None),
            P(),
            P(),
            P(),
            P(),
            P(),
        ),
        out_specs=(P("seq", "mp"), P("seq", "mp")),
        check_vma=False,
    )
```

time: 310 us -> 266 us (0.86)
  the two profiles are of different devices: /device:TPU:1 before, /device:TPU:2 now
where the time goes in v1:
time: 266 us; the launch traced here: 262 us
  waiting for transfers between devices  137 us (52%)
  Pallas kernels  32 us (12%)
  local copies, waits for them, and re-layouts  29.8 us (11%)
  between operations  15.7 us (6%)
  starting transfers between devices  13.9 us (5%)
  blocking collectives  13.6 us (5%)
  other arithmetic  12.9 us (5%)
  matrix products  6.61 us (2%)
    all_gather x1, waiting for transfers between devices, local(): all_queries = lax.all_gather(queries, 'seq', axis=0, tiled=False)  71.1 us
    reduce_scatter x1, waiting for transfers between devices, local(): lax.psum_scatter(projected, 'mp', scatter_dimension=1, tiled=True)  33.4 us
    pallas_call x1, Pallas kernels, passage_attention(): pl.pallas_call(passage_kernel, grid_spec=grid_spec, out_shape=[jax.ShapeD...  32 us
    all_to_all x1, waiting for transfers between devices, local(): acc_back = lax.all_to_all(acc, 'seq', 0, 0, tiled=True)  28.2 us
    all_gather x1, blocking collectives, local(): full_rows = lax.all_gather(rows_local, 'mp', axis=1, tiled=True)  13.6 us
    mul x2, local copies, waits for them, and re-layouts, local(): part_acc * part_scale[..., None]  10.6 us
    all_to_all x1, starting transfers between devices, local(): stats_back = lax.all_to_all(stats, 'seq', 0, 0, tiled=True)  8.4 us
    all_to_all x1, starting transfers between devices, local(): acc_back = lax.all_to_all(acc, 'seq', 0, 0, tiled=True)  5.4 us
  transfers between devices with their start and end apart: 4, of which 4 were waited for; matrix products, arithmetic and copies ran while one was open for 11% of the time, Pallas kernels for 0%

profile of v1, /device:TPU:2, one launch (start us, length us, event | category | flops | bytes accessed | tf_op | source)
XLA Modules:
  0.0 261.7 jit_solution(3289172806355252384)
XLA Ops:
  7.2 0.0 all-gather.2.cloned.1.call-start
  7.3 1.0 select_reduce_fusion.1
  8.3 0.6 dynamic_slice.23
  8.9 0.6 dynamic_slice.22
  10.8 0.8 pad_maximum_fusion
  11.5 13.6 %all_gather.7 = bf16[64,4096]{1,0:T(8,128)(2,1)S(1)} all-gather(bf16[64,512]{1,0:T(8,128)(2,1)S(1)} %pad_maximum_fusion), channel_id=1, replica_groups=mesh['seq'=32,'mp'=8] {'mp'}, dimensions={1}, use_global_device_ids=true | all-gather | bytes 589824 | tf_op jit(solution)/shard_map/all_gather | solution.py:145
  25.2 0.2 fusion.1
  25.4 3.2 %fusion.52 = f32[64,512]{1,0:T(8,128)S(1)} fusion(bf16[4096,512]{1,0:T(8,128)(2,1)} %param.19, bf16[64,4096]{1,0:T(8,128)(2,1)S(1)} %all_gather.7, f32[4096]{0:T(1024)} %param.18, f32[64]{0:T(128)S(1)} %add_rsqrt_fusion), kind=kOutput, calls=%fused_computation.100 | convolution fusion | flops 269484032 | bytes 4866304 | tf_op jit(solution)/shard_map/dot_general | solution.py:149
  28.6 0.1 fusion.54
  28.8 0.7 broadcast_add_fusion
  29.5 0.1 add_convert_fusion.2
  29.6 0.2 multiply_cosine_fusion.1
  29.8 0.7 pad_maximum_fusion.1
  30.6 0.6 dynamic_slice.21
  31.2 0.6 dynamic_slice.20
  31.8 0.6 fusion.45
  32.4 0.1 copy.50
  32.5 0.6 reshape.331.flags_ref
  33.2 0.1 broadcast_in_dim.118
  33.2 0.7 reshape_reshape.4.lim_ref
  34.0 0.3 convolution_convert_fusion.1
  34.3 0.6 iota_compare_fusion.3
  35.1 0.3 convolution_bitcast_fusion
  35.4 0.2 fusion.27
  35.6 0.1 fusion.41
  35.7 0.1 fusion.11
  35.8 0.4 convolution_convert_fusion
  36.3 0.2 fusion.4
  36.5 2.1 slice_select_fusion
  38.6 71.1 %all-gather.2.cloned.1.call-done = bf16[32,64,4,128]{3,1,2,0:T(8,128)(2,1)} async-done(((bf16[1,64,4,128]{3,1,2,0:T(8,128)(2,1)}), bf16[32,64,4,128]{3,1,2,0:T(8,128)(2,1)}) %all-gather.2.cloned.1.call-update) | async-done | bytes 2097168 | tf_op jit(solution)/shard_map/all_gather | solution.py:193
  109.7 4.9 %copy.53 = bf16[32,64,4,128]{3,2,1,0:T(4,128)(2,1)} copy(bf16[32,64,4,128]{3,1,2,0:T(8,128)(2,1)} %all-gather.2.cloned.1.call-done) | data formatting | bytes 4194304 | tf_op jit(solution)/shard_map/all_gather | solution.py:193
  114.6 32.0 %shard_map.149 = (bf16[64,128,128]{2,1,0:T(8,128)(2,1)}, f32[64,8,128]{2,1,0:T(8,128)}) custom-call(s32[64]{0:T(128)} %reshape.331.flags_ref, bf16[64,128,128]{2,1,0:T(8,128)(2,1)} %bitcast.67, bf16[1024,128]{1,0:T(8,128)(2,1)} %get-tuple-element.13.k_ref, bf16[1024,128]{1,0:T(8,128)(2,1)} %get-tuple-element.12.v_ref, s32[128,1]{1,0:T(8,128)} %reshape_reshape.4.lim_ref), custom_call_target="tpu_custom_call" | custom-call | tf_op jit(solution)/shard_map/pallas_call | solution.py:84
  146.6 1.6 slice.71
  148.2 8.4 %all-to-all-start.1 = ((f32[32,2,2,128]{3,2,1,0:T(2,128)}), f32[32,2,2,128]{3,2,1,0:T(2,128)S(1)}, u32[]{:S(2)}, u32[]{:S(2)}) async-start(f32[32,2,2,128]{3,2,1,0:T(2,128)} %bitcast.18), calls=%async_computation.1 | async-start | bytes 131072 | tf_op jit(solution)/shard_map/all_to_all | solution.py:206
  156.7 4.4 %reshape.335 = bf16[32,64,512]{2,1,0:T(8,128)(2,1)} reshape(bf16[64,128,128]{2,1,0:T(8,128)(2,1)} %get-tuple-element.4) | data formatting | bytes 4194304 | tf_op jit(solution)/shard_map/reshape | solution.py:203
  161.1 4.4 %all-to-all-done.1 = f32[32,2,2,128]{3,2,1,0:T(2,128)S(1)} async-done(((f32[32,2,2,128]{3,2,1,0:T(2,128)}), f32[32,2,2,128]{3,2,1,0:T(2,128)S(1)}, u32[]{:S(2)}, u32[]{:S(2)}) %all-to-all-start.1) | async-done | bytes 65568 | tf_op jit(solution)/shard_map/all_to_all | solution.py:206
  165.4 5.4 %all-to-all-start = ((bf16[32,64,512]{2,1,0:T(8,128)(2,1)}), bf16[32,64,512]{2,1,0:T(8,128)(2,1)S(1)}, u32[]{:S(2)}, u32[]{:S(2)}) async-start(bf16[32,64,512]{2,1,0:T(8,128)(2,1)} %reshape.335), calls=%async_computation | async-start | bytes 4194304 | tf_op jit(solution)/shard_map/all_to_all | solution.py:205
  170.8 0.0 reduce-scatter.2.cloned.1.call-start
  170.9 0.6 dynamic_slice.19
  171.5 0.6 iota_compare_fusion.4
  172.2 0.1 pad_add_fusion
  172.3 0.1 fusion.39
  172.3 0.3 fusion.57
  172.6 0.2 fusion.28
  172.8 0.1 fusion.56
  172.9 0.1 reduce_max.21
  173.0 0.1 copy.56
  173.1 0.1 copy.57
  173.2 0.1 sub.47
  173.3 0.1 fusion.34
  173.4 0.1 reduce_sum.64
  173.5 0.1 copy.62
  173.6 0.1 copy.55
  173.7 0.1 subtract_exponential_fusion
  173.8 1.8 copy.58
  175.7 5.1 %mul.250 = f32[32,64,4,128]{3,2,1,0:T(4,128)} broadcast(f32[32,64,4]{2,1,0:T(8,128)} %copy.58), dimensions={0,1,2} | broadcast | bytes 4227072 | tf_op jit(solution)/shard_map/mul | solution.py:233
  180.8 5.5 %mul.251 = f32[32,64,512]{2,1,0:T(8,128)} reshape(f32[32,64,4,128]{3,2,1,0:T(4,128)} %mul.250) | data formatting | bytes 8388608 | tf_op jit(solution)/shard_map/mul | solution.py:233
  186.3 28.2 %all-to-all-done = bf16[32,64,512]{2,1,0:T(8,128)(2,1)S(1)} async-done(((bf16[32,64,512]{2,1,0:T(8,128)(2,1)}), bf16[32,64,512]{2,1,0:T(8,128)(2,1)S(1)}, u32[]{:S(2)}, u32[]{:S(2)}) %all-to-all-start) | async-done | bytes 2097184 | tf_op jit(solution)/shard_map/all_to_all | solution.py:205
  214.5 3.0 %multiply_reduce_fusion = f32[64,512]{1,0:T(8,128)S(1)} fusion(f32[32,64,512]{2,1,0:T(8,128)} %mul.251, bf16[32,64,512]{2,1,0:T(8,128)(2,1)S(1)} %all-to-all-done), kind=kLoop, calls=%fused_computation | loop fusion | flops 3112960 | bytes 6422528 | tf_op jit(solution)/shard_map/reduce_sum | solution.py:233
  217.6 0.4 copy-done.1
  218.0 1.9 fusion.12
  219.8 33.4 %reduce-scatter.2.cloned.1.call-done = f32[64,512]{1,0:T(8,128)} async-done(((f32[64,4096]{1,0:T(8,128)}), f32[64,512]{1,0:T(8,128)}) %reduce-scatter.2.cloned.1.call-update) | async-done | bytes 131088 | tf_op jit(solution)/shard_map/reduce_scatter | solution.py:240
  253.3 0.9 convert_element_type.105
  254.2 0.6 fusion.55
  (42 shorter events, 0.4 us)
Async XLA Ops:
  7.2 26.8 %copy-start = (bf16[4096,128]{1,0:T(8,128)(2,1)S(1)}, bf16[4096,128]{1,0:T(8,128)(2,1)}, u32[]{:S(2)}) copy-start(bf16[4096,128]{1,0:T(8,128)(2,1)} %param.21) | copy-start | bytes 3145732
  7.2 23.4 %copy-start.9 = (s32[32]{0:T(128)S(1)}, s32[32]{0:T(128)}, u32[]{:S(2)}) copy-start(s32[32]{0:T(128)} %param.23) | copy-start | bytes 388
  7.2 24.6 %copy-start.10 = (s32[32]{0:T(128)S(1)}, s32[32]{0:T(128)}, u32[]{:S(2)}) copy-start(s32[32]{0:T(128)} %param.24) | copy-start | bytes 388
  7.2 26.8 %copy-start.6 = (f32[4096]{0:T(1024)S(1)}, f32[4096]{0:T(1024)}, u32[]{:S(2)}) copy-start(f32[4096]{0:T(1024)} %param.18) | copy-start | bytes 49156
  7.2 23.9 %copy-start.13 = (s32[32]{0:T(128)S(1)}, s32[32]{0:T(128)}, u32[]{:S(2)}) copy-start(s32[32]{0:T(128)} %param.26) | copy-start | bytes 388
  7.2 102.5 %all-gather.2.cloned.1.call-start = ((), (), s32[]{:S(2)}) async-start(), calls=%async_computation.3 | async-start | bytes 2162688 | tf_op jit(solution)/shard_map/all_gather | solution.py:193
  25.4 9.7 %copy-start.2 = (bf16[4096,128]{1,0:T(8,128)(2,1)S(1)}, bf16[4096,128]{1,0:T(8,128)(2,1)}, u32[]{:S(2)}) copy-start(bf16[4096,128]{1,0:T(8,128)(2,1)} %param.20) | copy-start | bytes 3145732
  25.4 10.9 %copy-start.3 = (bf16[1,1024,128]{2,1,0:T(8,128)(2,1)S(1)}, bf16[1,1024,128]{2,1,0:T(8,128)(2,1)}, u32[]{:S(2)}) copy-start(bf16[1,1024,128]{2,1,0:T(8,128)(2,1)} %param.16) | copy-start | bytes 786436
  34.3 0.7 copy-start.7
  35.0 79.6 %copy-start.11 = (pred[32]{0:T(512)(128)(4,1)}, pred[32]{0:T(512)(128)(4,1)S(1)}, u32[]{:S(2)}) copy-start(pred[32]{0:T(512)(128)(4,1)S(1)} %iota_compare_fusion.3) | copy-start | bytes 100
  35.6 79.0 %copy-start.4 = (bf16[64,1,64]{2,0,1:T(8,128)(2,1)}, bf16[64,1,64]{2,0,1:T(8,128)(2,1)S(1)}, u32[]{:S(2)}) copy-start(bf16[64,1,64]{2,0,1:T(8,128)(2,1)S(1)} %get-tuple-element.25) | copy-start | bytes 24580
  148.2 17.2 %all-to-all-start.1 = ((f32[32,2,2,128]{3,2,1,0:T(2,128)}), f32[32,2,2,128]{3,2,1,0:T(2,128)S(1)}, u32[]{:S(2)}, u32[]{:S(2)}) async-start(f32[32,2,2,128]{3,2,1,0:T(2,128)} %bitcast.18), calls=%async_computation.1 | async-start | bytes 131072 | tf_op jit(solution)/shard_map/all_to_all | solution.py:206
  156.6 14.3 %copy-start.14 = (s32[32]{0:T(128)S(1)}, s32[32]{0:T(128)}, u32[]{:S(2)}) copy-start(s32[32]{0:T(128)} %param.25) | copy-start | bytes 388
  156.6 15.5 %copy-start.12 = (pred[32]{0:T(512)(128)(4,1)S(1)}, pred[32]{0:T(512)(128)(4,1)}, u32[]{:S(2)}) copy-start(pred[32]{0:T(512)(128)(4,1)} %copy-done.11) | copy-start | bytes 100
  156.6 15.7 %copy-start.5 = (bf16[64,1,64]{2,0,1:T(8,128)(2,1)S(1)}, bf16[64,1,64]{2,0,1:T(8,128)(2,1)}, u32[]{:S(2)}) copy-start(bf16[64,1,64]{2,0,1:T(8,128)(2,1)} %copy-done.4) | copy-start | bytes 24580
  156.6 16.0 %copy-start.8 = (bf16[64,128]{1,0:T(8,128)(2,1)S(1)}, bf16[64,128]{1,0:T(8,128)(2,1)}, u32[]{:S(2)}) copy-start(bf16[64,128]{1,0:T(8,128)(2,1)} %copy-done.7) | copy-start | bytes 49156
  165.4 49.1 %all-to-all-start = ((bf16[32,64,512]{2,1,0:T(8,128)(2,1)}), bf16[32,64,512]{2,1,0:T(8,128)(2,1)S(1)}, u32[]{:S(2)}, u32[]{:S(2)}) async-start(bf16[32,64,512]{2,1,0:T(8,128)(2,1)} %reshape.335), calls=%async_computation | async-start | bytes 4194304 | tf_op jit(solution)/shard_map/all_to_all | solution.py:205
  170.8 82.4 %reduce-scatter.2.cloned.1.call-start = ((), (), s32[]{:S(2)}) async-start(), calls=%async_computation.4 | async-start | bytes 1179648 | tf_op jit(solution)/shard_map/reduce_scatter | solution.py:240
  214.5 3.4 %copy-start.1 = (bf16[512,4096]{1,0:T(8,128)(2,1)S(1)}, bf16[512,4096]{1,0:T(8,128)(2,1)}, u32[]{:S(2)}) copy-start(bf16[512,4096]{1,0:T(8,128)(2,1)} %param.22) | copy-start | bytes 12582916
Sparse Core Ops, SparseCore 0:
  30.7 79.0 all-gather.1
  220.0 33.2 reduce-scatter.1

commit v2 on v1

--- a/solution.py
+++ b/solution.py
@@ -32,63 +32,115 @@
     return (values * inverse_rms * norm_gain).astype(jnp.bfloat16)
 
 
+MESH = pl.DeviceIdType.MESH
+
+
 def passage_kernel(flags_ref, q_ref, k_ref, v_ref, lim_ref, acc_ref, st_ref):
-    b = pl.program_id(0)
-    flag = flags_ref[b]
-    rows = q_ref.shape[1]
+    nb, rows, _ = q_ref.shape
     keys = k_ref.shape[0]
-
-    @pl.when(flag == 0)
-    def _():
-        acc_ref[...] = jnp.zeros_like(acc_ref)
-        sub = lax.broadcasted_iota(jnp.int32, st_ref.shape, 1)
-        st_ref[...] = jnp.where(sub == 0, NEGATIVE_FLOOR, 0.0).astype(jnp.float32)
-
-    @pl.when(flag > 0)
-    def _():
-        scores = lax.dot_general(
-            q_ref[0], k_ref[...], (((1,), (1,)), ((), ())), preferred_element_type=jnp.float32
-        ) * (1.0 / math.sqrt(HEAD_SIZE))
-        limit = jnp.where(flag == 2, lim_ref[...], keys - 1)
-        token = lax.broadcasted_iota(jnp.int32, (rows, keys), 1)
-        scores = jnp.where(token <= limit, scores, NEGATIVE_FLOOR)
-        maxima = jnp.max(scores, axis=1, keepdims=True)
-        weights = jnp.exp(scores - maxima)
-        totals = jnp.sum(weights, axis=1, keepdims=True)
-        acc_ref[0] = jnp.dot(
-            weights.astype(jnp.bfloat16), v_ref[...], preferred_element_type=jnp.float32
-        ).astype(acc_ref.dtype)
-        m_row = jnp.transpose(jnp.broadcast_to(maxima, (rows, rows)))[0:8]
-        l_row = jnp.transpose(jnp.broadcast_to(totals, (rows, rows)))[0:8]
-        sub = lax.broadcasted_iota(jnp.int32, (8, rows), 0)
-        st_ref[0] = jnp.where(sub == 0, m_row, jnp.where(sub == 1, l_row, 0.0))
+    token = lax.broadcasted_iota(jnp.int32, (rows, keys), 1)
+    sub = lax.broadcasted_iota(jnp.int32, (8, rows), 0)
+
+    def body(b, carry):
+        flag = flags_ref[b]
+
+        @pl.when(flag == 0)
+        def _():
+            acc_ref[b] = jnp.zeros((rows, HEAD_SIZE), acc_ref.dtype)
+            st_ref[b] = jnp.where(sub == 0, NEGATIVE_FLOOR, 0.0).astype(jnp.float32)
+
+        @pl.when(flag > 0)
+        def _():
+            scores = lax.dot_general(
+                q_ref[b], k_ref[...], (((1,), (1,)), ((), ())), preferred_element_type=jnp.float32
+            ) * (1.0 / math.sqrt(HEAD_SIZE))
+            limit = jnp.where(flag == 2, lim_ref[...], keys - 1)
+            scores = jnp.where(token <= limit, scores, NEGATIVE_FLOOR)
+            maxima = jnp.max(scores, axis=1, keepdims=True)
+            weights = jnp.exp(scores - maxima)
+            totals = jnp.sum(weights, axis=1, keepdims=True)
+            acc_ref[b] = jnp.dot(
+                weights.astype(jnp.bfloat16), v_ref[...], preferred_element_type=jnp.float32
+            ).astype(acc_ref.dtype)
+            m_row = jnp.transpose(jnp.broadcast_to(maxima, (rows, rows)))[0:8]
+            l_row = jnp.transpose(jnp.broadcast_to(totals, (rows, rows)))[0:8]
+            st_ref[b] = jnp.where(sub == 0, m_row, jnp.where(sub == 1, l_row, 0.0))
+
+        return carry
+
+    lax.fori_loop(0, nb, body, 0)
 
 
 def passage_attention(flags, q_blocks, keys, values, lim):
     nb, rows, _ = q_blocks.shape
-    n_keys = keys.shape[0]
-    grid_spec = pltpu.PrefetchScalarGridSpec(
-        num_scalar_prefetch=1,
-        grid=(nb,),
-        in_specs=[
-            pl.BlockSpec((1, rows, HEAD_SIZE), lambda b, f: (b, 0, 0)),
-            pl.BlockSpec((n_keys, HEAD_SIZE), lambda b, f: (0, 0)),
-            pl.BlockSpec((n_keys, HEAD_SIZE), lambda b, f: (0, 0)),
-            pl.BlockSpec((rows, 1), lambda b, f: (0, 0)),
-        ],
-        out_specs=[
-            pl.BlockSpec((1, rows, HEAD_SIZE), lambda b, f: (b, 0, 0)),
-            pl.BlockSpec((1, 8, rows), lambda b, f: (b, 0, 0)),
-        ],
-    )
+    vmem = pl.BlockSpec(memory_space=pltpu.VMEM)
     return pl.pallas_call(
         passage_kernel,
-        grid_spec=grid_spec,
+        in_specs=[pl.BlockSpec(memory_space=pltpu.SMEM), vmem, vmem, vmem, vmem],
+        out_specs=[vmem, vmem],
         out_shape=[
             jax.ShapeDtypeStruct((nb, rows, HEAD_SIZE), jnp.bfloat16),
             jax.ShapeDtypeStruct((nb, 8, rows), jnp.float32),
         ],
     )(flags, q_blocks, keys, values, lim)
+
+
+def exchange_kernel(n, gather, *refs):
+    count = len(refs) // 2 - 1
+    ins, outs = refs[:count], refs[count : 2 * count]
+    send_sem, recv_sem, local_sem = refs[2 * count :]
+    me = lax.axis_index("seq")
+    mp = lax.axis_index("mp")
+    barrier = pltpu.get_barrier_semaphore()
+    for k in range(1, n):
+        peer = lax.rem(me + k, n)
+        pl.semaphore_signal(barrier, inc=1, device_id=(peer, mp), device_id_type=MESH)
+    pl.semaphore_wait(barrier, n - 1)
+    copies = []
+    for a in range(count):
+        for k in range(1, n):
+            peer = lax.rem(me + k, n)
+            src = ins[a] if gather else ins[a].at[peer]
+            c = pltpu.make_async_remote_copy(
+                src_ref=src,
+                dst_ref=outs[a].at[me],
+                send_sem=send_sem.at[a, k],
+                recv_sem=recv_sem.at[a, k],
+                device_id=(peer, mp),
+                device_id_type=MESH,
+            )
+            c.start()
+            copies.append(c)
+    locals_ = []
+    for a in range(count):
+        src = ins[a] if gather else ins[a].at[me]
+        c = pltpu.make_async_copy(src, outs[a].at[me], local_sem.at[a])
+        c.start()
+        locals_.append(c)
+    for c in copies:
+        c.wait()
+    for c in locals_:
+        c.wait()
+
+
+def exchange(arrays, n, gather, collective_id):
+    count = len(arrays)
+    vmem = pl.BlockSpec(memory_space=pltpu.VMEM)
+    out_shape = [
+        jax.ShapeDtypeStruct(((n,) + x.shape) if gather else x.shape, x.dtype) for x in arrays
+    ]
+    return pl.pallas_call(
+        functools.partial(exchange_kernel, n, gather),
+        in_specs=[vmem] * count,
+        out_specs=[vmem] * count,
+        out_shape=out_shape,
+        scratch_shapes=[
+            pltpu.SemaphoreType.DMA((count, n)),
+            pltpu.SemaphoreType.DMA((count, n)),
+            pltpu.SemaphoreType.DMA((count,)),
+        ],
+        compiler_params=pltpu.CompilerParams(collective_id=collective_id, has_side_effects=True),
+    )(*arrays)
 
 
 def local(
@@ -190,7 +242,9 @@
     passage_keys = jnp.where(replaced, placed[:, :HEAD_SIZE], shifted_keys)
     passage_values = jnp.where(replaced, placed[:, HEAD_SIZE:], value_cache[0])
 
-    all_queries = lax.all_gather(queries, "seq", axis=0, tiled=False)
+    (all_queries,) = exchange(
+        [queries.reshape(2, prompt_rows * local_heads, HEAD_SIZE)], n_seq, True, 0
+    )
     q_blocks = all_queries.reshape(n_seq * 2, prompt_rows * local_heads, HEAD_SIZE)
     prompt_flag = jnp.where(prompt_slot == own_owner, 1, 0)
     recompute_flag = jnp.where(
@@ -200,11 +254,16 @@
     lim = jnp.repeat(own_index, local_heads).reshape(-1, 1).astype(jnp.int32)
     acc, stats = passage_attention(flags, q_blocks, passage_keys, passage_values, lim)
 
-    acc = acc.reshape(n_seq, query_rows, local_heads * HEAD_SIZE)
-    stats = stats[:, 0:2].reshape(n_seq, 2, 2, prompt_rows * local_heads)
-    acc_back = lax.all_to_all(acc, "seq", 0, 0, tiled=True)
-    stats_back = lax.all_to_all(stats, "seq", 0, 0, tiled=True)
-    part_max = jnp.transpose(stats_back[:, :, 0], (0, 1, 2)).reshape(n_seq, query_rows, local_heads)
+    acc_back, stats_back = exchange(
+        [
+            acc.reshape(n_seq, 2, prompt_rows * local_heads, HEAD_SIZE),
+            stats.reshape(n_seq, 2, 8, prompt_rows * local_heads),
+        ],
+        n_seq,
+        False,
+        1,
+    )
+    part_max = stats_back[:, :, 0].reshape(n_seq, query_rows, local_heads)
     part_tot = stats_back[:, :, 1].reshape(n_seq, query_rows, local_heads)
     part_acc = acc_back.reshape(n_seq, query_rows, local_heads, HEAD_SIZE).astype(jnp.float32)
 

time: 266 us -> 224 us (0.84)
  the two profiles are of different devices: /device:TPU:2 before, /device:TPU:1 now
where the time goes in v2:
time: 224 us; the launch traced here: 221 us
  Pallas kernels  127 us (57%)
  waiting for transfers between devices  32.1 us (14%)
  blocking collectives  16.2 us (7%)
  between operations  15.9 us (7%)
  other arithmetic  13.2 us (6%)
  matrix products  8.54 us (4%)
  local copies, waits for them, and re-layouts  8.07 us (4%)
    pallas_call x2, Pallas kernels, exchange(): pl.pallas_call(functools.partial(exchange_kernel, n, gather), in_specs=[v...  119 us
    reduce_scatter x1, waiting for transfers between devices, local(): lax.psum_scatter(projected, 'mp', scatter_dimension=1, tiled=True)  32 us
    all_gather x1, blocking collectives, local(): full_rows = lax.all_gather(rows_local, 'mp', axis=1, tiled=True)  16.2 us
    pallas_call x1, Pallas kernels, passage_attention(): pl.pallas_call(passage_kernel, in_specs=[pl.BlockSpec(memory_space=pltpu....  8.51 us
  transfers between devices with their start and end apart: 1, of which 1 were waited for; matrix products, arithmetic and copies ran while one was open for 0% of the time, Pallas kernels for 0%

profile of v2, /device:TPU:1, one launch (start us, length us, event | category | flops | bytes accessed | tf_op | source)
XLA Modules:
  0.0 221.5 jit_solution(18315138400194168450)
XLA Ops:
  7.2 0.0 copy-start
  7.2 0.0 copy-start.4
  7.2 0.0 reduce-scatter.2.cloned.1.call-start
  7.3 1.3 dynamic_slice.21
  8.6 1.3 dynamic_slice.20
  9.9 1.2 dynamic_slice.19
  11.1 0.9 select_reduce_fusion.1
  12.0 0.6 dynamic_slice.23
  13.3 0.0 copy-start.1
  13.3 0.6 dynamic_slice.22
  14.9 1.3 iota_compare_fusion.3
  16.1 0.1 fusion.38
  16.2 0.8 pad_maximum_fusion
  17.0 16.2 %all_gather.3 = bf16[64,4096]{1,0:T(8,128)(2,1)S(1)} all-gather(bf16[64,512]{1,0:T(8,128)(2,1)S(1)} %pad_maximum_fusion), channel_id=1, replica_groups=mesh['seq'=32,'mp'=8] {'mp'}, dimensions={1}, use_global_device_ids=true | all-gather | bytes 589824 | tf_op jit(solution)/shard_map/all_gather | solution.py:197
  33.1 0.2 fusion.1
  33.4 0.0 copy-done
  33.4 1.1 convolution_convert_fusion.1
  34.5 0.0 copy-start.5
  34.5 0.0 copy-start.6
  34.5 0.0 copy-start.2
  34.5 1.6 convolution_bitcast_fusion
  36.1 0.0 copy-done.4
  36.2 0.0 copy-done.1
  36.2 0.9 fusion.51
  37.1 0.0 copy-start.3
  37.1 0.7 broadcast_add_fusion
  37.8 0.1 add_convert_fusion.2
  37.9 0.2 multiply_cosine_fusion.1
  38.1 0.2 fusion.27
  38.4 0.1 fusion.54
  38.5 0.1 copy.51
  38.6 0.1 copy.52
  38.7 0.1 fusion.40
  38.7 0.3 fusion.56
  39.0 0.2 fusion.28
  39.2 0.0 copy-done.5
  39.2 0.7 fusion.44
  39.9 0.1 pad_add_fusion
  40.0 0.1 fusion.11
  40.1 0.1 copy.48
  40.2 0.6 reshape.307.flags_ref
  40.9 0.1 broadcast_in_dim.118
  40.9 0.7 reshape_reshape.4.lim_ref
  41.7 0.7 pad_maximum_fusion.1.refs_0_
  42.4 58.5 %shard_map.149 = bf16[32,2,128,128]{3,2,1,0:T(8,128)(2,1)} custom-call(bf16[2,128,128]{2,1,0:T(8,128)(2,1)} %pad_maximum_fusion.1.refs_0_), custom_call_target="tpu_custom_call" | custom-call | tf_op jit(solution)/shard_map/pallas_call | solution.py:132
  100.9 0.4 convolution_convert_fusion
  101.4 0.2 fusion.4
  101.6 1.1 slice_select_fusion
  102.7 8.5 %shard_map.150 = (bf16[64,128,128]{2,1,0:T(8,128)(2,1)}, f32[64,8,128]{2,1,0:T(8,128)}) custom-call(s32[64]{0:T(128)} %reshape.307.flags_ref, bf16[64,128,128]{2,1,0:T(8,128)(2,1)} %bitcast.55, bf16[1024,128]{1,0:T(8,128)(2,1)} %get-tuple-element.17.k_ref, bf16[1024,128]{1,0:T(8,128)(2,1)} %get-tuple-element.16.v_ref, s32[128,1]{1,0:T(8,128)} %reshape_reshape.4.lim_ref), custom_call_target="tpu_custom_call" | custom-call | tf_op jit(solution)/shard_map/pallas_call | solution.py:77
  111.2 60.4 %shard_map.151 = (bf16[32,2,128,128]{3,2,1,0:T(8,128)(2,1)}, f32[32,2,8,128]{3,2,1,0:T(8,128)}) custom-call(bf16[32,2,128,128]{3,2,1,0:T(8,128)(2,1)} %bitcast.56, f32[32,2,8,128]{3,2,1,0:T(8,128)} %bitcast.58), custom_call_target="tpu_custom_call" | custom-call | tf_op jit(solution)/shard_map/pallas_call | solution.py:132
  171.7 1.0 fusion.53
  172.7 0.1 reduce_max.21
  172.8 0.1 copy.54
  172.9 0.1 copy.55
  173.0 0.1 sub.42
  173.1 1.1 multiply_reduce_fusion.1
  174.2 0.1 reduce_sum.64
  174.3 0.1 copy.58
  174.4 2.5 %multiply_reduce_fusion = f32[2,128,128]{2,1,0:T(8,128)S(1)} fusion(bf16[32,2,128,128]{3,2,1,0:T(8,128)(2,1)} %get-tuple-element.8, f32[32,2,128]{2,1,0:T(2,128)S(1)} %bitcast.61), kind=kLoop, calls=%fused_computation | loop fusion | flops 3112960 | bytes 2260992 | tf_op jit(solution)/shard_map/reduce_sum | solution.py:292
  176.9 4.1 %fusion.12 = f32[64,4096]{1,0:T(8,128)} fusion(bf16[512,4096]{1,0:T(8,128)(2,1)} %param.22, f32[64,4]{0,1:T(4,128)S(1)} %get-tuple-element.12, f32[64,4]{0,1:T(4,128)S(1)} %get-tuple-element.13, f32[32,4,128]{2,0,1:T(8,128)S(1)} %fusion.28, f32[64,4,128]{2,1,0:T(4,128)S(1)} %bitcast.57, pred[64]{0:T(512)(128)(4,1)S(1)} %pad_add_fusion), kind=kOutput, calls=%fused_computation.27 | convolution fusion | flops 268599296 | bytes 5441600 | tf_op jit(solution)/shard_map/dot_general | solution.py:298
  181.0 0.0 reduce-scatter.2.cloned.1.call-update
  181.0 32.0 %reduce-scatter.2.cloned.1.call-done = f32[64,512]{1,0:T(8,128)} async-done(((f32[64,4096]{1,0:T(8,128)}), f32[64,512]{1,0:T(8,128)}) %reduce-scatter.2.cloned.1.call-update) | async-done | bytes 131088 | tf_op jit(solution)/shard_map/reduce_scatter | solution.py:299
  213.1 0.9 convert_element_type.99
  214.0 0.6 fusion.55
  (16 shorter events, 0.3 us)
Async XLA Ops:
  7.2 26.2 %copy-start = (bf16[4096,128]{1,0:T(8,128)(2,1)S(1)}, bf16[4096,128]{1,0:T(8,128)(2,1)}, u32[]{:S(2)}) copy-start(bf16[4096,128]{1,0:T(8,128)(2,1)} %param.21) | copy-start | bytes 3145732
  7.2 29.0 %copy-start.4 = (f32[4096]{0:T(1024)S(1)}, f32[4096]{0:T(1024)}, u32[]{:S(2)}) copy-start(f32[4096]{0:T(1024)} %param.18) | copy-start | bytes 49156
  7.2 205.9 %reduce-scatter.2.cloned.1.call-start = ((), (), s32[]{:S(2)}) async-start(), calls=%async_computation.1 | async-start | bytes 1179648 | tf_op jit(solution)/shard_map/reduce_scatter | solution.py:299
  13.3 22.9 %copy-start.1 = (bf16[4096,512]{1,0:T(8,128)(2,1)S(1)}, bf16[4096,512]{1,0:T(8,128)(2,1)}, u32[]{:S(2)}) copy-start(bf16[4096,512]{1,0:T(8,128)(2,1)} %param.19) | copy-start | bytes 12582916
  34.5 4.8 %copy-start.5 = (s32[32]{0:T(128)S(1)}, s32[32]{0:T(128)}, u32[]{:S(2)}) copy-start(s32[32]{0:T(128)} %param.23) | copy-start | bytes 388
  34.5 4.8 %copy-start.6 = (s32[32]{0:T(128)S(1)}, s32[32]{0:T(128)}, u32[]{:S(2)}) copy-start(s32[32]{0:T(128)} %param.24) | copy-start | bytes 388
  34.5 7.1 %copy-start.2 = (bf16[1,1024,128]{2,1,0:T(8,128)(2,1)S(1)}, bf16[1,1024,128]{2,1,0:T(8,128)(2,1)}, u32[]{:S(2)}) copy-start(bf16[1,1024,128]{2,1,0:T(8,128)(2,1)} %param.16) | copy-start | bytes 786436
  37.1 64.5 %copy-start.3 = (bf16[1,1024,128]{2,1,0:T(8,128)(2,1)S(1)}, bf16[1,1024,128]{2,1,0:T(8,128)(2,1)}, u32[]{:S(2)}) copy-start(bf16[1,1024,128]{2,1,0:T(8,128)(2,1)} %param.17) | copy-start | bytes 786436
Sparse Core Ops, SparseCore 0:
  181.1 31.8 reduce-scatter.1

commit v3 on v2

--- a/solution.py
+++ b/solution.py
@@ -194,7 +194,11 @@
     )
 
     rows_local = jnp.concatenate([prompt_hidden, recompute_hidden], axis=0)
-    full_rows = lax.all_gather(rows_local, "mp", axis=1, tiled=True)
+    n_mp = w_out.shape[1] // rows_local.shape[1]
+    gathered = lax.all_to_all(
+        jnp.broadcast_to(rows_local[None], (n_mp,) + rows_local.shape), "mp", 0, 0, tiled=True
+    )
+    full_rows = jnp.transpose(gathered, (1, 0, 2)).reshape(query_rows, -1)
     normalized_hidden = normalize(full_rows, norm_gain)
     queries = (
         apply_rotation(
@@ -242,8 +246,9 @@
     passage_keys = jnp.where(replaced, placed[:, :HEAD_SIZE], shifted_keys)
     passage_values = jnp.where(replaced, placed[:, HEAD_SIZE:], value_cache[0])
 
-    (all_queries,) = exchange(
-        [queries.reshape(2, prompt_rows * local_heads, HEAD_SIZE)], n_seq, True, 0
+    own_blocks = queries.reshape(1, 2, prompt_rows * local_heads, HEAD_SIZE)
+    all_queries = lax.all_to_all(
+        jnp.broadcast_to(own_blocks, (n_seq,) + own_blocks.shape[1:]), "seq", 0, 0, tiled=True
     )
     q_blocks = all_queries.reshape(n_seq * 2, prompt_rows * local_heads, HEAD_SIZE)
     prompt_flag = jnp.where(prompt_slot == own_owner, 1, 0)
@@ -254,14 +259,11 @@
     lim = jnp.repeat(own_index, local_heads).reshape(-1, 1).astype(jnp.int32)
     acc, stats = passage_attention(flags, q_blocks, passage_keys, passage_values, lim)
 
-    acc_back, stats_back = exchange(
-        [
-            acc.reshape(n_seq, 2, prompt_rows * local_heads, HEAD_SIZE),
-            stats.reshape(n_seq, 2, 8, prompt_rows * local_heads),
-        ],
-        n_seq,
-        False,
-        1,
+    acc_back = lax.all_to_all(
+        acc.reshape(n_seq, 2, prompt_rows * local_heads, HEAD_SIZE), "seq", 0, 0, tiled=True
+    )
+    stats_back = lax.all_to_all(
+        stats[:, 0:2].reshape(n_seq, 2, 2, prompt_rows * local_heads), "seq", 0, 0, tiled=True
     )
     part_max = stats_back[:, :, 0].reshape(n_seq, query_rows, local_heads)
     part_tot = stats_back[:, :, 1].reshape(n_seq, query_rows, local_heads)
@@ -296,9 +298,8 @@
         own_live[:, None, None], accumulated / safe_totals[..., None], 0.0
     ).astype(jnp.bfloat16).reshape(query_rows, local_heads * HEAD_SIZE)
     projected = jnp.dot(attention, w_out, preferred_element_type=jnp.float32)
-    combined = lax.psum_scatter(projected, "mp", scatter_dimension=1, tiled=True).astype(
-        jnp.bfloat16
-    )
+    pieces = jnp.transpose(projected.reshape(query_rows, n_mp, -1), (1, 0, 2))
+    combined = jnp.sum(lax.all_to_all(pieces, "mp", 0, 0, tiled=True), axis=0).astype(jnp.bfloat16)
     return (combined[:prompt_rows], combined[prompt_rows:])
 
 

time: 224 us -> 195 us (0.87)
  Pallas kernels: 127 us -> 5.46 us
  waiting for transfers between devices: 32.1 us -> 70.5 us
  blocking collectives: 16.2 us -> 41.5 us
  local copies, waits for them, and re-layouts: 8.07 us -> 30.8 us
  starting transfers between devices: 0.04 us -> 21.1 us
  between operations: 15.9 us -> 2.39 us
    pallas_call x2 -> x0, Pallas kernels: 119 us -> none  [exchange(): pl.pallas_call(functools.partial(exchange_kernel, n, gather), in_specs=[v...]
    all_to_all x0 -> x3, waiting for transfers between devices: none -> 70.5 us  [the longest x1 37.1 us: local(): lax.all_to_all(acc.reshape(n_seq, 2, prompt_rows * local_heads, HEAD_SIZE...]
    all_to_all x0 -> x2, blocking collectives: none -> 41.5 us  [the longest x1 24.7 us: local(): lax.all_to_all(pieces, 'mp', 0, 0, tiled=True)]
    reduce_scatter x1 -> x0, waiting for transfers between devices: 32 us -> none  [local(): lax.psum_scatter(projected, 'mp', scatter_dimension=1, tiled=True)]
    all_to_all x0 -> x3, starting transfers between devices: none -> 21.1 us  [the longest x1 10.5 us: local(): lax.all_to_all(jnp.broadcast_to(own_blocks, (n_seq,) + own_blocks.shape[1...]
    all_gather x1 -> x0, blocking collectives: 16.2 us -> none  [local(): full_rows = lax.all_gather(rows_local, 'mp', axis=1, tiled=True)]
    dot_general x0 -> x2, local copies, waits for them, and re-layouts: none -> 12.9 us  [the longest x1 6.46 us: local(): projected = jnp.dot(attention, w_out, preferred_element_type=jnp.float32)]
    pallas_call x1, Pallas kernels: 8.51 us -> 5.46 us  [passage_attention(): pl.pallas_call(passage_kernel, in_specs=[pl.BlockSpec(memory_space=pltpu....]
  transfers between devices with their start and end apart: 1 -> 3, of which waited for: 1 -> 2; matrix products, arithmetic and copies ran while one was open for 0% -> 18% of each run, Pallas kernels for 0% -> 0%
where the time goes in v3:
time: 195 us; the launch traced here: 193 us
  waiting for transfers between devices  70.5 us (36%)
  blocking collectives  41.5 us (21%)
  local copies, waits for them, and re-layouts  30.8 us (16%)
  starting transfers between devices  21.1 us (11%)
  other arithmetic  12.8 us (7%)
  matrix products  8.7 us (4%)
  Pallas kernels  5.46 us (3%)
  between operations  2.39 us (1%)
    all_to_all x1, waiting for transfers between devices, local(): lax.all_to_all(acc.reshape(n_seq, 2, prompt_rows * local_heads, HEAD_SIZE...  37.1 us
    all_to_all x1, waiting for transfers between devices, local(): lax.all_to_all(jnp.broadcast_to(own_blocks, (n_seq,) + own_blocks.shape[1...  33.3 us
    all_to_all x1, blocking collectives, local(): lax.all_to_all(pieces, 'mp', 0, 0, tiled=True)  24.7 us
    all_to_all x1, blocking collectives, local(): lax.all_to_all(stats[:, 0:2].reshape(n_seq, 2, 2, prompt_rows * local_hea...  16.8 us
    all_to_all x1, starting transfers between devices, local(): lax.all_to_all(jnp.broadcast_to(own_blocks, (n_seq,) + own_blocks.shape[1...  10.5 us
    all_to_all x1, starting transfers between devices, local(): lax.all_to_all(jnp.broadcast_to(rows_local[None], (n_mp,) + rows_local.sh...  6.63 us
    dot_general x1, local copies, waits for them, and re-layouts, local(): projected = jnp.dot(attention, w_out, preferred_element_type=jnp.float32)  6.46 us
    dot_general x1, local copies, waits for them, and re-layouts, local(): jnp.dot(normalized_hidden, w_query, preferred_element_type=jnp.float32)  6.42 us
  transfers between devices with their start and end apart: 3, of which 2 were waited for; matrix products, arithmetic and copies ran while one was open for 18% of the time, Pallas kernels for 0%

profile of v3, /device:TPU:1, one launch (start us, length us, event | category | flops | bytes accessed | tf_op | source)
XLA Modules:
  0.0 193.4 jit_solution(11740271823572996305)
XLA Ops:
  0.6 0.9 pad_maximum_fusion
  1.5 0.8 broadcast_in_dim.75
  2.4 6.6 %all-to-all-start = ((bf16[8,64,512]{2,1,0:T(8,128)(2,1)}), bf16[8,64,512]{2,1,0:T(8,128)(2,1)S(1)}, u32[]{:S(2)}, u32[]{:S(2)}) async-start(bf16[8,64,512]{2,1,0:T(8,128)(2,1)} %broadcast_in_dim.75), calls=%async_computation | async-start | bytes 1048576 | tf_op jit(solution)/shard_map/all_to_all | solution.py:198
  9.0 0.9 select_reduce_fusion.1
  9.9 0.6 dynamic_slice.22
  11.2 0.6 dynamic_slice.23
  12.4 0.7 mul.232
  13.2 6.4 %copy.74 = bf16[512,4096]{1,0:T(8,128)(2,1)} copy(bf16[512,4096]{0,1:T(8,128)(2,1)} %bitcast.67) | data formatting | bytes 8388608 | tf_op jit(solution)/shard_map/dot_general | solution.py:205
  19.6 1.3 broadcast_add_fusion
  20.8 0.1 add_convert_fusion.2
  20.9 0.2 multiply_cosine_fusion.1
  21.1 0.2 fusion.1
  21.4 0.2 fusion.4
  21.6 0.4 copy-done.8
  21.9 0.3 copy.60
  22.2 0.2 reshape.344
  22.5 3.6 %fusion.49 = f32[64,4,128]{2,0,1:T(8,128)S(1)} fusion(bf16[64,4096,1]{1,0,2:T(8,128)(2,1)S(1)} %reshape.344, bf16[4,128,4096]{2,1,0:T(8,128)(2,1)} %bitcast.63), kind=kOutput, calls=%fused_computation.102 | convolution fusion | flops 268435456 | bytes 4849664 | tf_op jit(solution)/shard_map/dot_general | solution.py:205
  26.1 0.1 subtract_convert_fusion.1
  26.3 0.1 pad_maximum_fusion.1
  26.4 1.9 broadcast_in_dim.129
  28.3 10.5 %all-to-all-start.1 = ((bf16[32,2,128,128]{3,2,1,0:T(8,128)(2,1)}), bf16[32,2,128,128]{3,2,1,0:T(8,128)(2,1)S(1)}, u32[]{:S(2)}, u32[]{:S(2)}) async-start(bf16[32,2,128,128]{3,2,1,0:T(8,128)(2,1)} %broadcast_in_dim.129), calls=%async_computation.1 | async-start | bytes 4194304 | tf_op jit(solution)/shard_map/all_to_all | solution.py:250
  38.8 1.2 dynamic_slice.21
  40.0 1.3 dynamic_slice.20
  41.3 1.3 fusion.42
  42.7 0.6 pad_add_fusion.1
  43.2 1.4 copy.59
  44.6 1.3 reshape.336.flags_ref
  45.9 1.3 broadcast_in_dim.131
  47.3 1.4 reshape_reshape.4.lim_ref
  48.7 0.8 iota_compare_fusion.3
  49.5 0.8 fusion.12
  50.4 0.2 fusion.5
  50.6 1.2 convert_bitcast_fusion
  51.9 0.1 copy.76
  52.0 0.3 convolution_convert_fusion.1
  52.4 0.3 convolution_bitcast_fusion.1
  52.7 0.2 fusion.22
  52.9 0.1 fusion.38
  53.0 0.4 convolution_convert_fusion
  53.5 1.1 slice_select_fusion
  54.6 33.3 %all-to-all-done.1 = bf16[32,2,128,128]{3,2,1,0:T(8,128)(2,1)S(1)} async-done(((bf16[32,2,128,128]{3,2,1,0:T(8,128)(2,1)}), bf16[32,2,128,128]{3,2,1,0:T(8,128)(2,1)S(1)}, u32[]{:S(2)}, u32[]{:S(2)}) %all-to-all-start.1) | async-done | bytes 2097184 | tf_op jit(solution)/shard_map/all_to_all | solution.py:250
  88.0 1.3 copy-done.1
  89.3 5.5 %shard_map.149 = (bf16[64,128,128]{2,1,0:T(8,128)(2,1)}, f32[64,8,128]{2,1,0:T(8,128)}) custom-call(s32[64]{0:T(128)} %reshape.336.flags_ref, bf16[64,128,128]{2,1,0:T(8,128)(2,1)} %bitcast.66, bf16[1024,128]{1,0:T(8,128)(2,1)} %get-tuple-element.13.k_ref, bf16[1024,128]{1,0:T(8,128)(2,1)} %get-tuple-element.12.v_ref, s32[128,1]{1,0:T(8,128)} %reshape_reshape.4.lim_ref), custom_call_target="tpu_custom_call" | custom-call | tf_op jit(solution)/shard_map/pallas_call | solution.py:77
  94.8 1.0 slice.71
  95.7 16.8 %all_to_all.25 = f32[32,2,2,128]{3,2,1,0:T(2,128)S(1)} all-to-all(f32[32,2,2,128]{3,2,1,0:T(2,128)S(1)} %bitcast.73), channel_id=1, replica_groups=mesh['seq'=32,'mp'=8] {'seq'}, dimensions={0} | all-to-all | bytes 131072 | tf_op jit(solution)/shard_map/all_to_all | solution.py:265
  112.5 4.0 %all-to-all-start.2 = ((bf16[32,2,128,128]{3,2,1,0:T(8,128)(2,1)}), bf16[32,2,128,128]{3,2,1,0:T(8,128)(2,1)S(1)}, u32[]{:S(2)}, u32[]{:S(2)}) async-start(bf16[32,2,128,128]{3,2,1,0:T(8,128)(2,1)} %bitcast.69), calls=%async_computation.2 | async-start | bytes 4194304 | tf_op jit(solution)/shard_map/all_to_all | solution.py:262
  116.6 0.6 dynamic_slice.19
  117.2 6.5 %copy.75 = bf16[4096,512]{1,0:T(8,128)(2,1)} copy(bf16[4096,512]{0,1:T(8,128)(2,1)} %bitcast.68) | data formatting | bytes 8388608 | tf_op jit(solution)/shard_map/dot_general | solution.py:300
  123.6 0.6 iota_compare_fusion.4
  124.3 0.1 pad_add_fusion
  124.4 0.3 fusion.48
  124.7 0.2 fusion.25
  125.0 0.1 reduce_max.21
  125.2 0.1 copy.67
  125.3 0.1 sub.42
  125.4 0.1 fusion.31
  125.5 0.1 reduce_sum.73
  125.7 37.1 %all-to-all-done.2 = bf16[32,2,128,128]{3,2,1,0:T(8,128)(2,1)S(1)} async-done(((bf16[32,2,128,128]{3,2,1,0:T(8,128)(2,1)}), bf16[32,2,128,128]{3,2,1,0:T(8,128)(2,1)S(1)}, u32[]{:S(2)}, u32[]{:S(2)}) %all-to-all-start.2) | async-done | bytes 2097184 | tf_op jit(solution)/shard_map/all_to_all | solution.py:262
  162.9 1.2 multiply_reduce_fusion
  164.1 0.1 fusion.9
  164.4 3.6 %convolution_bitcast_fusion = f32[8,64,512]{2,1,0:T(8,128)S(1)} fusion(bf16[64,512,1]{1,0,2:T(8,128)(2,1)S(1)} %reshape.347, bf16[8,512,512]{2,1,0:T(8,128)(2,1)} %bitcast.62), kind=kOutput, calls=%fused_computation.4 | convolution fusion | flops 268435456 | bytes 5308416 | tf_op jit(solution)/shard_map/dot_general | solution.py:300
  167.9 24.7 %all_to_all.26 = f32[8,64,512]{2,1,0:T(8,128)S(1)} all-to-all(f32[8,64,512]{2,1,0:T(8,128)S(1)} %convolution_bitcast_fusion), channel_id=1, replica_groups=mesh['seq'=32,'mp'=8] {'mp'}, dimensions={0} | all-to-all | bytes 2097152 | tf_op jit(solution)/shard_map/all_to_all | solution.py:302
  192.7 0.1 reduce_sum.75
  192.7 0.6 fusion.47
  (52 shorter events, 0.7 us)
Async XLA Ops:
  0.6 51.3 %copy-start = (bf16[4096,128]{1,0:T(8,128)(2,1)S(1)}, bf16[4096,128]{1,0:T(8,128)(2,1)}, u32[]{:S(2)}) copy-start(bf16[4096,128]{1,0:T(8,128)(2,1)} %param.21) | copy-start | bytes 3145732
  2.4 18.8 %all-to-all-start = ((bf16[8,64,512]{2,1,0:T(8,128)(2,1)}), bf16[8,64,512]{2,1,0:T(8,128)(2,1)S(1)}, u32[]{:S(2)}, u32[]{:S(2)}) async-start(bf16[8,64,512]{2,1,0:T(8,128)(2,1)} %broadcast_in_dim.75), calls=%async_computation | async-start | bytes 1048576 | tf_op jit(solution)/shard_map/all_to_all | solution.py:198
  9.0 11.9 %copy-start.10 = (f32[64]{0:T(128)}, f32[64]{0:T(128)S(1)}, u32[]{:S(2)}) copy-start(f32[64]{0:T(128)S(1)} %multiply_exponential_fusion) | copy-start | bytes 772
  20.9 0.7 copy-start.12
  21.1 4.9 %copy-start.2 = (bf16[8,64,512]{2,1,0:T(8,128)(2,1)}, bf16[8,64,512]{2,1,0:T(8,128)(2,1)S(1)}, u32[]{:S(2)}) copy-start(bf16[8,64,512]{2,1,0:T(8,128)(2,1)S(1)} %all-to-all-done) | copy-start | bytes 1572868
  21.4 0.6 copy-start.8
  26.1 24.2 %copy-start.4 = (bf16[1,1024,128]{2,1,0:T(8,128)(2,1)S(1)}, bf16[1,1024,128]{2,1,0:T(8,128)(2,1)}, u32[]{:S(2)}) copy-start(bf16[1,1024,128]{2,1,0:T(8,128)(2,1)} %param.16) | copy-start | bytes 786436
  28.3 23.7 %copy-start.6 = (f32[4096]{0:T(1024)S(1)}, f32[4096]{0:T(1024)}, u32[]{:S(2)}) copy-start(f32[4096]{0:T(1024)} %param.18) | copy-start | bytes 49156
  28.3 59.7 %all-to-all-start.1 = ((bf16[32,2,128,128]{3,2,1,0:T(8,128)(2,1)}), bf16[32,2,128,128]{3,2,1,0:T(8,128)(2,1)S(1)}, u32[]{:S(2)}, u32[]{:S(2)}) async-start(bf16[32,2,128,128]{3,2,1,0:T(8,128)(2,1)} %broadcast_in_dim.129), calls=%async_computation.1 | async-start | bytes 4194304 | tf_op jit(solution)/shard_map/all_to_all | solution.py:250
  48.7 3.3 %copy-start.9 = (f32[64]{0:T(128)S(1)}, f32[64]{0:T(128)}, u32[]{:S(2)}) copy-start(f32[64]{0:T(128)} %copy-done.8) | copy-start | bytes 772
  48.7 3.6 %copy-start.3 = (bf16[4096,128]{1,0:T(8,128)(2,1)S(1)}, bf16[4096,128]{1,0:T(8,128)(2,1)}, u32[]{:S(2)}) copy-start(bf16[4096,128]{1,0:T(8,128)(2,1)} %param.20) | copy-start | bytes 3145732
  49.5 3.5 %copy-start.14 = (pred[32]{0:T(512)(128)(4,1)}, pred[32]{0:T(512)(128)(4,1)S(1)}, u32[]{:S(2)}) copy-start(pred[32]{0:T(512)(128)(4,1)S(1)} %iota_compare_fusion.3) | copy-start | bytes 100
  50.6 2.1 %copy-start.11 = (f32[64]{0:T(128)S(1)}, f32[64]{0:T(128)}, u32[]{:S(2)}) copy-start(f32[64]{0:T(128)} %copy-done.10) | copy-start | bytes 772
  50.6 2.1 %copy-start.13 = (f32[64]{0:T(128)S(1)}, f32[64]{0:T(128)}, u32[]{:S(2)}) copy-start(f32[64]{0:T(128)} %copy-done.12) | copy-start | bytes 772
  50.6 2.4 %copy-start.7 = (s32[32]{0:T(128)S(1)}, s32[32]{0:T(128)}, u32[]{:S(2)}) copy-start(s32[32]{0:T(128)} %get-tuple-element.11) | copy-start | bytes 388
  50.6 2.8 %copy-start.5 = (bf16[1,1024,128]{2,1,0:T(8,128)(2,1)S(1)}, bf16[1,1024,128]{2,1,0:T(8,128)(2,1)}, u32[]{:S(2)}) copy-start(bf16[1,1024,128]{2,1,0:T(8,128)(2,1)} %param.17) | copy-start | bytes 786436
  53.5 63.1 %copy-start.16 = (s32[32]{0:T(128)S(1)}, s32[32]{0:T(128)}, u32[]{:S(2)}) copy-start(s32[32]{0:T(128)} %param.25) | copy-start | bytes 388
  88.0 1.3 copy-start.1
  112.5 50.3 %all-to-all-start.2 = ((bf16[32,2,128,128]{3,2,1,0:T(8,128)(2,1)}), bf16[32,2,128,128]{3,2,1,0:T(8,128)(2,1)S(1)}, u32[]{:S(2)}, u32[]{:S(2)}) async-start(bf16[32,2,128,128]{3,2,1,0:T(8,128)(2,1)} %bitcast.69), calls=%async_computation.2 | async-start | bytes 4194304 | tf_op jit(solution)/shard_map/all_to_all | solution.py:262
  117.2 7.1 %copy-start.15 = (pred[32]{0:T(512)(128)(4,1)S(1)}, pred[32]{0:T(512)(128)(4,1)}, u32[]{:S(2)}) copy-start(pred[32]{0:T(512)(128)(4,1)} %copy-done.14) | copy-start | bytes 100

commit v4 on v3

--- a/solution.py
+++ b/solution.py
@@ -35,19 +35,34 @@
 MESH = pl.DeviceIdType.MESH
 
 
-def passage_kernel(flags_ref, q_ref, k_ref, v_ref, lim_ref, acc_ref, st_ref):
+def passage_kernel(flags_ref, q_ref, k_ref, v_ref, lim_ref, out_ref):
     nb, rows, _ = q_ref.shape
     keys = k_ref.shape[0]
     token = lax.broadcasted_iota(jnp.int32, (rows, keys), 1)
-    sub = lax.broadcasted_iota(jnp.int32, (8, rows), 0)
+    sub = lax.broadcasted_iota(jnp.int32, (16, rows), 0)
+
+    def split(m_row, l_row):
+        m_hi = m_row.astype(jnp.bfloat16).astype(jnp.float32)
+        l_hi = l_row.astype(jnp.bfloat16).astype(jnp.float32)
+        st = jnp.where(
+            sub == 0,
+            m_row,
+            jnp.where(
+                sub == 1,
+                m_row - m_hi,
+                jnp.where(sub == 2, l_row, jnp.where(sub == 3, l_row - l_hi, 0.0)),
+            ),
+        )
+        return st.astype(jnp.bfloat16)
 
     def body(b, carry):
         flag = flags_ref[b]
 
         @pl.when(flag == 0)
         def _():
-            acc_ref[b] = jnp.zeros((rows, HEAD_SIZE), acc_ref.dtype)
-            st_ref[b] = jnp.where(sub == 0, NEGATIVE_FLOOR, 0.0).astype(jnp.float32)
+            out_ref[b, 0:rows] = jnp.zeros((rows, HEAD_SIZE), out_ref.dtype)
+            floor = jnp.full((16, rows), NEGATIVE_FLOOR, jnp.float32)
+            out_ref[b, rows:] = split(floor, jnp.zeros((16, rows), jnp.float32))
 
         @pl.when(flag > 0)
         def _():
@@ -59,12 +74,12 @@
             maxima = jnp.max(scores, axis=1, keepdims=True)
             weights = jnp.exp(scores - maxima)
             totals = jnp.sum(weights, axis=1, keepdims=True)
-            acc_ref[b] = jnp.dot(
+            out_ref[b, 0:rows] = jnp.dot(
                 weights.astype(jnp.bfloat16), v_ref[...], preferred_element_type=jnp.float32
-            ).astype(acc_ref.dtype)
-            m_row = jnp.transpose(jnp.broadcast_to(maxima, (rows, rows)))[0:8]
-            l_row = jnp.transpose(jnp.broadcast_to(totals, (rows, rows)))[0:8]
-            st_ref[b] = jnp.where(sub == 0, m_row, jnp.where(sub == 1, l_row, 0.0))
+            ).astype(out_ref.dtype)
+            m_row = jnp.transpose(jnp.broadcast_to(maxima, (rows, rows)))[0:16]
+            l_row = jnp.transpose(jnp.broadcast_to(totals, (rows, rows)))[0:16]
+            out_ref[b, rows:] = split(m_row, l_row)
 
         return carry
 
@@ -77,70 +92,102 @@
     return pl.pallas_call(
         passage_kernel,
         in_specs=[pl.BlockSpec(memory_space=pltpu.SMEM), vmem, vmem, vmem, vmem],
-        out_specs=[vmem, vmem],
-        out_shape=[
-            jax.ShapeDtypeStruct((nb, rows, HEAD_SIZE), jnp.bfloat16),
-            jax.ShapeDtypeStruct((nb, 8, rows), jnp.float32),
-        ],
+        out_specs=vmem,
+        out_shape=jax.ShapeDtypeStruct((nb, rows + 16, HEAD_SIZE), jnp.bfloat16),
     )(flags, q_blocks, keys, values, lim)
 
 
-def exchange_kernel(n, gather, *refs):
-    count = len(refs) // 2 - 1
-    ins, outs = refs[:count], refs[count : 2 * count]
-    send_sem, recv_sem, local_sem = refs[2 * count :]
-    me = lax.axis_index("seq")
-    mp = lax.axis_index("mp")
+def mp_gather_kernel(n, x_ref, y_ref, send_sem, recv_sem, local_sem):
+    me = lax.axis_index("mp")
+    row = lax.axis_index("seq")
+    width = x_ref.shape[1]
     barrier = pltpu.get_barrier_semaphore()
     for k in range(1, n):
         peer = lax.rem(me + k, n)
-        pl.semaphore_signal(barrier, inc=1, device_id=(peer, mp), device_id_type=MESH)
+        pl.semaphore_signal(barrier, inc=1, device_id=(row, peer), device_id_type=MESH)
+    pl.semaphore_wait(barrier, n - 1)
+    cols = pl.ds(pl.multiple_of(me * width, width), width)
+    copies = []
+    for k in range(1, n):
+        peer = lax.rem(me + k, n)
+        c = pltpu.make_async_remote_copy(
+            src_ref=x_ref,
+            dst_ref=y_ref.at[:, cols],
+            send_sem=send_sem.at[k],
+            recv_sem=recv_sem.at[k],
+            device_id=(row, peer),
+            device_id_type=MESH,
+        )
+        c.start()
+        copies.append(c)
+    own = pltpu.make_async_copy(x_ref, y_ref.at[:, cols], local_sem)
+    own.start()
+    for c in copies:
+        c.wait()
+    own.wait()
+
+
+def mp_gather(x, n):
+    vmem = pl.BlockSpec(memory_space=pltpu.VMEM)
+    return pl.pallas_call(
+        functools.partial(mp_gather_kernel, n),
+        in_specs=[vmem],
+        out_specs=vmem,
+        out_shape=jax.ShapeDtypeStruct((x.shape[0], x.shape[1] * n), x.dtype),
+        scratch_shapes=[
+            pltpu.SemaphoreType.DMA((n,)),
+            pltpu.SemaphoreType.DMA((n,)),
+            pltpu.SemaphoreType.DMA(()),
+        ],
+        compiler_params=pltpu.CompilerParams(collective_id=0, has_side_effects=True),
+    )(x)
+
+
+def mp_scatter_kernel(n, x_ref, y_ref, send_sem, recv_sem, local_sem):
+    me = lax.axis_index("mp")
+    row = lax.axis_index("seq")
+    width = y_ref.shape[2]
+    barrier = pltpu.get_barrier_semaphore()
+    for k in range(1, n):
+        peer = lax.rem(me + k, n)
+        pl.semaphore_signal(barrier, inc=1, device_id=(row, peer), device_id_type=MESH)
     pl.semaphore_wait(barrier, n - 1)
     copies = []
-    for a in range(count):
-        for k in range(1, n):
-            peer = lax.rem(me + k, n)
-            src = ins[a] if gather else ins[a].at[peer]
-            c = pltpu.make_async_remote_copy(
-                src_ref=src,
-                dst_ref=outs[a].at[me],
-                send_sem=send_sem.at[a, k],
-                recv_sem=recv_sem.at[a, k],
-                device_id=(peer, mp),
-                device_id_type=MESH,
-            )
-            c.start()
-            copies.append(c)
-    locals_ = []
-    for a in range(count):
-        src = ins[a] if gather else ins[a].at[me]
-        c = pltpu.make_async_copy(src, outs[a].at[me], local_sem.at[a])
+    for k in range(1, n):
+        peer = lax.rem(me + k, n)
+        c = pltpu.make_async_remote_copy(
+            src_ref=x_ref.at[:, pl.ds(pl.multiple_of(peer * width, width), width)],
+            dst_ref=y_ref.at[me],
+            send_sem=send_sem.at[k],
+            recv_sem=recv_sem.at[k],
+            device_id=(row, peer),
+            device_id_type=MESH,
+        )
         c.start()
-        locals_.append(c)
+        copies.append(c)
+    own = pltpu.make_async_copy(
+        x_ref.at[:, pl.ds(pl.multiple_of(me * width, width), width)], y_ref.at[me], local_sem
+    )
+    own.start()
     for c in copies:
         c.wait()
-    for c in locals_:
-        c.wait()
-
-
-def exchange(arrays, n, gather, collective_id):
-    count = len(arrays)
+    own.wait()
+
+
+def mp_scatter(x, n):
     vmem = pl.BlockSpec(memory_space=pltpu.VMEM)
-    out_shape = [
-        jax.ShapeDtypeStruct(((n,) + x.shape) if gather else x.shape, x.dtype) for x in arrays
-    ]
     return pl.pallas_call(
-        functools.partial(exchange_kernel, n, gather),
-        in_specs=[vmem] * count,
-        out_specs=[vmem] * count,
-        out_shape=out_shape,
+        functools.partial(mp_scatter_kernel, n),
+        in_specs=[vmem],
+        out_specs=vmem,
+        out_shape=jax.ShapeDtypeStruct((n, x.shape[0], x.shape[1] // n), x.dtype),
         scratch_shapes=[
-            pltpu.SemaphoreType.DMA((count, n)),
-            pltpu.SemaphoreType.DMA((count, n)),
-            pltpu.SemaphoreType.DMA((count,)),
+            pltpu.SemaphoreType.DMA((n,)),
+            pltpu.SemaphoreType.DMA((n,)),
+            pltpu.SemaphoreType.DMA(()),
         ],
-        compiler_params=pltpu.CompilerParams(collective_id=collective_id, has_side_effects=True),
-    )(*arrays)
+        compiler_params=pltpu.CompilerParams(collective_id=1, has_side_effects=True),
+    )(x)
 
 
 def local(
@@ -195,10 +242,7 @@
 
     rows_local = jnp.concatenate([prompt_hidden, recompute_hidden], axis=0)
     n_mp = w_out.shape[1] // rows_local.shape[1]
-    gathered = lax.all_to_all(
-        jnp.broadcast_to(rows_local[None], (n_mp,) + rows_local.shape), "mp", 0, 0, tiled=True
-    )
-    full_rows = jnp.transpose(gathered, (1, 0, 2)).reshape(query_rows, -1)
+    full_rows = mp_gather(rows_local, n_mp)
     normalized_hidden = normalize(full_rows, norm_gain)
     queries = (
         apply_rotation(
@@ -257,17 +301,19 @@
     )
     flags = jnp.stack([prompt_flag, recompute_flag], axis=1).reshape(-1).astype(jnp.int32)
     lim = jnp.repeat(own_index, local_heads).reshape(-1, 1).astype(jnp.int32)
-    acc, stats = passage_attention(flags, q_blocks, passage_keys, passage_values, lim)
-
-    acc_back = lax.all_to_all(
-        acc.reshape(n_seq, 2, prompt_rows * local_heads, HEAD_SIZE), "seq", 0, 0, tiled=True
-    )
-    stats_back = lax.all_to_all(
-        stats[:, 0:2].reshape(n_seq, 2, 2, prompt_rows * local_heads), "seq", 0, 0, tiled=True
-    )
-    part_max = stats_back[:, :, 0].reshape(n_seq, query_rows, local_heads)
-    part_tot = stats_back[:, :, 1].reshape(n_seq, query_rows, local_heads)
-    part_acc = acc_back.reshape(n_seq, query_rows, local_heads, HEAD_SIZE).astype(jnp.float32)
+    packed = passage_attention(flags, q_blocks, passage_keys, passage_values, lim)
+    block_rows = packed.shape[1]
+
+    back = lax.all_to_all(
+        packed.reshape(n_seq, 2, block_rows, HEAD_SIZE), "seq", 0, 0, tiled=True
+    )
+    rows128 = prompt_rows * local_heads
+    stats_back = back[:, :, rows128 : rows128 + 4].astype(jnp.float32)
+    part_max = (stats_back[:, :, 0] + stats_back[:, :, 1]).reshape(n_seq, query_rows, local_heads)
+    part_tot = (stats_back[:, :, 2] + stats_back[:, :, 3]).reshape(n_seq, query_rows, local_heads)
+    part_acc = (
+        back[:, :, :rows128].reshape(n_seq, query_rows, local_heads, HEAD_SIZE).astype(jnp.float32)
+    )
 
     pq = queries[:prompt_rows].astype(jnp.float32)
     pk = fresh_keys[:prompt_rows].astype(jnp.float32)
@@ -298,8 +344,7 @@
         own_live[:, None, None], accumulated / safe_totals[..., None], 0.0
     ).astype(jnp.bfloat16).reshape(query_rows, local_heads * HEAD_SIZE)
     projected = jnp.dot(attention, w_out, preferred_element_type=jnp.float32)
-    pieces = jnp.transpose(projected.reshape(query_rows, n_mp, -1), (1, 0, 2))
-    combined = jnp.sum(lax.all_to_all(pieces, "mp", 0, 0, tiled=True), axis=0).astype(jnp.bfloat16)
+    combined = jnp.sum(mp_scatter(projected, n_mp), axis=0).astype(jnp.bfloat16)
     return (combined[:prompt_rows], combined[prompt_rows:])
 
 

time: 195 us -> 190 us (0.974)
  blocking collectives: 41.5 us -> 0 us
  Pallas kernels: 5.46 us -> 40 us
  waiting for transfers between devices: 70.5 us -> 90.6 us
  local copies, waits for them, and re-layouts: 30.8 us -> 11.9 us
  starting transfers between devices: 21.1 us -> 17.2 us
  other arithmetic: 12.8 us -> 16.1 us
  matrix products: 8.7 us -> 10.9 us
    all_to_all x2 -> x0, blocking collectives: 41.5 us -> none  [the longest x1 24.7 us: local(): lax.all_to_all(pieces, 'mp', 0, 0, tiled=True)]
    pallas_call x0 -> x2, Pallas kernels: none -> 34 us  [the longest x1 19.5 us: mp_scatter(): pl.pallas_call(functools.partial(mp_scatter_kernel, n), in_specs=[vmem],...]
    dot_general x2 -> x0, local copies, waits for them, and re-layouts: 12.9 us -> none  [the longest x1 6.46 us: local(): projected = jnp.dot(attention, w_out, preferred_element_type=jnp.float32)]
    all_to_all x2 -> x1, waiting for transfers between devices: 37.1 us -> 48.1 us  [local(): lax.all_to_all(packed.reshape(n_seq, 2, block_rows, HEAD_SIZE), 'seq', 0,...]
    all_to_all x1, waiting for transfers between devices: 33.3 us -> 42.5 us  [local(): lax.all_to_all(jnp.broadcast_to(own_blocks, (n_seq,) + own_blocks.shape[1...]
    all_to_all x2 -> x1, starting transfers between devices: 10.6 us -> 6.73 us  [local(): lax.all_to_all(packed.reshape(n_seq, 2, block_rows, HEAD_SIZE), 'seq', 0,...]
  transfers between devices with their start and end apart: 3 -> 2, of which waited for: 2 -> 2; matrix products, arithmetic and copies ran while one was open for 18% -> 7% of each run, Pallas kernels for 0% -> 0%
where the time goes in v4:
time: 190 us; the launch traced here: 189 us
  waiting for transfers between devices  90.6 us (48%)
  Pallas kernels  40 us (21%)
  starting transfers between devices  17.2 us (9%)
  other arithmetic  16.1 us (8%)
  local copies, waits for them, and re-layouts  11.9 us (6%)
  matrix products  10.9 us (6%)
  between operations  2.3 us (1%)
    all_to_all x1, waiting for transfers between devices, local(): lax.all_to_all(packed.reshape(n_seq, 2, block_rows, HEAD_SIZE), 'seq', 0,...  48.1 us
    all_to_all x1, waiting for transfers between devices, local(): lax.all_to_all(jnp.broadcast_to(own_blocks, (n_seq,) + own_blocks.shape[1...  42.5 us
    pallas_call x1, Pallas kernels, mp_scatter(): pl.pallas_call(functools.partial(mp_scatter_kernel, n), in_specs=[vmem],...  19.5 us
    pallas_call x1, Pallas kernels, mp_gather(): pl.pallas_call(functools.partial(mp_gather_kernel, n), in_specs=[vmem], o...  14.5 us
    all_to_all x1, starting transfers between devices, local(): lax.all_to_all(jnp.broadcast_to(own_blocks, (n_seq,) + own_blocks.shape[1...  10.5 us
    all_to_all x1, starting transfers between devices, local(): lax.all_to_all(packed.reshape(n_seq, 2, block_rows, HEAD_SIZE), 'seq', 0,...  6.73 us
    pallas_call x1, Pallas kernels, passage_attention(): pl.pallas_call(passage_kernel, in_specs=[pl.BlockSpec(memory_space=pltpu....  5.99 us
    dot_general x1, matrix products, local(): projected = jnp.dot(attention, w_out, preferred_element_type=jnp.float32)  4.09 us
  transfers between devices with their start and end apart: 2, of which 2 were waited for; matrix products, arithmetic and copies ran while one was open for 7% of the time, Pallas kernels for 0%

profile of v4, /device:TPU:1, one launch (start us, length us, event | category | flops | bytes accessed | tf_op | source)
XLA Modules:
  0.0 189.1 jit_solution(9314575382413714926)
XLA Ops:
  0.6 0.0 copy-start
  0.7 1.0 select_reduce_fusion.1
  1.6 0.6 dynamic_slice.23
  2.2 0.6 dynamic_slice.22
  4.1 1.4 pad_maximum_fusion.x_ref
  5.5 14.5 %shard_map.149 = bf16[64,4096]{1,0:T(8,128)(2,1)} custom-call(bf16[64,512]{1,0:T(8,128)(2,1)} %pad_maximum_fusion.x_ref), custom_call_target="tpu_custom_call" | custom-call | tf_op jit(solution)/shard_map/pallas_call | solution.py:132
  20.0 1.2 fusion.1
  21.3 3.3 %fusion.53 = f32[64,512]{1,0:T(8,128)S(1)} fusion(bf16[4096,512]{1,0:T(8,128)(2,1)} %param.19, bf16[64,4096]{1,0:T(8,128)(2,1)} %shard_map.149, f32[4096]{0:T(1024)} %param.18, f32[64]{0:T(128)S(1)} %add_rsqrt_fusion), kind=kOutput, calls=%fused_computation.102 | convolution fusion | flops 269484032 | bytes 4866304 | tf_op jit(solution)/shard_map/dot_general | solution.py:249
  24.5 0.0 copy-start.9
  24.5 0.0 copy-start.12
  24.6 0.1 fusion.56
  24.8 0.7 broadcast_add_fusion
  25.5 0.1 add_convert_fusion.2
  25.6 0.2 multiply_cosine_fusion.1
  25.8 0.1 copy.48
  25.9 0.1 copy.49
  25.9 0.0 copy-start.2
  25.9 0.1 pad_maximum_fusion.1
  26.0 1.8 broadcast_in_dim.122
  27.9 10.5 %all-to-all-start = ((bf16[32,2,128,128]{3,2,1,0:T(8,128)(2,1)}), bf16[32,2,128,128]{3,2,1,0:T(8,128)(2,1)}, u32[]{:S(2)}, u32[]{:S(2)}) async-start(bf16[32,2,128,128]{3,2,1,0:T(8,128)(2,1)} %broadcast_in_dim.122), calls=%async_computation | async-start | bytes 4194304 | tf_op jit(solution)/shard_map/all_to_all | solution.py:294
  38.4 0.0 copy-start.4
  38.4 0.6 dynamic_slice.21
  39.0 0.6 dynamic_slice.20
  39.7 0.6 fusion.46
  40.3 0.1 copy.45
  40.4 0.6 reshape.329.flags_ref
  41.1 0.1 broadcast_in_dim.124
  41.1 0.7 reshape_reshape.4.lim_ref
  41.8 0.3 convolution_convert_fusion.1
  42.2 0.6 iota_compare_fusion.3
  42.9 0.4 convolution_bitcast_fusion
  43.3 0.2 fusion.27
  43.5 0.1 fusion.42
  43.6 0.1 fusion.11
  43.7 0.4 convolution_convert_fusion
  44.2 0.2 fusion.4
  44.4 1.1 slice_select_fusion
  45.5 42.5 %all-to-all-done = bf16[32,2,128,128]{3,2,1,0:T(8,128)(2,1)} async-done(((bf16[32,2,128,128]{3,2,1,0:T(8,128)(2,1)}), bf16[32,2,128,128]{3,2,1,0:T(8,128)(2,1)}, u32[]{:S(2)}, u32[]{:S(2)}) %all-to-all-start) | async-done | bytes 2097184 | tf_op jit(solution)/shard_map/all_to_all | solution.py:294
  88.1 6.0 %shard_map.150 = bf16[64,144,128]{2,1,0:T(8,128)(2,1)} custom-call(s32[64]{0:T(128)} %reshape.329.flags_ref, bf16[64,128,128]{2,1,0:T(8,128)(2,1)} %bitcast.10.q_ref, bf16[1024,128]{1,0:T(8,128)(2,1)} %get-tuple-element.11.k_ref, bf16[1024,128]{1,0:T(8,128)(2,1)} %get-tuple-element.10.v_ref, s32[128,1]{1,0:T(8,128)} %reshape_reshape.4.lim_ref), custom_call_target="tpu_custom_call" | custom-call | tf_op jit(solution)/shard_map/pallas_call | solution.py:92
  94.1 6.7 %all-to-all-start.1 = ((bf16[32,2,144,128]{3,2,1,0:T(8,128)(2,1)}), bf16[32,2,144,128]{3,2,1,0:T(8,128)(2,1)S(1)}, u32[]{:S(2)}, u32[]{:S(2)}) async-start(bf16[32,2,144,128]{3,2,1,0:T(8,128)(2,1)} %bitcast.54), calls=%async_computation.1 | async-start | bytes 4718592 | tf_op jit(solution)/shard_map/all_to_all | solution.py:307
  100.8 1.3 dynamic_slice.19
  102.1 0.7 iota_compare_fusion.4
  102.8 1.3 pad_add_fusion
  104.1 0.1 fusion.40
  104.2 0.9 fusion.58
  105.2 0.5 copy-done.7
  105.7 1.5 fusion.28
  107.2 48.1 %all-to-all-done.1 = bf16[32,2,144,128]{3,2,1,0:T(8,128)(2,1)S(1)} async-done(((bf16[32,2,144,128]{3,2,1,0:T(8,128)(2,1)}), bf16[32,2,144,128]{3,2,1,0:T(8,128)(2,1)S(1)}, u32[]{:S(2)}, u32[]{:S(2)}) %all-to-all-start.1) | async-done | bytes 2359328 | tf_op jit(solution)/shard_map/all_to_all | solution.py:307
  155.3 0.7 fusion.55
  156.0 0.7 reduce_max.21
  156.7 0.8 copy.51
  157.5 0.7 pad_maximum_fusion.5
  158.2 0.7 copy.52
  158.9 0.9 sub.42
  159.8 0.9 fusion.35
  160.6 0.1 reduce_sum.73
  160.7 0.1 copy.55
  160.8 0.8 subtract_exponential_fusion
  161.6 0.7 compare_select_fusion
  162.3 1.3 multiply_reduce_fusion
  163.5 4.1 %fusion.12.x_ref = f32[64,4096]{1,0:T(8,128)} fusion(bf16[512,4096]{1,0:T(8,128)(2,1)} %param.22, f32[64,4]{0,1:T(4,128)S(1)} %get-tuple-element.4, f32[64,4]{0,1:T(4,128)S(1)} %get-tuple-element.5, f32[32,4,128]{2,0,1:T(8,128)} %fusion.28, f32[64,4,128]{2,1,0:T(4,128)S(1)} %bitcast.55, pred[64]{0:T(512)(128)(4,1)} %pad_add_fusion), kind=kOutput, calls=%fused_computation.27 | convolution fusion | flops 268599296 | bytes 5441600 | tf_op jit(solution)/shard_map/dot_general | solution.py:346
  167.6 19.5 %shard_map.151 = f32[8,64,512]{2,1,0:T(8,128)} custom-call(f32[64,4096]{1,0:T(8,128)} %fusion.12.x_ref), custom_call_target="tpu_custom_call" | custom-call | tf_op jit(solution)/shard_map/pallas_call | solution.py:179
  187.2 1.3 reduce_sum.75
  188.5 0.6 fusion.57
  (31 shorter events, 0.3 us)
Async XLA Ops:
  0.6 41.2 %copy-start = (bf16[4096,128]{1,0:T(8,128)(2,1)S(1)}, bf16[4096,128]{1,0:T(8,128)(2,1)}, u32[]{:S(2)}) copy-start(bf16[4096,128]{1,0:T(8,128)(2,1)} %param.21) | copy-start | bytes 3145732
  24.5 13.9 %copy-start.9 = (s32[32]{0:T(128)S(1)}, s32[32]{0:T(128)}, u32[]{:S(2)}) copy-start(s32[32]{0:T(128)} %param.23) | copy-start | bytes 388
  24.5 14.5 %copy-start.12 = (s32[32]{0:T(128)S(1)}, s32[32]{0:T(128)}, u32[]{:S(2)}) copy-start(s32[32]{0:T(128)} %param.26) | copy-start | bytes 388
  24.6 15.1 %copy-start.10 = (s32[32]{0:T(128)S(1)}, s32[32]{0:T(128)}, u32[]{:S(2)}) copy-start(s32[32]{0:T(128)} %param.24) | copy-start | bytes 388
  24.6 17.3 %copy-start.1 = (bf16[64,4096]{1,0:T(8,128)(2,1)S(1)}, bf16[64,4096]{1,0:T(8,128)(2,1)}, u32[]{:S(2)}) copy-start(bf16[64,4096]{1,0:T(8,128)(2,1)} %shard_map.149) | copy-start | bytes 1572868
  24.6 17.3 %copy-start.6 = (f32[4096]{0:T(1024)S(1)}, f32[4096]{0:T(1024)}, u32[]{:S(2)}) copy-start(f32[4096]{0:T(1024)} %param.18) | copy-start | bytes 49156
  25.9 17.0 %copy-start.2 = (bf16[4096,128]{1,0:T(8,128)(2,1)S(1)}, bf16[4096,128]{1,0:T(8,128)(2,1)}, u32[]{:S(2)}) copy-start(bf16[4096,128]{1,0:T(8,128)(2,1)} %param.20) | copy-start | bytes 3145732
  27.9 16.2 %copy-start.3 = (bf16[1,1024,128]{2,1,0:T(8,128)(2,1)S(1)}, bf16[1,1024,128]{2,1,0:T(8,128)(2,1)}, u32[]{:S(2)}) copy-start(bf16[1,1024,128]{2,1,0:T(8,128)(2,1)} %param.16) | copy-start | bytes 786436
  27.9 60.2 %all-to-all-start = ((bf16[32,2,128,128]{3,2,1,0:T(8,128)(2,1)}), bf16[32,2,128,128]{3,2,1,0:T(8,128)(2,1)}, u32[]{:S(2)}, u32[]{:S(2)}) async-start(bf16[32,2,128,128]{3,2,1,0:T(8,128)(2,1)} %broadcast_in_dim.122), calls=%async_computation | async-start | bytes 4194304 | tf_op jit(solution)/shard_map/all_to_all | solution.py:294
  38.4 6.0 %copy-start.4 = (bf16[1,1024,128]{2,1,0:T(8,128)(2,1)S(1)}, bf16[1,1024,128]{2,1,0:T(8,128)(2,1)}, u32[]{:S(2)}) copy-start(bf16[1,1024,128]{2,1,0:T(8,128)(2,1)} %param.17) | copy-start | bytes 786436
  42.2 0.7 copy-start.8
  42.9 51.2 %copy-start.11 = (pred[32]{0:T(512)(128)(4,1)}, pred[32]{0:T(512)(128)(4,1)S(1)}, u32[]{:S(2)}) copy-start(pred[32]{0:T(512)(128)(4,1)S(1)} %iota_compare_fusion.3) | copy-start | bytes 100
  43.5 50.6 %copy-start.5 = (bf16[64,1,64]{2,0,1:T(8,128)(2,1)}, bf16[64,1,64]{2,0,1:T(8,128)(2,1)S(1)}, u32[]{:S(2)}) copy-start(bf16[64,1,64]{2,0,1:T(8,128)(2,1)S(1)} %get-tuple-element.21) | copy-start | bytes 24580
  94.1 61.2 %all-to-all-start.1 = ((bf16[32,2,144,128]{3,2,1,0:T(8,128)(2,1)}), bf16[32,2,144,128]{3,2,1,0:T(8,128)(2,1)S(1)}, u32[]{:S(2)}, u32[]{:S(2)}) async-start(bf16[32,2,144,128]{3,2,1,0:T(8,128)(2,1)} %bitcast.54), calls=%async_computation.1 | async-start | bytes 4718592 | tf_op jit(solution)/shard_map/all_to_all | solution.py:307
  105.1 0.6 copy-start.7

commit v5 on v4

--- a/solution.py
+++ b/solution.py
@@ -35,7 +35,7 @@
 MESH = pl.DeviceIdType.MESH
 
 
-def passage_kernel(flags_ref, q_ref, k_ref, v_ref, lim_ref, out_ref):
+def passage_kernel(nx, nz, flags_ref, q_ref, k_ref, v_ref, lim_ref, out_ref):
     nb, rows, _ = q_ref.shape
     keys = k_ref.shape[0]
     token = lax.broadcasted_iota(jnp.int32, (rows, keys), 1)
@@ -66,8 +66,10 @@
 
         @pl.when(flag > 0)
         def _():
+            d = b // 2
+            stored = ((d % nz) * nx + d // nz) * 2 + b % 2
             scores = lax.dot_general(
-                q_ref[b], k_ref[...], (((1,), (1,)), ((), ())), preferred_element_type=jnp.float32
+                q_ref[stored], k_ref[...], (((1,), (1,)), ((), ())), preferred_element_type=jnp.float32
             ) * (1.0 / math.sqrt(HEAD_SIZE))
             limit = jnp.where(flag == 2, lim_ref[...], keys - 1)
             scores = jnp.where(token <= limit, scores, NEGATIVE_FLOOR)
@@ -86,11 +88,11 @@
     lax.fori_loop(0, nb, body, 0)
 
 
-def passage_attention(flags, q_blocks, keys, values, lim):
+def passage_attention(nx, nz, flags, q_blocks, keys, values, lim):
     nb, rows, _ = q_blocks.shape
     vmem = pl.BlockSpec(memory_space=pltpu.VMEM)
     return pl.pallas_call(
-        passage_kernel,
+        functools.partial(passage_kernel, nx, nz),
         in_specs=[pl.BlockSpec(memory_space=pltpu.SMEM), vmem, vmem, vmem, vmem],
         out_specs=vmem,
         out_shape=jax.ShapeDtypeStruct((nb, rows + 16, HEAD_SIZE), jnp.bfloat16),
@@ -187,6 +189,98 @@
             pltpu.SemaphoreType.DMA(()),
         ],
         compiler_params=pltpu.CompilerParams(collective_id=1, has_side_effects=True),
+    )(x)
+
+
+def relay_gather_kernel(nx, nz, x_ref, y_ref, sx_send, sx_recv, zp_send, zp_recv, zm_send, zm_recv, own_sem):
+    me = lax.axis_index("seq")
+    mp = lax.axis_index("mp")
+    x = me // nz
+    z = me % nz
+    up = lax.rem(z + 1, nz)
+    down = lax.rem(z + nz - 1, nz)
+    barrier = pltpu.get_barrier_semaphore()
+    peers = [(lax.rem(x + k, nx) * nz + z, mp) for k in range(1, nx)]
+    peers += [(x * nz + up, mp), (x * nz + down, mp)]
+    for p in peers:
+        pl.semaphore_signal(barrier, inc=1, device_id=p, device_id_type=MESH)
+    pl.semaphore_wait(barrier, len(peers))
+
+    slot = z * nx + x
+    first = []
+    for k in range(1, nx):
+        c = pltpu.make_async_remote_copy(
+            src_ref=x_ref,
+            dst_ref=y_ref.at[slot],
+            send_sem=sx_send.at[k],
+            recv_sem=sx_recv.at[k],
+            device_id=peers[k - 1],
+            device_id_type=MESH,
+        )
+        c.start()
+        first.append(c)
+    own = pltpu.make_async_copy(x_ref, y_ref.at[slot], own_sem)
+    own.start()
+    for c in first:
+        c.wait()
+    own.wait()
+
+    plus_steps = nz // 2
+    minus_steps = nz - 1 - plus_steps
+    sent = []
+    for t in range(1, plus_steps + 1):
+        step = []
+        column = lax.rem(z - (t - 1) + nz, nz)
+        bundle = pl.ds(pl.multiple_of(column * nx, nx), nx)
+        c = pltpu.make_async_remote_copy(
+            src_ref=y_ref.at[bundle],
+            dst_ref=y_ref.at[bundle],
+            send_sem=zp_send.at[t],
+            recv_sem=zp_recv.at[t],
+            device_id=(x * nz + up, mp),
+            device_id_type=MESH,
+        )
+        c.start()
+        step.append(c)
+        if t <= minus_steps:
+            column = lax.rem(z + (t - 1), nz)
+            bundle = pl.ds(pl.multiple_of(column * nx, nx), nx)
+            c = pltpu.make_async_remote_copy(
+                src_ref=y_ref.at[bundle],
+                dst_ref=y_ref.at[bundle],
+                send_sem=zm_send.at[t],
+                recv_sem=zm_recv.at[t],
+                device_id=(x * nz + down, mp),
+                device_id_type=MESH,
+            )
+            c.start()
+            step.append(c)
+        for c in step:
+            c.wait_recv()
+        sent += step
+    for c in sent:
+        c.wait_send()
+
+
+def relay_gather(x, nx, nz):
+    vmem = pl.BlockSpec(memory_space=pltpu.VMEM)
+    plus_steps = nz // 2
+    minus_steps = nz - 1 - plus_steps
+    return pl.pallas_call(
+        functools.partial(relay_gather_kernel, nx, nz),
+        in_specs=[vmem],
+        out_specs=vmem,
+        out_shape=jax.ShapeDtypeStruct((nx * nz,) + x.shape, x.dtype),
+        scratch_shapes=[
+            pltpu.SemaphoreType.DMA((nx,)),
+            pltpu.SemaphoreType.DMA((nx,)),
+            pltpu.SemaphoreType.DMA((plus_steps + 1,)),
+            pltpu.SemaphoreType.DMA((plus_steps + 1,)),
+            pltpu.SemaphoreType.DMA((minus_steps + 1,)),
+            pltpu.SemaphoreType.DMA((minus_steps + 1,)),
+            pltpu.SemaphoreType.DMA(()),
+        ],
+        compiler_params=pltpu.CompilerParams(collective_id=2, has_side_effects=True),
     )(x)
 
 
@@ -290,9 +384,9 @@
     passage_keys = jnp.where(replaced, placed[:, :HEAD_SIZE], shifted_keys)
     passage_values = jnp.where(replaced, placed[:, HEAD_SIZE:], value_cache[0])
 
-    own_blocks = queries.reshape(1, 2, prompt_rows * local_heads, HEAD_SIZE)
-    all_queries = lax.all_to_all(
-        jnp.broadcast_to(own_blocks, (n_seq,) + own_blocks.shape[1:]), "seq", 0, 0, tiled=True
+    nx, nz = SEQ_SHAPE
+    all_queries = relay_gather(
+        queries.reshape(2, prompt_rows * local_heads, HEAD_SIZE), nx, nz
     )
     q_blocks = all_queries.reshape(n_seq * 2, prompt_rows * local_heads, HEAD_SIZE)
     prompt_flag = jnp.where(prompt_slot == own_owner, 1, 0)
@@ -301,7 +395,7 @@
     )
     flags = jnp.stack([prompt_flag, recompute_flag], axis=1).reshape(-1).astype(jnp.int32)
     lim = jnp.repeat(own_index, local_heads).reshape(-1, 1).astype(jnp.int32)
-    packed = passage_attention(flags, q_blocks, passage_keys, passage_values, lim)
+    packed = passage_attention(nx, nz, flags, q_blocks, passage_keys, passage_values, lim)
     block_rows = packed.shape[1]
 
     back = lax.all_to_all(
@@ -349,6 +443,11 @@
 
 
 def solution(mesh):
+    global SEQ_SHAPE
+    sizes = dict(zip(mesh.axis_names, mesh.devices.shape))
+    seq_devices = mesh.devices.reshape(sizes["seq"], sizes["mp"])[:, 0]
+    xs = sorted({d.coords[0] for d in seq_devices})
+    SEQ_SHAPE = (len(xs), sizes["seq"] // len(xs))
     return jax.shard_map(
         local,
         mesh=mesh,

time: 190 us -> 182 us (0.958)
  Pallas kernels: 40 us -> 84.9 us
  waiting for transfers between devices: 90.6 us -> 47.5 us
  starting transfers between devices: 17.2 us -> 4.06 us
  matrix products: 10.9 us -> 13.4 us
    pallas_call x1 -> x2, Pallas kernels: 5.99 us -> 48.8 us  [the longest x1 39.7 us: relay_gather(): pl.pallas_call(functools.partial(relay_gather_kernel, nx, nz), in_specs=[...]
    all_to_all x1 -> x0, waiting for transfers between devices: 42.5 us -> none  [local(): lax.all_to_all(jnp.broadcast_to(own_blocks, (n_seq,) + own_blocks.shape[1...]
    all_to_all x1 -> x0, starting transfers between devices: 10.5 us -> none  [local(): lax.all_to_all(jnp.broadcast_to(own_blocks, (n_seq,) + own_blocks.shape[1...]
    all_to_all x1, starting transfers between devices: 6.73 us -> 4.06 us  [local(): lax.all_to_all(packed.reshape(n_seq, 2, block_rows, HEAD_SIZE), 'seq', 0,...]
    pallas_call x1, Pallas kernels: 19.5 us -> 21.6 us  [mp_scatter(): pl.pallas_call(functools.partial(mp_scatter_kernel, n), in_specs=[vmem],...]
  transfers between devices with their start and end apart: 2 -> 1, of which waited for: 2 -> 1; matrix products, arithmetic and copies ran while one was open for 7% -> 3% of each run, Pallas kernels for 0% -> 0%
where the time goes in v5:
time: 182 us; the launch traced here: 181 us
  Pallas kernels  84.9 us (47%)
  waiting for transfers between devices  47.5 us (26%)
  other arithmetic  17.3 us (10%)
  matrix products  13.4 us (7%)
  local copies, waits for them, and re-layouts  11.2 us (6%)
  starting transfers between devices  4.06 us (2%)
  between operations  2.27 us (1%)
    all_to_all x1, waiting for transfers between devices, local(): lax.all_to_all(packed.reshape(n_seq, 2, block_rows, HEAD_SIZE), 'seq', 0,...  47.5 us
    pallas_call x1, Pallas kernels, relay_gather(): pl.pallas_call(functools.partial(relay_gather_kernel, nx, nz), in_specs=[...  39.7 us
    pallas_call x1, Pallas kernels, mp_scatter(): pl.pallas_call(functools.partial(mp_scatter_kernel, n), in_specs=[vmem],...  21.6 us
    pallas_call x1, Pallas kernels, mp_gather(): pl.pallas_call(functools.partial(mp_gather_kernel, n), in_specs=[vmem], o...  14.5 us
    pallas_call x1, Pallas kernels, passage_attention(): pl.pallas_call(functools.partial(passage_kernel, nx, nz), in_specs=[pl.Bl...  9.03 us
    dot_general x1, matrix products, local(): projected = jnp.dot(attention, w_out, preferred_element_type=jnp.float32)  4.1 us
    all_to_all x1, starting transfers between devices, local(): lax.all_to_all(packed.reshape(n_seq, 2, block_rows, HEAD_SIZE), 'seq', 0,...  4.06 us
  transfers between devices with their start and end apart: 1, of which 1 were waited for; matrix products, arithmetic and copies ran while one was open for 3% of the time, Pallas kernels for 0%

profile of v5, /device:TPU:1, one launch (start us, length us, event | category | flops | bytes accessed | tf_op | source)
XLA Modules:
  0.0 180.6 jit_solution(9100212004676309886)
XLA Ops:
  0.6 0.0 copy-start
  0.6 0.0 copy-start.4
  0.7 1.3 dynamic_slice.21
  2.0 1.2 dynamic_slice.20
  3.2 0.6 iota_compare_fusion.3
  3.9 0.9 select_reduce_fusion.1
  4.8 1.3 fusion.46
  6.1 0.6 dynamic_slice.23
  7.4 0.6 dynamic_slice.22
  8.7 0.1 copy.47
  8.8 0.6 reshape.316.flags_ref
  9.4 0.7 broadcast_add_fusion
  10.1 0.1 fusion.11
  10.2 0.1 broadcast_in_dim.118
  10.2 0.7 reshape_reshape.4.lim_ref
  10.9 1.4 pad_maximum_fusion.x_ref
  12.3 14.5 %shard_map.149 = bf16[64,4096]{1,0:T(8,128)(2,1)} custom-call(bf16[64,512]{1,0:T(8,128)(2,1)} %pad_maximum_fusion.x_ref), custom_call_target="tpu_custom_call" | custom-call | tf_op jit(solution)/shard_map/pallas_call | solution.py:134
  26.8 1.2 fusion.1
  28.1 1.4 convolution_convert_fusion.1
  29.5 0.0 copy-start.6
  29.5 0.0 copy-start.1
  29.5 1.8 convolution_bitcast_fusion
  31.3 3.2 %fusion.53 = f32[64,512]{1,0:T(8,128)S(1)} fusion(bf16[4096,512]{1,0:T(8,128)(2,1)} %param.19, bf16[64,4096]{1,0:T(8,128)(2,1)} %shard_map.149, f32[4096]{0:T(1024)S(1)} %copy-done.4, f32[64]{0:T(128)S(1)} %add_rsqrt_fusion), kind=kOutput, calls=%fused_computation.102 | convolution fusion | flops 269484032 | bytes 4866304 | tf_op jit(solution)/shard_map/dot_general | solution.py:343
  34.6 0.0 copy-start.2
  34.6 0.1 add_convert_fusion.2
  34.7 0.2 multiply_cosine_fusion.1
  34.9 0.2 fusion.27
  35.1 0.0 copy-start.3
  35.2 0.1 fusion.56
  35.3 0.1 copy.50
  35.4 0.1 copy.51
  35.5 0.0 copy-done.1
  35.5 0.7 pad_maximum_fusion.1.x_ref
  36.2 39.7 %shard_map.150 = bf16[32,2,128,128]{3,2,1,0:T(8,128)(2,1)} custom-call(bf16[2,128,128]{2,1,0:T(8,128)(2,1)} %pad_maximum_fusion.1.x_ref), custom_call_target="tpu_custom_call" | custom-call | tf_op jit(solution)/shard_map/pallas_call | solution.py:269
  76.0 0.1 fusion.42
  76.0 0.4 convolution_convert_fusion
  76.5 0.2 fusion.4
  76.7 1.1 slice_select_fusion
  77.9 9.0 %shard_map.151 = bf16[64,144,128]{2,1,0:T(8,128)(2,1)} custom-call(s32[64]{0:T(128)} %reshape.316.flags_ref, bf16[64,128,128]{2,1,0:T(8,128)(2,1)} %bitcast.55, bf16[1024,128]{1,0:T(8,128)(2,1)} %get-tuple-element.11.k_ref, bf16[1024,128]{1,0:T(8,128)(2,1)} %get-tuple-element.10.v_ref, s32[128,1]{1,0:T(8,128)} %reshape_reshape.4.lim_ref), custom_call_target="tpu_custom_call" | custom-call | tf_op jit(solution)/shard_map/pallas_call | solution.py:94
  86.9 4.1 %all-to-all-start = ((bf16[32,2,144,128]{3,2,1,0:T(8,128)(2,1)}), bf16[32,2,144,128]{3,2,1,0:T(8,128)(2,1)S(1)}, u32[]{:S(2)}, u32[]{:S(2)}) async-start(bf16[32,2,144,128]{3,2,1,0:T(8,128)(2,1)} %bitcast.54), calls=%async_computation | async-start | bytes 4718592 | tf_op jit(solution)/shard_map/all_to_all | solution.py:401
  91.0 1.2 dynamic_slice.19
  92.2 0.6 iota_compare_fusion.4
  92.8 1.3 pad_add_fusion
  94.0 0.1 fusion.40
  94.1 0.9 fusion.58
  95.1 0.5 copy-done.5
  95.6 1.5 fusion.28
  97.1 47.5 %all-to-all-done = bf16[32,2,144,128]{3,2,1,0:T(8,128)(2,1)S(1)} async-done(((bf16[32,2,144,128]{3,2,1,0:T(8,128)(2,1)}), bf16[32,2,144,128]{3,2,1,0:T(8,128)(2,1)S(1)}, u32[]{:S(2)}, u32[]{:S(2)}) %all-to-all-start) | async-done | bytes 2359328 | tf_op jit(solution)/shard_map/all_to_all | solution.py:401
  144.7 0.7 fusion.55
  145.4 0.7 reduce_max.21
  146.1 0.8 copy.53
  146.9 0.7 pad_maximum_fusion.5
  147.6 0.7 copy.54
  148.3 0.9 sub.42
  149.2 0.9 fusion.35
  150.0 0.1 reduce_sum.73
  150.2 0.1 copy.57
  150.2 0.8 subtract_exponential_fusion
  151.0 0.7 compare_select_fusion
  151.7 1.3 multiply_reduce_fusion
  153.0 4.1 %fusion.12.x_ref = f32[64,4096]{1,0:T(8,128)} fusion(bf16[512,4096]{1,0:T(8,128)(2,1)} %param.22, f32[64,4]{0,1:T(4,128)S(1)} %get-tuple-element.4, f32[64,4]{0,1:T(4,128)S(1)} %get-tuple-element.5, f32[32,4,128]{2,0,1:T(8,128)} %fusion.28, f32[64,4,128]{2,1,0:T(4,128)S(1)} %bitcast.56, pred[64]{0:T(512)(128)(4,1)} %pad_add_fusion), kind=kOutput, calls=%fused_computation.27 | convolution fusion | flops 268599296 | bytes 5441600 | tf_op jit(solution)/shard_map/dot_general | solution.py:440
  157.1 21.6 %shard_map.152 = f32[8,64,512]{2,1,0:T(8,128)} custom-call(f32[64,4096]{1,0:T(8,128)} %fusion.12.x_ref), custom_call_target="tpu_custom_call" | custom-call | tf_op jit(solution)/shard_map/pallas_call | solution.py:181
  178.7 1.3 reduce_sum.75
  180.0 0.6 fusion.57
  (19 shorter events, 0.3 us)
Async XLA Ops:
  0.6 27.5 %copy-start = (bf16[4096,128]{1,0:T(8,128)(2,1)S(1)}, bf16[4096,128]{1,0:T(8,128)(2,1)}, u32[]{:S(2)}) copy-start(bf16[4096,128]{1,0:T(8,128)(2,1)} %param.21) | copy-start | bytes 3145732
  0.6 30.7 %copy-start.4 = (f32[4096]{0:T(1024)S(1)}, f32[4096]{0:T(1024)}, u32[]{:S(2)}) copy-start(f32[4096]{0:T(1024)} %param.18) | copy-start | bytes 49156
  3.9 72.2 %copy-start.7 = (pred[32]{0:T(512)(128)(4,1)}, pred[32]{0:T(512)(128)(4,1)S(1)}, u32[]{:S(2)}) copy-start(pred[32]{0:T(512)(128)(4,1)S(1)} %iota_compare_fusion.3) | copy-start | bytes 100
  29.5 1.8 %copy-start.6 = (bf16[64,128]{1,0:T(8,128)(2,1)}, bf16[64,128]{1,0:T(8,128)(2,1)S(1)}, u32[]{:S(2)}) copy-start(bf16[64,128]{1,0:T(8,128)(2,1)S(1)} %convolution_convert_fusion.1) | copy-start | bytes 49156
  29.5 6.0 %copy-start.1 = (bf16[1,1024,128]{2,1,0:T(8,128)(2,1)S(1)}, bf16[1,1024,128]{2,1,0:T(8,128)(2,1)}, u32[]{:S(2)}) copy-start(bf16[1,1024,128]{2,1,0:T(8,128)(2,1)} %param.16) | copy-start | bytes 786436
  34.6 42.1 %copy-start.2 = (bf16[1,1024,128]{2,1,0:T(8,128)(2,1)S(1)}, bf16[1,1024,128]{2,1,0:T(8,128)(2,1)}, u32[]{:S(2)}) copy-start(bf16[1,1024,128]{2,1,0:T(8,128)(2,1)} %param.17) | copy-start | bytes 786436
  35.1 42.8 %copy-start.3 = (bf16[64,1,64]{2,0,1:T(8,128)(2,1)}, bf16[64,1,64]{2,0,1:T(8,128)(2,1)S(1)}, u32[]{:S(2)}) copy-start(bf16[64,1,64]{2,0,1:T(8,128)(2,1)S(1)} %get-tuple-element.21) | copy-start | bytes 24580
  86.9 57.8 %all-to-all-start = ((bf16[32,2,144,128]{3,2,1,0:T(8,128)(2,1)}), bf16[32,2,144,128]{3,2,1,0:T(8,128)(2,1)S(1)}, u32[]{:S(2)}, u32[]{:S(2)}) async-start(bf16[32,2,144,128]{3,2,1,0:T(8,128)(2,1)} %bitcast.54), calls=%async_computation | async-start | bytes 4718592 | tf_op jit(solution)/shard_map/all_to_all | solution.py:401
  95.0 0.6 copy-start.5

commit v6 on v5

--- a/solution.py
+++ b/solution.py
@@ -225,47 +225,41 @@
         c.wait()
     own.wait()
 
-    plus_steps = nz // 2
-    minus_steps = nz - 1 - plus_steps
+    steps = nz // 2
+    half = nx // 2
+    last = {}
     sent = []
-    for t in range(1, plus_steps + 1):
-        step = []
-        column = lax.rem(z - (t - 1) + nz, nz)
-        bundle = pl.ds(pl.multiple_of(column * nx, nx), nx)
-        c = pltpu.make_async_remote_copy(
-            src_ref=y_ref.at[bundle],
-            dst_ref=y_ref.at[bundle],
-            send_sem=zp_send.at[t],
-            recv_sem=zp_recv.at[t],
-            device_id=(x * nz + up, mp),
-            device_id_type=MESH,
-        )
-        c.start()
-        step.append(c)
-        if t <= minus_steps:
-            column = lax.rem(z + (t - 1), nz)
-            bundle = pl.ds(pl.multiple_of(column * nx, nx), nx)
-            c = pltpu.make_async_remote_copy(
-                src_ref=y_ref.at[bundle],
-                dst_ref=y_ref.at[bundle],
-                send_sem=zm_send.at[t],
-                recv_sem=zm_recv.at[t],
-                device_id=(x * nz + down, mp),
-                device_id_type=MESH,
-            )
-            c.start()
-            step.append(c)
-        for c in step:
-            c.wait_recv()
-        sent += step
+    for t in range(1, steps + 1):
+        for i in range(nx):
+            for sign, send_sem, recv_sem, target in (
+                (1, zp_send, zp_recv, up),
+                (-1, zm_send, zm_recv, down),
+            ):
+                if t == steps and (i < half) != (sign == 1):
+                    continue
+                if t > 1:
+                    last[(sign, i)].wait_recv()
+                column = lax.rem(z - sign * (t - 1) + nz, nz)
+                c = pltpu.make_async_remote_copy(
+                    src_ref=y_ref.at[column * nx + i],
+                    dst_ref=y_ref.at[column * nx + i],
+                    send_sem=send_sem.at[t, i],
+                    recv_sem=recv_sem.at[t, i],
+                    device_id=(x * nz + target, mp),
+                    device_id_type=MESH,
+                )
+                c.start()
+                last[(sign, i)] = c
+                sent.append(c)
+    for c in last.values():
+        c.wait_recv()
     for c in sent:
         c.wait_send()
 
 
 def relay_gather(x, nx, nz):
     vmem = pl.BlockSpec(memory_space=pltpu.VMEM)
-    plus_steps = nz // 2
-    minus_steps = nz - 1 - plus_steps
+    steps = nz // 2
     return pl.pallas_call(
         functools.partial(relay_gather_kernel, nx, nz),
         in_specs=[vmem],
@@ -274,10 +268,10 @@
         scratch_shapes=[
             pltpu.SemaphoreType.DMA((nx,)),
             pltpu.SemaphoreType.DMA((nx,)),
-            pltpu.SemaphoreType.DMA((plus_steps + 1,)),
-            pltpu.SemaphoreType.DMA((plus_steps + 1,)),
-            pltpu.SemaphoreType.DMA((minus_steps + 1,)),
-            pltpu.SemaphoreType.DMA((minus_steps + 1,)),
+            pltpu.SemaphoreType.DMA((steps + 1, nx)),
+            pltpu.SemaphoreType.DMA((steps + 1, nx)),
+            pltpu.SemaphoreType.DMA((steps + 1, nx)),
+            pltpu.SemaphoreType.DMA((steps + 1, nx)),
             pltpu.SemaphoreType.DMA(()),
         ],
         compiler_params=pltpu.CompilerParams(collective_id=2, has_side_effects=True),

time: 182 us -> 178 us (0.978)
  Pallas kernels: 84.9 us -> 79.3 us
    pallas_call x1, Pallas kernels: 39.7 us -> 35.4 us  [relay_gather(): pl.pallas_call(functools.partial(relay_gather_kernel, nx, nz), in_specs=[...]
where the time goes in v6:
time: 178 us; the launch traced here: 177 us
  Pallas kernels  79.3 us (45%)
  waiting for transfers between devices  48.5 us (27%)
  other arithmetic  17.3 us (10%)
  matrix products  13.4 us (8%)
  local copies, waits for them, and re-layouts  11.2 us (6%)
  starting transfers between devices  5.1 us (3%)
  between operations  2.27 us (1%)
    all_to_all x1, waiting for transfers between devices, local(): lax.all_to_all(packed.reshape(n_seq, 2, block_rows, HEAD_SIZE), 'seq', 0,...  48.5 us
    pallas_call x1, Pallas kernels, relay_gather(): pl.pallas_call(functools.partial(relay_gather_kernel, nx, nz), in_specs=[...  35.4 us
    pallas_call x1, Pallas kernels, mp_scatter(): pl.pallas_call(functools.partial(mp_scatter_kernel, n), in_specs=[vmem],...  21.4 us
    pallas_call x1, Pallas kernels, mp_gather(): pl.pallas_call(functools.partial(mp_gather_kernel, n), in_specs=[vmem], o...  14.5 us
    pallas_call x1, Pallas kernels, passage_attention(): pl.pallas_call(functools.partial(passage_kernel, nx, nz), in_specs=[pl.Bl...  8.01 us
    all_to_all x1, starting transfers between devices, local(): lax.all_to_all(packed.reshape(n_seq, 2, block_rows, HEAD_SIZE), 'seq', 0,...  5.1 us
    dot_general x1, matrix products, local(): projected = jnp.dot(attention, w_out, preferred_element_type=jnp.float32)  4.11 us
  transfers between devices with their start and end apart: 1, of which 1 were waited for; matrix products, arithmetic and copies ran while one was open for 3% of the time, Pallas kernels for 0%

profile of v6, /device:TPU:1, one launch (start us, length us, event | category | flops | bytes accessed | tf_op | source)
XLA Modules:
  0.0 177.2 jit_solution(1233946316306648522)
XLA Ops:
  0.6 0.0 copy-start
  0.6 0.0 copy-start.4
  0.7 1.3 dynamic_slice.21
  2.0 1.2 dynamic_slice.20
  3.2 0.6 iota_compare_fusion.3
  3.9 0.9 select_reduce_fusion.1
  4.8 1.3 fusion.46
  6.1 0.6 dynamic_slice.23
  7.4 0.6 dynamic_slice.22
  8.7 0.1 copy.47
  8.8 0.6 reshape.316.flags_ref
  9.4 0.7 broadcast_add_fusion
  10.1 0.1 fusion.11
  10.2 0.1 broadcast_in_dim.118
  10.2 0.7 reshape_reshape.4.lim_ref
  10.9 1.4 pad_maximum_fusion.x_ref
  12.3 14.5 %shard_map.149 = bf16[64,4096]{1,0:T(8,128)(2,1)} custom-call(bf16[64,512]{1,0:T(8,128)(2,1)} %pad_maximum_fusion.x_ref), custom_call_target="tpu_custom_call" | custom-call | tf_op jit(solution)/shard_map/pallas_call | solution.py:134
  26.8 1.2 fusion.1
  28.1 1.4 convolution_convert_fusion.1
  29.5 0.0 copy-start.6
  29.5 0.0 copy-start.1
  29.5 1.8 %convolution_bitcast_fusion = f32[64,1,128]{2,0,1:T(8,128)S(1)} fusion(bf16[4096,128]{1,0:T(8,128)(2,1)} %param.20, bf16[64,4096]{1,0:T(8,128)(2,1)} %shard_map.149, f32[4096]{0:T(1024)} %param.18, f32[64]{0:T(128)S(1)} %add_rsqrt_fusion), kind=kOutput, calls=%fused_computation.6 | convolution fusion | flops 68157440 | bytes 1622272 | tf_op jit(solution)/shard_map/dot_general | solution.py:346
  31.3 3.2 %fusion.53 = f32[64,512]{1,0:T(8,128)S(1)} fusion(bf16[4096,512]{1,0:T(8,128)(2,1)} %param.19, bf16[64,4096]{1,0:T(8,128)(2,1)} %shard_map.149, f32[4096]{0:T(1024)S(1)} %copy-done.4, f32[64]{0:T(128)S(1)} %add_rsqrt_fusion), kind=kOutput, calls=%fused_computation.102 | convolution fusion | flops 269484032 | bytes 4866304 | tf_op jit(solution)/shard_map/dot_general | solution.py:337
  34.6 0.0 copy-start.2
  34.6 0.1 add_convert_fusion.2
  34.7 0.2 multiply_cosine_fusion.1
  34.9 0.2 fusion.27
  35.1 0.0 copy-start.3
  35.2 0.1 fusion.56
  35.3 0.1 copy.50
  35.4 0.1 copy.51
  35.5 0.0 copy-done.1
  35.5 0.7 pad_maximum_fusion.1.x_ref
  36.2 35.4 %shard_map.150 = bf16[32,2,128,128]{3,2,1,0:T(8,128)(2,1)} custom-call(bf16[2,128,128]{2,1,0:T(8,128)(2,1)} %pad_maximum_fusion.1.x_ref), custom_call_target="tpu_custom_call" | custom-call | tf_op jit(solution)/shard_map/pallas_call | solution.py:263
  71.6 0.1 fusion.42
  71.7 0.4 convolution_convert_fusion
  72.2 0.2 fusion.4
  72.4 1.1 slice_select_fusion
  73.5 8.0 %shard_map.151 = bf16[64,144,128]{2,1,0:T(8,128)(2,1)} custom-call(s32[64]{0:T(128)} %reshape.316.flags_ref, bf16[64,128,128]{2,1,0:T(8,128)(2,1)} %bitcast.55, bf16[1024,128]{1,0:T(8,128)(2,1)} %get-tuple-element.11.k_ref, bf16[1024,128]{1,0:T(8,128)(2,1)} %get-tuple-element.10.v_ref, s32[128,1]{1,0:T(8,128)} %reshape_reshape.4.lim_ref), custom_call_target="tpu_custom_call" | custom-call | tf_op jit(solution)/shard_map/pallas_call | solution.py:94
  81.6 5.1 %all-to-all-start = ((bf16[32,2,144,128]{3,2,1,0:T(8,128)(2,1)}), bf16[32,2,144,128]{3,2,1,0:T(8,128)(2,1)S(1)}, u32[]{:S(2)}, u32[]{:S(2)}) async-start(bf16[32,2,144,128]{3,2,1,0:T(8,128)(2,1)} %bitcast.54), calls=%async_computation | async-start | bytes 4718592 | tf_op jit(solution)/shard_map/all_to_all | solution.py:395
  86.7 1.2 dynamic_slice.19
  87.9 0.6 iota_compare_fusion.4
  88.5 1.3 pad_add_fusion
  89.7 0.1 fusion.40
  89.8 0.9 fusion.58
  90.8 0.5 copy-done.5
  91.3 1.5 fusion.28
  92.8 48.5 %all-to-all-done = bf16[32,2,144,128]{3,2,1,0:T(8,128)(2,1)S(1)} async-done(((bf16[32,2,144,128]{3,2,1,0:T(8,128)(2,1)}), bf16[32,2,144,128]{3,2,1,0:T(8,128)(2,1)S(1)}, u32[]{:S(2)}, u32[]{:S(2)}) %all-to-all-start) | async-done | bytes 2359328 | tf_op jit(solution)/shard_map/all_to_all | solution.py:395
  141.4 0.7 fusion.55
  142.1 0.7 reduce_max.21
  142.8 0.8 copy.53
  143.6 0.7 pad_maximum_fusion.5
  144.3 0.7 copy.54
  145.0 0.9 sub.42
  145.9 0.9 fusion.35
  146.8 0.1 reduce_sum.73
  146.9 0.1 copy.57
  147.0 0.8 subtract_exponential_fusion
  147.7 0.7 compare_select_fusion
  148.4 1.3 multiply_reduce_fusion
  149.7 4.1 %fusion.12.x_ref = f32[64,4096]{1,0:T(8,128)} fusion(bf16[512,4096]{1,0:T(8,128)(2,1)} %param.22, f32[64,4]{0,1:T(4,128)S(1)} %get-tuple-element.4, f32[64,4]{0,1:T(4,128)S(1)} %get-tuple-element.5, f32[32,4,128]{2,0,1:T(8,128)} %fusion.28, f32[64,4,128]{2,1,0:T(4,128)S(1)} %bitcast.56, pred[64]{0:T(512)(128)(4,1)} %pad_add_fusion), kind=kOutput, calls=%fused_computation.27 | convolution fusion | flops 268599296 | bytes 5441600 | tf_op jit(solution)/shard_map/dot_general | solution.py:434
  153.8 21.4 %shard_map.152 = f32[8,64,512]{2,1,0:T(8,128)} custom-call(f32[64,4096]{1,0:T(8,128)} %fusion.12.x_ref), custom_call_target="tpu_custom_call" | custom-call | tf_op jit(solution)/shard_map/pallas_call | solution.py:181
  175.2 1.3 reduce_sum.75
  176.5 0.6 fusion.57
  (19 shorter events, 0.3 us)
Async XLA Ops:
  0.6 27.5 %copy-start = (bf16[4096,128]{1,0:T(8,128)(2,1)S(1)}, bf16[4096,128]{1,0:T(8,128)(2,1)}, u32[]{:S(2)}) copy-start(bf16[4096,128]{1,0:T(8,128)(2,1)} %param.21) | copy-start | bytes 3145732
  0.6 30.7 %copy-start.4 = (f32[4096]{0:T(1024)S(1)}, f32[4096]{0:T(1024)}, u32[]{:S(2)}) copy-start(f32[4096]{0:T(1024)} %param.18) | copy-start | bytes 49156
  3.9 67.8 %copy-start.7 = (pred[32]{0:T(512)(128)(4,1)}, pred[32]{0:T(512)(128)(4,1)S(1)}, u32[]{:S(2)}) copy-start(pred[32]{0:T(512)(128)(4,1)S(1)} %iota_compare_fusion.3) | copy-start | bytes 100
  29.5 1.8 %copy-start.6 = (bf16[64,128]{1,0:T(8,128)(2,1)}, bf16[64,128]{1,0:T(8,128)(2,1)S(1)}, u32[]{:S(2)}) copy-start(bf16[64,128]{1,0:T(8,128)(2,1)S(1)} %convolution_convert_fusion.1) | copy-start | bytes 49156
  29.5 6.0 %copy-start.1 = (bf16[1,1024,128]{2,1,0:T(8,128)(2,1)S(1)}, bf16[1,1024,128]{2,1,0:T(8,128)(2,1)}, u32[]{:S(2)}) copy-start(bf16[1,1024,128]{2,1,0:T(8,128)(2,1)} %param.16) | copy-start | bytes 786436
  34.6 37.8 %copy-start.2 = (bf16[1,1024,128]{2,1,0:T(8,128)(2,1)S(1)}, bf16[1,1024,128]{2,1,0:T(8,128)(2,1)}, u32[]{:S(2)}) copy-start(bf16[1,1024,128]{2,1,0:T(8,128)(2,1)} %param.17) | copy-start | bytes 786436
  35.1 38.5 %copy-start.3 = (bf16[64,1,64]{2,0,1:T(8,128)(2,1)}, bf16[64,1,64]{2,0,1:T(8,128)(2,1)S(1)}, u32[]{:S(2)}) copy-start(bf16[64,1,64]{2,0,1:T(8,128)(2,1)S(1)} %get-tuple-element.21) | copy-start | bytes 24580
  81.6 59.8 %all-to-all-start = ((bf16[32,2,144,128]{3,2,1,0:T(8,128)(2,1)}), bf16[32,2,144,128]{3,2,1,0:T(8,128)(2,1)S(1)}, u32[]{:S(2)}, u32[]{:S(2)}) async-start(bf16[32,2,144,128]{3,2,1,0:T(8,128)(2,1)} %bitcast.54), calls=%async_computation | async-start | bytes 4718592 | tf_op jit(solution)/shard_map/all_to_all | solution.py:395
  90.8 0.6 copy-start.5

commit v7 on v6

--- a/solution.py
+++ b/solution.py
@@ -278,6 +278,137 @@
     )(x)
 
 
+def merge_piece(a, b, rows):
+    af = a.astype(jnp.float32)
+    bf = b.astype(jnp.float32)
+    m1 = af[rows : rows + 1] + af[rows + 1 : rows + 2]
+    l1 = af[rows + 2 : rows + 3] + af[rows + 3 : rows + 4]
+    m2 = bf[rows : rows + 1] + bf[rows + 1 : rows + 2]
+    l2 = bf[rows + 2 : rows + 3] + bf[rows + 3 : rows + 4]
+    top = jnp.maximum(m1, m2)
+    s1 = jnp.exp(m1 - top)
+    s2 = jnp.exp(m2 - top)
+    total = l1 * s1 + l2 * s2
+    c1 = jnp.transpose(jnp.broadcast_to(s1, (rows, rows)))
+    c2 = jnp.transpose(jnp.broadcast_to(s2, (rows, rows)))
+    acc = af[0:rows] * c1 + bf[0:rows] * c2
+    sub = lax.broadcasted_iota(jnp.int32, (16, rows), 0)
+    top_hi = top.astype(jnp.bfloat16).astype(jnp.float32)
+    tot_hi = total.astype(jnp.bfloat16).astype(jnp.float32)
+    st = jnp.where(
+        sub == 0,
+        top,
+        jnp.where(
+            sub == 1, top - top_hi, jnp.where(sub == 2, total, jnp.where(sub == 3, total - tot_hi, 0.0))
+        ),
+    )
+    return acc.astype(jnp.bfloat16), st.astype(jnp.bfloat16)
+
+
+def relay_reduce_kernel(
+    nx, nz, x_ref, y_ref, rp, rm, bp, bm, col, sp_send, sp_recv, sm_send, sm_recv, sx_send, sx_recv
+):
+    me = lax.axis_index("seq")
+    mp = lax.axis_index("mp")
+    x = me // nz
+    z = me % nz
+    up = lax.rem(z + 1, nz)
+    down = lax.rem(z + nz - 1, nz)
+    rows = x_ref.shape[2] - 16
+    barrier = pltpu.get_barrier_semaphore()
+    peers = [(lax.rem(x + k, nx) * nz + z, mp) for k in range(1, nx)]
+    peers += [(x * nz + up, mp), (x * nz + down, mp)]
+    for p in peers:
+        pl.semaphore_signal(barrier, inc=1, device_id=p, device_id_type=MESH)
+    pl.semaphore_wait(barrier, len(peers))
+
+    def merge_into(dst, first, second):
+        for h in range(2):
+            acc, st = merge_piece(first[h], second[h], rows)
+            dst[h, 0:rows] = acc
+            dst[h, rows:] = st
+
+    steps = nz // 2
+    half = nx // 2
+    last = {}
+    sent = []
+    dirs = ((1, rp, bp, sp_send, sp_recv, up), (-1, rm, bm, sm_send, sm_recv, down))
+    for t in range(1, steps + 1):
+        for i in range(nx):
+            for sign, recv_buf, send_buf, send_sem, recv_sem, target in dirs:
+                if t == 1 and (i < half) != (sign == 1):
+                    continue
+                column = lax.rem(z + sign * (steps + 1 - t) + nz, nz)
+                own = x_ref.at[i * nz + column]
+                if (sign, i) in last:
+                    last[(sign, i)].wait_recv()
+                    merge_into(send_buf.at[t, i], own, recv_buf.at[t - 1, i])
+                    src = send_buf.at[t, i]
+                else:
+                    src = own
+                c = pltpu.make_async_remote_copy(
+                    src_ref=src,
+                    dst_ref=recv_buf.at[t, i],
+                    send_sem=send_sem.at[t, i],
+                    recv_sem=recv_sem.at[t, i],
+                    device_id=(x * nz + target, mp),
+                    device_id_type=MESH,
+                )
+                c.start()
+                last[(sign, i)] = c
+                sent.append(c)
+
+    mine = []
+    for i in range(nx):
+        last[(1, i)].wait_recv()
+        last[(-1, i)].wait_recv()
+        merge_into(col.at[i], x_ref.at[i * nz + z], rp.at[steps, i])
+        merge_into(col.at[i], col.at[i], rm.at[steps, i])
+    for k in range(1, nx):
+        target = lax.rem(x + k, nx)
+        c = pltpu.make_async_remote_copy(
+            src_ref=col.at[target],
+            dst_ref=y_ref.at[x],
+            send_sem=sx_send.at[k],
+            recv_sem=sx_recv.at[k],
+            device_id=(target * nz + z, mp),
+            device_id_type=MESH,
+        )
+        c.start()
+        mine.append(c)
+    y_ref[x] = col[x]
+    for c in sent:
+        c.wait_send()
+    for c in mine:
+        c.wait()
+
+
+def relay_reduce(parts, nx, nz):
+    vmem = pl.BlockSpec(memory_space=pltpu.VMEM)
+    steps = nz // 2
+    piece = parts.shape[1:]
+    return pl.pallas_call(
+        functools.partial(relay_reduce_kernel, nx, nz),
+        in_specs=[vmem],
+        out_specs=vmem,
+        out_shape=jax.ShapeDtypeStruct((nx,) + piece, parts.dtype),
+        scratch_shapes=[
+            pltpu.VMEM((steps + 1, nx) + piece, parts.dtype),
+            pltpu.VMEM((steps + 1, nx) + piece, parts.dtype),
+            pltpu.VMEM((steps + 1, nx) + piece, parts.dtype),
+            pltpu.VMEM((steps + 1, nx) + piece, parts.dtype),
+            pltpu.VMEM((nx,) + piece, parts.dtype),
+            pltpu.SemaphoreType.DMA((steps + 1, nx)),
+            pltpu.SemaphoreType.DMA((steps + 1, nx)),
+            pltpu.SemaphoreType.DMA((steps + 1, nx)),
+            pltpu.SemaphoreType.DMA((steps + 1, nx)),
+            pltpu.SemaphoreType.DMA((nx,)),
+            pltpu.SemaphoreType.DMA((nx,)),
+        ],
+        compiler_params=pltpu.CompilerParams(collective_id=3, has_side_effects=True),
+    )(parts)
+
+
 def local(
     prompt_hidden,
     recompute_hidden,
@@ -392,15 +523,14 @@
     packed = passage_attention(nx, nz, flags, q_blocks, passage_keys, passage_values, lim)
     block_rows = packed.shape[1]
 
-    back = lax.all_to_all(
-        packed.reshape(n_seq, 2, block_rows, HEAD_SIZE), "seq", 0, 0, tiled=True
-    )
+    back = relay_reduce(packed.reshape(n_seq, 2, block_rows, HEAD_SIZE), nx, nz)
+    n_parts = back.shape[0]
     rows128 = prompt_rows * local_heads
     stats_back = back[:, :, rows128 : rows128 + 4].astype(jnp.float32)
-    part_max = (stats_back[:, :, 0] + stats_back[:, :, 1]).reshape(n_seq, query_rows, local_heads)
-    part_tot = (stats_back[:, :, 2] + stats_back[:, :, 3]).reshape(n_seq, query_rows, local_heads)
+    part_max = (stats_back[:, :, 0] + stats_back[:, :, 1]).reshape(n_parts, query_rows, local_heads)
+    part_tot = (stats_back[:, :, 2] + stats_back[:, :, 3]).reshape(n_parts, query_rows, local_heads)
     part_acc = (
-        back[:, :, :rows128].reshape(n_seq, query_rows, local_heads, HEAD_SIZE).astype(jnp.float32)
+        back[:, :, :rows128].reshape(n_parts, query_rows, local_heads, HEAD_SIZE).astype(jnp.float32)
     )
 
     pq = queries[:prompt_rows].astype(jnp.float32)

time: 178 us -> 147 us (0.83)
  waiting for transfers between devices: 48.5 us -> 0 us
  Pallas kernels: 79.3 us -> 112 us
  starting transfers between devices: 5.1 us -> 0 us
  other arithmetic: 17.3 us -> 13.3 us
  local copies, waits for them, and re-layouts: 11.2 us -> 8.05 us
  matrix products: 13.4 us -> 11.4 us
    all_to_all x1 -> x0, waiting for transfers between devices: 48.5 us -> none  [local(): lax.all_to_all(packed.reshape(n_seq, 2, block_rows, HEAD_SIZE), 'seq', 0,...]
    pallas_call x0 -> x1, Pallas kernels: none -> 29.8 us  [relay_reduce(): pl.pallas_call(functools.partial(relay_reduce_kernel, nx, nz), in_specs=[...]
    all_to_all x1 -> x0, starting transfers between devices: 5.1 us -> none  [local(): lax.all_to_all(packed.reshape(n_seq, 2, block_rows, HEAD_SIZE), 'seq', 0,...]
  transfers between devices with their start and end apart: 1 -> 0, of which waited for: 1 -> 0; matrix products, arithmetic and copies ran while one was open for 3% -> 0% of each run, Pallas kernels for 0% -> 0%
where the time goes in v7:
time: 147 us; the launch traced here: 146 us
  Pallas kernels  112 us (76%)
  other arithmetic  13.3 us (9%)
  matrix products  11.4 us (8%)
  local copies, waits for them, and re-layouts  8.05 us (5%)
  between operations  2.23 us (2%)
    pallas_call x1, Pallas kernels, relay_gather(): pl.pallas_call(functools.partial(relay_gather_kernel, nx, nz), in_specs=[...  35.4 us
    pallas_call x1, Pallas kernels, relay_reduce(): pl.pallas_call(functools.partial(relay_reduce_kernel, nx, nz), in_specs=[...  29.8 us
    pallas_call x1, Pallas kernels, mp_scatter(): pl.pallas_call(functools.partial(mp_scatter_kernel, n), in_specs=[vmem],...  22.1 us
    pallas_call x1, Pallas kernels, mp_gather(): pl.pallas_call(functools.partial(mp_gather_kernel, n), in_specs=[vmem], o...  14.6 us
    pallas_call x1, Pallas kernels, passage_attention(): pl.pallas_call(functools.partial(passage_kernel, nx, nz), in_specs=[pl.Bl...  9.54 us
    dot_general x1, matrix products, local(): projected = jnp.dot(attention, w_out, preferred_element_type=jnp.float32)  4.06 us
    dot_general x1, matrix products, local(): jnp.dot(normalized_hidden, w_query, preferred_element_type=jnp.float32)  3.29 us

profile of v7, /device:TPU:1, one launch (start us, length us, event | category | flops | bytes accessed | tf_op | source)
XLA Modules:
  0.0 146.4 jit_solution(12369393575804594810)
XLA Ops:
  0.6 0.0 copy-start
  0.6 0.0 copy-start.3
  0.7 1.3 dynamic_slice.21
  2.0 1.2 dynamic_slice.20
  3.2 1.3 dynamic_slice.19
  4.5 1.3 iota_compare_fusion.3
  5.9 1.3 fusion.46
  7.2 0.1 pad_add_fusion
  7.3 0.9 select_reduce_fusion.1
  8.2 0.6 dynamic_slice.23
  9.5 0.6 dynamic_slice.22
  10.7 0.7 broadcast_add_fusion
  11.4 0.1 add_convert_fusion.2
  11.5 0.1 fusion.11
  11.6 0.1 fusion.38
  11.7 0.1 copy.48
  11.8 0.6 reshape.316.flags_ref
  12.4 0.1 broadcast_in_dim.118
  12.5 0.7 reshape_reshape.4.lim_ref
  13.2 1.4 pad_maximum_fusion.x_ref
  14.6 0.2 multiply_cosine_fusion.1
  14.8 14.6 %shard_map.149 = bf16[64,4096]{1,0:T(8,128)(2,1)} custom-call(bf16[64,512]{1,0:T(8,128)(2,1)} %pad_maximum_fusion.x_ref), custom_call_target="tpu_custom_call" | custom-call | tf_op jit(solution)/shard_map/pallas_call | solution.py:134
  29.4 1.2 fusion.1
  30.7 0.0 copy-done
  30.7 1.4 convolution_convert_fusion.1
  32.1 1.7 %convolution_bitcast_fusion = f32[64,1,128]{2,0,1:T(8,128)S(1)} fusion(bf16[4096,128]{1,0:T(8,128)(2,1)} %param.20, bf16[64,4096]{1,0:T(8,128)(2,1)} %shard_map.149, f32[4096]{0:T(1024)} %param.18, f32[64]{0:T(128)S(1)} %add_rsqrt_fusion), kind=kOutput, calls=%fused_computation.5 | convolution fusion | flops 68157440 | bytes 1622272 | tf_op jit(solution)/shard_map/dot_general | solution.py:477
  33.9 0.0 copy-done.3
  33.9 0.0 copy-start.1
  33.9 0.0 copy-start.2
  33.9 3.3 %fusion.53 = f32[64,512]{1,0:T(8,128)S(1)} fusion(bf16[4096,512]{1,0:T(8,128)(2,1)} %param.19, bf16[64,4096]{1,0:T(8,128)(2,1)} %shard_map.149, f32[4096]{0:T(1024)S(1)} %copy-done.3, f32[64]{0:T(128)S(1)} %add_rsqrt_fusion), kind=kOutput, calls=%fused_computation.102 | convolution fusion | flops 269484032 | bytes 4866304 | tf_op jit(solution)/shard_map/dot_general | solution.py:468
  37.2 0.2 fusion.27
  37.4 0.1 fusion.40
  37.5 0.1 fusion.56
  37.7 0.3 fusion.58
  38.0 0.1 copy.51
  38.0 0.1 copy.52
  38.1 0.7 pad_maximum_fusion.1.x_ref
  38.8 0.2 fusion.28
  39.0 0.4 convolution_convert_fusion
  39.5 0.0 copy-done.1
  39.5 0.2 fusion.4
  39.7 0.0 copy-done.2
  39.8 1.1 slice_select_fusion
  40.9 35.4 %shard_map.150 = bf16[32,2,128,128]{3,2,1,0:T(8,128)(2,1)} custom-call(bf16[2,128,128]{2,1,0:T(8,128)(2,1)} %pad_maximum_fusion.1.x_ref), custom_call_target="tpu_custom_call" | custom-call | tf_op jit(solution)/shard_map/pallas_call | solution.py:263
  76.3 9.5 %shard_map.151 = bf16[64,144,128]{2,1,0:T(8,128)(2,1)} custom-call(s32[64]{0:T(128)} %reshape.316.flags_ref, bf16[64,128,128]{2,1,0:T(8,128)(2,1)} %bitcast.55, bf16[1024,128]{1,0:T(8,128)(2,1)} %get-tuple-element.11.k_ref, bf16[1024,128]{1,0:T(8,128)(2,1)} %get-tuple-element.10.v_ref, s32[128,1]{1,0:T(8,128)} %reshape_reshape.4.lim_ref), custom_call_target="tpu_custom_call" | custom-call | tf_op jit(solution)/shard_map/pallas_call | solution.py:94
  85.9 29.8 %shard_map.152 = bf16[4,2,144,128]{3,2,1,0:T(8,128)(2,1)} custom-call(bf16[32,2,144,128]{3,2,1,0:T(8,128)(2,1)} %bitcast.54), custom_call_target="tpu_custom_call" | custom-call | tf_op jit(solution)/shard_map/pallas_call | solution.py:390
  115.7 0.7 slice_convert_fusion
  116.5 0.1 reduce_max.21
  116.6 0.1 copy.54
  116.7 0.1 copy.55
  116.8 0.1 sub.42
  116.9 1.2 multiply_reduce_fusion
  118.1 0.1 reduce_sum.73
  118.2 0.1 copy.58
  118.3 4.1 %fusion.12.x_ref = f32[64,4096]{1,0:T(8,128)} fusion(bf16[512,4096]{1,0:T(8,128)(2,1)} %param.22, f32[64,4]{0,1:T(4,128)S(1)} %get-tuple-element.4, f32[64,4]{0,1:T(4,128)S(1)} %get-tuple-element.5, f32[32,4,128]{2,0,1:T(8,128)S(1)} %fusion.28, f32[64,4,128]{2,1,0:T(4,128)S(1)} %bitcast.56, pred[64]{0:T(512)(128)(4,1)S(1)} %pad_add_fusion), kind=kOutput, calls=%fused_computation.27 | convolution fusion | flops 268599296 | bytes 5441600 | tf_op jit(solution)/shard_map/dot_general | solution.py:564
  122.4 22.1 %shard_map.153 = f32[8,64,512]{2,1,0:T(8,128)} custom-call(f32[64,4096]{1,0:T(8,128)} %fusion.12.x_ref), custom_call_target="tpu_custom_call" | custom-call | tf_op jit(solution)/shard_map/pallas_call | solution.py:181
  144.5 1.3 reduce_sum.75
  145.8 0.6 fusion.57
  (15 shorter events, 0.3 us)
Async XLA Ops:
  0.6 30.1 %copy-start = (bf16[4096,128]{1,0:T(8,128)(2,1)S(1)}, bf16[4096,128]{1,0:T(8,128)(2,1)}, u32[]{:S(2)}) copy-start(bf16[4096,128]{1,0:T(8,128)(2,1)} %param.21) | copy-start | bytes 3145732
  0.6 33.2 %copy-start.3 = (f32[4096]{0:T(1024)S(1)}, f32[4096]{0:T(1024)}, u32[]{:S(2)}) copy-start(f32[4096]{0:T(1024)} %param.18) | copy-start | bytes 49156
  33.9 5.6 %copy-start.1 = (bf16[1,1024,128]{2,1,0:T(8,128)(2,1)S(1)}, bf16[1,1024,128]{2,1,0:T(8,128)(2,1)}, u32[]{:S(2)}) copy-start(bf16[1,1024,128]{2,1,0:T(8,128)(2,1)} %param.16) | copy-start | bytes 786436
  33.9 5.9 %copy-start.2 = (bf16[1,1024,128]{2,1,0:T(8,128)(2,1)S(1)}, bf16[1,1024,128]{2,1,0:T(8,128)(2,1)}, u32[]{:S(2)}) copy-start(bf16[1,1024,128]{2,1,0:T(8,128)(2,1)} %param.17) | copy-start | bytes 786436

commit v8 on v7

--- a/solution.py
+++ b/solution.py
@@ -562,7 +562,8 @@
         own_live[:, None, None], accumulated / safe_totals[..., None], 0.0
     ).astype(jnp.bfloat16).reshape(query_rows, local_heads * HEAD_SIZE)
     projected = jnp.dot(attention, w_out, preferred_element_type=jnp.float32)
-    combined = jnp.sum(mp_scatter(projected, n_mp), axis=0).astype(jnp.bfloat16)
+    shares = mp_scatter(projected.astype(jnp.bfloat16), n_mp)
+    combined = jnp.sum(shares.astype(jnp.float32), axis=0).astype(jnp.bfloat16)
     return (combined[:prompt_rows], combined[prompt_rows:])
 
 

time: 147 us -> 139 us (0.946)
  Pallas kernels: 112 us -> 103 us
    pallas_call x1, Pallas kernels: 22.1 us -> 15.7 us  [mp_scatter(): pl.pallas_call(functools.partial(mp_scatter_kernel, n), in_specs=[vmem],...]
    pallas_call x1, Pallas kernels: 9.54 us -> 7 us  [passage_attention(): pl.pallas_call(functools.partial(passage_kernel, nx, nz), in_specs=[pl.Bl...]
where the time goes in v8:
time: 139 us; the launch traced here: 138 us
  Pallas kernels  103 us (74%)
  other arithmetic  13.1 us (9%)
  matrix products  11.2 us (8%)
  local copies, waits for them, and re-layouts  8.05 us (6%)
  between operations  2.23 us (2%)
    pallas_call x1, Pallas kernels, relay_gather(): pl.pallas_call(functools.partial(relay_gather_kernel, nx, nz), in_specs=[...  35.4 us
    pallas_call x1, Pallas kernels, relay_reduce(): pl.pallas_call(functools.partial(relay_reduce_kernel, nx, nz), in_specs=[...  30.6 us
    pallas_call x1, Pallas kernels, mp_scatter(): pl.pallas_call(functools.partial(mp_scatter_kernel, n), in_specs=[vmem],...  15.7 us
    pallas_call x1, Pallas kernels, mp_gather(): pl.pallas_call(functools.partial(mp_gather_kernel, n), in_specs=[vmem], o...  14.6 us
    pallas_call x1, Pallas kernels, passage_attention(): pl.pallas_call(functools.partial(passage_kernel, nx, nz), in_specs=[pl.Bl...  7 us
    dot_general x1, matrix products, local(): projected = jnp.dot(attention, w_out, preferred_element_type=jnp.float32)  3.86 us
    dot_general x1, matrix products, local(): jnp.dot(normalized_hidden, w_query, preferred_element_type=jnp.float32)  3.29 us

profile of v8, /device:TPU:1, one launch (start us, length us, event | category | flops | bytes accessed | tf_op | source)
XLA Modules:
  0.0 137.9 jit_solution(3071444345458356810)
XLA Ops:
  0.6 0.0 copy-start
  0.6 0.0 copy-start.3
  0.7 1.3 dynamic_slice.21
  2.0 1.2 dynamic_slice.20
  3.2 1.3 dynamic_slice.19
  4.5 1.3 iota_compare_fusion.3
  5.9 1.3 fusion.45
  7.2 0.1 pad_add_fusion
  7.3 0.9 select_reduce_fusion.1
  8.2 0.6 dynamic_slice.23
  9.5 0.6 dynamic_slice.22
  10.7 0.7 broadcast_add_fusion
  11.4 0.1 add_convert_fusion.2
  11.5 0.1 fusion.11
  11.6 0.1 fusion.37
  11.7 0.1 copy.48
  11.8 0.6 reshape.316.flags_ref
  12.4 0.1 broadcast_in_dim.118
  12.5 0.7 reshape_reshape.4.lim_ref
  13.2 1.4 %pad_maximum_fusion.x_ref = bf16[64,512]{1,0:T(8,128)(2,1)} fusion(bf16[32,512]{1,0:T(8,128)(2,1)} %param.15, bf16[32,512]{1,0:T(8,128)(2,1)} %param.14), kind=kLoop, calls=%fused_computation.30 | loop fusion | flops 131072 | bytes 131072 | tf_op jit(solution)/shard_map/concatenate | solution.py:462
  14.6 0.2 multiply_cosine_fusion.1
  14.8 14.6 %shard_map.149 = bf16[64,4096]{1,0:T(8,128)(2,1)} custom-call(bf16[64,512]{1,0:T(8,128)(2,1)} %pad_maximum_fusion.x_ref), custom_call_target="tpu_custom_call" | custom-call | tf_op jit(solution)/shard_map/pallas_call | solution.py:134
  29.4 1.2 fusion.1
  30.7 0.0 copy-done
  30.7 1.4 %convolution_convert_fusion.2 = bf16[64,128]{1,0:T(8,128)(2,1)S(1)} fusion(bf16[4096,128]{1,0:T(8,128)(2,1)S(1)} %copy-done, bf16[64,4096]{1,0:T(8,128)(2,1)} %shard_map.149, f32[4096]{0:T(1024)} %param.18, f32[64]{0:T(128)S(1)} %add_rsqrt_fusion), kind=kOutput, calls=%fused_computation.7 | convolution fusion | flops 68165632 | bytes 1605888 | tf_op jit(solution)/shard_map/dot_general | solution.py:485
  32.1 1.7 %convolution_bitcast_fusion = f32[64,1,128]{2,0,1:T(8,128)S(1)} fusion(bf16[4096,128]{1,0:T(8,128)(2,1)} %param.20, bf16[64,4096]{1,0:T(8,128)(2,1)} %shard_map.149, f32[4096]{0:T(1024)} %param.18, f32[64]{0:T(128)S(1)} %add_rsqrt_fusion), kind=kOutput, calls=%fused_computation.6 | convolution fusion | flops 68157440 | bytes 1622272 | tf_op jit(solution)/shard_map/dot_general | solution.py:477
  33.9 0.0 copy-done.3
  33.9 0.0 copy-start.1
  33.9 0.0 copy-start.2
  33.9 3.3 %fusion.52 = f32[64,512]{1,0:T(8,128)S(1)} fusion(bf16[4096,512]{1,0:T(8,128)(2,1)} %param.19, bf16[64,4096]{1,0:T(8,128)(2,1)} %shard_map.149, f32[4096]{0:T(1024)S(1)} %copy-done.3, f32[64]{0:T(128)S(1)} %add_rsqrt_fusion), kind=kOutput, calls=%fused_computation.102 | convolution fusion | flops 269484032 | bytes 4866304 | tf_op jit(solution)/shard_map/dot_general | solution.py:468
  37.2 0.2 fusion.26
  37.4 0.1 fusion.39
  37.5 0.1 fusion.55
  37.7 0.3 fusion.57
  38.0 0.1 copy.51
  38.0 0.1 copy.52
  38.1 0.7 pad_maximum_fusion.1.x_ref
  38.8 0.2 fusion.27
  39.0 0.4 convolution_convert_fusion.1
  39.5 0.0 copy-done.1
  39.5 0.2 fusion.4
  39.7 0.0 copy-done.2
  39.8 1.1 slice_select_fusion
  40.9 35.4 %shard_map.150 = bf16[32,2,128,128]{3,2,1,0:T(8,128)(2,1)} custom-call(bf16[2,128,128]{2,1,0:T(8,128)(2,1)} %pad_maximum_fusion.1.x_ref), custom_call_target="tpu_custom_call" | custom-call | tf_op jit(solution)/shard_map/pallas_call | solution.py:263
  76.3 7.0 %shard_map.151 = bf16[64,144,128]{2,1,0:T(8,128)(2,1)} custom-call(s32[64]{0:T(128)} %reshape.316.flags_ref, bf16[64,128,128]{2,1,0:T(8,128)(2,1)} %bitcast.55, bf16[1024,128]{1,0:T(8,128)(2,1)} %get-tuple-element.11.k_ref, bf16[1024,128]{1,0:T(8,128)(2,1)} %get-tuple-element.10.v_ref, s32[128,1]{1,0:T(8,128)} %reshape_reshape.4.lim_ref), custom_call_target="tpu_custom_call" | custom-call | tf_op jit(solution)/shard_map/pallas_call | solution.py:94
  83.3 30.6 %shard_map.152 = bf16[4,2,144,128]{3,2,1,0:T(8,128)(2,1)} custom-call(bf16[32,2,144,128]{3,2,1,0:T(8,128)(2,1)} %bitcast.54), custom_call_target="tpu_custom_call" | custom-call | tf_op jit(solution)/shard_map/pallas_call | solution.py:390
  114.0 0.7 slice_convert_fusion
  114.7 0.1 reduce_max.21
  114.8 0.1 copy.54
  114.9 0.1 copy.55
  115.0 0.1 sub.42
  115.2 1.2 multiply_reduce_fusion
  116.3 0.1 reduce_sum.76
  116.5 0.1 copy.58
  116.6 3.9 %convolution_convert_fusion.x_ref = bf16[64,4096]{1,0:T(8,128)(2,1)} fusion(bf16[512,4096]{1,0:T(8,128)(2,1)} %param.22, f32[64,4]{0,1:T(4,128)S(1)} %get-tuple-element.4, f32[64,4]{0,1:T(4,128)S(1)} %get-tuple-element.5, f32[32,4,128]{2,0,1:T(8,128)S(1)} %fusion.27, f32[64,4,128]{2,1,0:T(4,128)S(1)} %bitcast.56, pred[64]{0:T(512)(128)(4,1)S(1)} %pad_add_fusion), kind=kOutput, calls=%fused_computation | convolution fusion | flops 268861440 | bytes 4917312 | tf_op jit(solution)/shard_map/dot_general | solution.py:564
  120.4 15.7 %shard_map.153 = bf16[8,64,512]{2,1,0:T(8,128)(2,1)} custom-call(bf16[64,4096]{1,0:T(8,128)(2,1)} %convolution_convert_fusion.x_ref), custom_call_target="tpu_custom_call" | custom-call | tf_op jit(solution)/shard_map/pallas_call | solution.py:181
  136.1 1.1 reduce_sum.78
  137.2 0.6 fusion.56
  (15 shorter events, 0.3 us)
Async XLA Ops:
  0.6 30.1 %copy-start = (bf16[4096,128]{1,0:T(8,128)(2,1)S(1)}, bf16[4096,128]{1,0:T(8,128)(2,1)}, u32[]{:S(2)}) copy-start(bf16[4096,128]{1,0:T(8,128)(2,1)} %param.21) | copy-start | bytes 3145732
  0.6 33.2 %copy-start.3 = (f32[4096]{0:T(1024)S(1)}, f32[4096]{0:T(1024)}, u32[]{:S(2)}) copy-start(f32[4096]{0:T(1024)} %param.18) | copy-start | bytes 49156
  33.9 5.6 %copy-start.1 = (bf16[1,1024,128]{2,1,0:T(8,128)(2,1)S(1)}, bf16[1,1024,128]{2,1,0:T(8,128)(2,1)}, u32[]{:S(2)}) copy-start(bf16[1,1024,128]{2,1,0:T(8,128)(2,1)} %param.16) | copy-start | bytes 786436
  33.9 5.9 %copy-start.2 = (bf16[1,1024,128]{2,1,0:T(8,128)(2,1)S(1)}, bf16[1,1024,128]{2,1,0:T(8,128)(2,1)}, u32[]{:S(2)}) copy-start(bf16[1,1024,128]{2,1,0:T(8,128)(2,1)} %param.17) | copy-start | bytes 786436

commit v9 on v8

--- a/solution.py
+++ b/solution.py
@@ -192,13 +192,18 @@
     )(x)
 
 
-def relay_gather_kernel(nx, nz, x_ref, y_ref, sx_send, sx_recv, zp_send, zp_recv, zm_send, zm_recv, own_sem):
+def relay_gather_kernel(nx, nz, x_ref, y_ref, *sems):
+    (sx_send, sx_recv, zp_send, zp_recv, zm_send, zm_recv, own_sem,
+     bp_send, bp_recv, bm_send, bm_recv, xp_send, xp_recv, xm_send, xm_recv,
+     fp_send, fp_recv, fm_send, fm_recv) = sems
     me = lax.axis_index("seq")
     mp = lax.axis_index("mp")
     x = me // nz
     z = me % nz
     up = lax.rem(z + 1, nz)
     down = lax.rem(z + nz - 1, nz)
+    right = lax.rem(x + 1, nx)
+    left = lax.rem(x + nx - 1, nx)
     barrier = pltpu.get_barrier_semaphore()
     peers = [(lax.rem(x + k, nx) * nz + z, mp) for k in range(1, nx)]
     peers += [(x * nz + up, mp), (x * nz + down, mp)]
@@ -206,30 +211,65 @@
         pl.semaphore_signal(barrier, inc=1, device_id=p, device_id_type=MESH)
     pl.semaphore_wait(barrier, len(peers))
 
+    def copy(src, dst, send_sem, recv_sem, device):
+        c = pltpu.make_async_remote_copy(
+            src_ref=src,
+            dst_ref=dst,
+            send_sem=send_sem,
+            recv_sem=recv_sem,
+            device_id=device,
+            device_id_type=MESH,
+        )
+        c.start()
+        return c
+
+    sent = []
     slot = z * nx + x
-    first = []
-    for k in range(1, nx):
-        c = pltpu.make_async_remote_copy(
-            src_ref=x_ref,
-            dst_ref=y_ref.at[slot],
-            send_sem=sx_send.at[k],
-            recv_sem=sx_recv.at[k],
-            device_id=peers[k - 1],
-            device_id_type=MESH,
-        )
-        c.start()
-        first.append(c)
+    first = [
+        copy(x_ref.at[0], y_ref.at[slot, 0], sx_send.at[k], sx_recv.at[k], peers[k - 1])
+        for k in range(1, nx)
+    ]
     own = pltpu.make_async_copy(x_ref, y_ref.at[slot], own_sem)
     own.start()
+
+    def x_out(column):
+        a = copy(
+            y_ref.at[column * nx + x, 1], y_ref.at[column * nx + x, 1],
+            xp_send.at[column], xp_recv.at[column], (right * nz + z, mp),
+        )
+        b = copy(
+            y_ref.at[column * nx + x, 1], y_ref.at[column * nx + x, 1],
+            xm_send.at[column], xm_recv.at[column], (left * nz + z, mp),
+        )
+        return [a, b]
+
+    own.wait()
+    steps = nz // 2
+    half = nx // 2
+    zlast = {}
+    blast = {}
+    xcopies = {}
     for c in first:
         c.wait()
-    own.wait()
-
-    steps = nz // 2
-    half = nx // 2
-    last = {}
-    sent = []
     for t in range(1, steps + 1):
+        for sign, send_sem, recv_sem, target, count in (
+            (1, bp_send, bp_recv, up, steps),
+            (-1, bm_send, bm_recv, down, nz - 1 - steps),
+        ):
+            if t > count:
+                continue
+            if t > 1:
+                blast[sign].wait_recv()
+            column = lax.rem(z - sign * (t - 1) + nz, nz)
+            if t > 1:
+                xcopies[(sign, t - 1)] = x_out(column)
+            elif sign == 1:
+                xcopies[(0, 0)] = x_out(column)
+            blast[sign] = copy(
+                y_ref.at[column * nx + x, 1], y_ref.at[column * nx + x, 1],
+                send_sem.at[t], recv_sem.at[t], (x * nz + target, mp),
+            )
+            sent.append(blast[sign])
         for i in range(nx):
             for sign, send_sem, recv_sem, target in (
                 (1, zp_send, zp_recv, up),
@@ -238,41 +278,68 @@
                 if t == steps and (i < half) != (sign == 1):
                     continue
                 if t > 1:
-                    last[(sign, i)].wait_recv()
+                    zlast[(sign, i)].wait_recv()
                 column = lax.rem(z - sign * (t - 1) + nz, nz)
-                c = pltpu.make_async_remote_copy(
-                    src_ref=y_ref.at[column * nx + i],
-                    dst_ref=y_ref.at[column * nx + i],
-                    send_sem=send_sem.at[t, i],
-                    recv_sem=recv_sem.at[t, i],
-                    device_id=(x * nz + target, mp),
-                    device_id_type=MESH,
+                zlast[(sign, i)] = copy(
+                    y_ref.at[column * nx + i, 0], y_ref.at[column * nx + i, 0],
+                    send_sem.at[t, i], recv_sem.at[t, i], (x * nz + target, mp),
                 )
-                c.start()
-                last[(sign, i)] = c
-                sent.append(c)
-    for c in last.values():
+                sent.append(zlast[(sign, i)])
+    for sign, count in ((1, steps), (-1, nz - 1 - steps)):
+        blast[sign].wait_recv()
+        column = lax.rem(z - sign * count + nz, nz)
+        xcopies[(sign, count)] = x_out(column)
+    order = [(0, 0)] + [(s, t) for t in range(1, steps + 1) for s in (1, -1) if (s, t) in xcopies]
+    forwards = []
+    for key in order:
+        sign, t = key
+        column = lax.rem(z - sign * t + nz, nz)
+        from_left, from_right = xcopies[key]
+        from_left.wait_recv()
+        from_right.wait_recv()
+        sent += xcopies[key]
+    for zc in range(nz):
+        if zc < nz // 2:
+            forwards.append(
+                copy(
+                    y_ref.at[zc * nx + left, 1], y_ref.at[zc * nx + left, 1],
+                    fp_send.at[zc], fp_recv.at[zc], (right * nz + z, mp),
+                )
+            )
+        else:
+            forwards.append(
+                copy(
+                    y_ref.at[zc * nx + right, 1], y_ref.at[zc * nx + right, 1],
+                    fm_send.at[zc], fm_recv.at[zc], (left * nz + z, mp),
+                )
+            )
+    for c in zlast.values():
+        c.wait_recv()
+    for c in forwards:
         c.wait_recv()
     for c in sent:
         c.wait_send()
+    for c in forwards:
+        c.wait_send()
 
 
 def relay_gather(x, nx, nz):
+    assert nx == 4 and nz % 2 == 0
     vmem = pl.BlockSpec(memory_space=pltpu.VMEM)
     steps = nz // 2
+    dma = pltpu.SemaphoreType.DMA
     return pl.pallas_call(
         functools.partial(relay_gather_kernel, nx, nz),
         in_specs=[vmem],
         out_specs=vmem,
         out_shape=jax.ShapeDtypeStruct((nx * nz,) + x.shape, x.dtype),
         scratch_shapes=[
-            pltpu.SemaphoreType.DMA((nx,)),
-            pltpu.SemaphoreType.DMA((nx,)),
-            pltpu.SemaphoreType.DMA((steps + 1, nx)),
-            pltpu.SemaphoreType.DMA((steps + 1, nx)),
-            pltpu.SemaphoreType.DMA((steps + 1, nx)),
-            pltpu.SemaphoreType.DMA((steps + 1, nx)),
-            pltpu.SemaphoreType.DMA(()),
+            dma((nx,)), dma((nx,)),
+            dma((steps + 1, nx)), dma((steps + 1, nx)), dma((steps + 1, nx)), dma((steps + 1, nx)),
+            dma(()),
+            dma((steps + 1,)), dma((steps + 1,)), dma((steps + 1,)), dma((steps + 1,)),
+            dma((nz,)), dma((nz,)), dma((nz,)), dma((nz,)),
+            dma((nz,)), dma((nz,)), dma((nz,)), dma((nz,)),
         ],
         compiler_params=pltpu.CompilerParams(collective_id=2, has_side_effects=True),
     )(x)

time: 139 us -> 139 us (level)
    pallas_call x1, Pallas kernels: 35.4 us -> 33.3 us  [relay_gather(): pl.pallas_call(functools.partial(relay_gather_kernel, nx, nz), in_specs=[...]
    pallas_call x1, Pallas kernels: 15.7 us -> 17.5 us  [mp_scatter(): pl.pallas_call(functools.partial(mp_scatter_kernel, n), in_specs=[vmem],...]
where the time goes in v9:
time: 139 us
  Pallas kernels  104 us (75%)
  other arithmetic  13.1 us (9%)
  matrix products  11.2 us (8%)
  local copies, waits for them, and re-layouts  8.05 us (6%)
  between operations  2.23 us (2%)
    pallas_call x1, Pallas kernels, relay_gather(): pl.pallas_call(functools.partial(relay_gather_kernel, nx, nz), in_specs=[...  33.3 us
    pallas_call x1, Pallas kernels, relay_reduce(): pl.pallas_call(functools.partial(relay_reduce_kernel, nx, nz), in_specs=[...  30.6 us
    pallas_call x1, Pallas kernels, mp_scatter(): pl.pallas_call(functools.partial(mp_scatter_kernel, n), in_specs=[vmem],...  17.5 us
    pallas_call x1, Pallas kernels, mp_gather(): pl.pallas_call(functools.partial(mp_gather_kernel, n), in_specs=[vmem], o...  14.6 us
    pallas_call x1, Pallas kernels, passage_attention(): pl.pallas_call(functools.partial(passage_kernel, nx, nz), in_specs=[pl.Bl...  8.01 us
    dot_general x1, matrix products, local(): projected = jnp.dot(attention, w_out, preferred_element_type=jnp.float32)  3.86 us
    dot_general x1, matrix products, local(): jnp.dot(normalized_hidden, w_query, preferred_element_type=jnp.float32)  3.29 us

profile of v9, /device:TPU:1, one launch (start us, length us, event | category | flops | bytes accessed | tf_op | source)
XLA Modules:
  0.0 138.5 jit_solution(16996798760070316757)
XLA Ops:
  0.6 0.0 copy-start
  0.6 0.0 copy-start.3
  0.7 1.3 dynamic_slice.21
  2.0 1.2 dynamic_slice.20
  3.2 1.3 dynamic_slice.19
  4.5 1.3 iota_compare_fusion.3
  5.9 1.3 fusion.45
  7.2 0.1 pad_add_fusion
  7.3 0.9 select_reduce_fusion.1
  8.2 0.6 dynamic_slice.23
  9.5 0.6 dynamic_slice.22
  10.7 0.7 broadcast_add_fusion
  11.4 0.1 add_convert_fusion.2
  11.5 0.1 fusion.11
  11.6 0.1 fusion.37
  11.7 0.1 copy.48
  11.8 0.6 reshape.316.flags_ref
  12.4 0.1 broadcast_in_dim.118
  12.5 0.7 reshape_reshape.4.lim_ref
  13.2 1.4 %pad_maximum_fusion.x_ref = bf16[64,512]{1,0:T(8,128)(2,1)} fusion(bf16[32,512]{1,0:T(8,128)(2,1)} %param.15, bf16[32,512]{1,0:T(8,128)(2,1)} %param.14), kind=kLoop, calls=%fused_computation.30 | loop fusion | flops 131072 | bytes 131072 | tf_op jit(solution)/shard_map/concatenate | solution.py:529
  14.6 0.2 multiply_cosine_fusion.1
  14.8 14.6 %shard_map.149 = bf16[64,4096]{1,0:T(8,128)(2,1)} custom-call(bf16[64,512]{1,0:T(8,128)(2,1)} %pad_maximum_fusion.x_ref), custom_call_target="tpu_custom_call" | custom-call | tf_op jit(solution)/shard_map/pallas_call | solution.py:134
  29.4 1.2 fusion.1
  30.7 0.0 copy-done
  30.7 1.4 %convolution_convert_fusion.2 = bf16[64,128]{1,0:T(8,128)(2,1)S(1)} fusion(bf16[4096,128]{1,0:T(8,128)(2,1)S(1)} %copy-done, bf16[64,4096]{1,0:T(8,128)(2,1)} %shard_map.149, f32[4096]{0:T(1024)} %param.18, f32[64]{0:T(128)S(1)} %add_rsqrt_fusion), kind=kOutput, calls=%fused_computation.7 | convolution fusion | flops 68165632 | bytes 1605888 | tf_op jit(solution)/shard_map/dot_general | solution.py:552
  32.1 1.7 %convolution_bitcast_fusion = f32[64,1,128]{2,0,1:T(8,128)S(1)} fusion(bf16[4096,128]{1,0:T(8,128)(2,1)} %param.20, bf16[64,4096]{1,0:T(8,128)(2,1)} %shard_map.149, f32[4096]{0:T(1024)} %param.18, f32[64]{0:T(128)S(1)} %add_rsqrt_fusion), kind=kOutput, calls=%fused_computation.6 | convolution fusion | flops 68157440 | bytes 1622272 | tf_op jit(solution)/shard_map/dot_general | solution.py:544
  33.9 0.0 copy-done.3
  33.9 0.0 copy-start.1
  33.9 0.0 copy-start.2
  33.9 3.3 %fusion.52 = f32[64,512]{1,0:T(8,128)S(1)} fusion(bf16[4096,512]{1,0:T(8,128)(2,1)} %param.19, bf16[64,4096]{1,0:T(8,128)(2,1)} %shard_map.149, f32[4096]{0:T(1024)S(1)} %copy-done.3, f32[64]{0:T(128)S(1)} %add_rsqrt_fusion), kind=kOutput, calls=%fused_computation.102 | convolution fusion | flops 269484032 | bytes 4866304 | tf_op jit(solution)/shard_map/dot_general | solution.py:535
  37.2 0.2 fusion.26
  37.4 0.1 fusion.39
  37.5 0.1 fusion.55
  37.7 0.3 fusion.57
  38.0 0.1 copy.51
  38.0 0.1 copy.52
  38.1 0.7 pad_maximum_fusion.1.x_ref
  38.8 0.2 fusion.27
  39.0 0.4 convolution_convert_fusion.1
  39.5 0.0 copy-done.1
  39.5 0.2 fusion.4
  39.7 0.0 copy-done.2
  39.8 1.1 slice_select_fusion
  40.9 33.3 %shard_map.150 = bf16[32,2,128,128]{3,2,1,0:T(8,128)(2,1)} custom-call(bf16[2,128,128]{2,1,0:T(8,128)(2,1)} %pad_maximum_fusion.1.x_ref), custom_call_target="tpu_custom_call" | custom-call | tf_op jit(solution)/shard_map/pallas_call | solution.py:331
  74.2 8.0 %shard_map.151 = bf16[64,144,128]{2,1,0:T(8,128)(2,1)} custom-call(s32[64]{0:T(128)} %reshape.316.flags_ref, bf16[64,128,128]{2,1,0:T(8,128)(2,1)} %bitcast.55, bf16[1024,128]{1,0:T(8,128)(2,1)} %get-tuple-element.11.k_ref, bf16[1024,128]{1,0:T(8,128)(2,1)} %get-tuple-element.10.v_ref, s32[128,1]{1,0:T(8,128)} %reshape_reshape.4.lim_ref), custom_call_target="tpu_custom_call" | custom-call | tf_op jit(solution)/shard_map/pallas_call | solution.py:94
  82.2 30.6 %shard_map.152 = bf16[4,2,144,128]{3,2,1,0:T(8,128)(2,1)} custom-call(bf16[32,2,144,128]{3,2,1,0:T(8,128)(2,1)} %bitcast.54), custom_call_target="tpu_custom_call" | custom-call | tf_op jit(solution)/shard_map/pallas_call | solution.py:457
  112.8 0.7 slice_convert_fusion
  113.5 0.1 reduce_max.21
  113.6 0.1 copy.54
  113.7 0.1 copy.55
  113.8 0.1 sub.42
  114.0 1.2 multiply_reduce_fusion
  115.2 0.1 reduce_sum.76
  115.3 0.1 copy.58
  115.4 3.9 %convolution_convert_fusion.x_ref = bf16[64,4096]{1,0:T(8,128)(2,1)} fusion(bf16[512,4096]{1,0:T(8,128)(2,1)} %param.22, f32[64,4]{0,1:T(4,128)S(1)} %get-tuple-element.4, f32[64,4]{0,1:T(4,128)S(1)} %get-tuple-element.5, f32[32,4,128]{2,0,1:T(8,128)S(1)} %fusion.27, f32[64,4,128]{2,1,0:T(4,128)S(1)} %bitcast.56, pred[64]{0:T(512)(128)(4,1)S(1)} %pad_add_fusion), kind=kOutput, calls=%fused_computation | convolution fusion | flops 268861440 | bytes 4917312 | tf_op jit(solution)/shard_map/dot_general | solution.py:631
  119.2 17.5 %shard_map.153 = bf16[8,64,512]{2,1,0:T(8,128)(2,1)} custom-call(bf16[64,4096]{1,0:T(8,128)(2,1)} %convolution_convert_fusion.x_ref), custom_call_target="tpu_custom_call" | custom-call | tf_op jit(solution)/shard_map/pallas_call | solution.py:181
  136.8 1.1 reduce_sum.78
  137.9 0.6 fusion.56
  (15 shorter events, 0.3 us)
Async XLA Ops:
  0.6 30.1 %copy-start = (bf16[4096,128]{1,0:T(8,128)(2,1)S(1)}, bf16[4096,128]{1,0:T(8,128)(2,1)}, u32[]{:S(2)}) copy-start(bf16[4096,128]{1,0:T(8,128)(2,1)} %param.21) | copy-start | bytes 3145732
  0.6 33.2 %copy-start.3 = (f32[4096]{0:T(1024)S(1)}, f32[4096]{0:T(1024)}, u32[]{:S(2)}) copy-start(f32[4096]{0:T(1024)} %param.18) | copy-start | bytes 49156
  33.9 5.6 %copy-start.1 = (bf16[1,1024,128]{2,1,0:T(8,128)(2,1)S(1)}, bf16[1,1024,128]{2,1,0:T(8,128)(2,1)}, u32[]{:S(2)}) copy-start(bf16[1,1024,128]{2,1,0:T(8,128)(2,1)} %param.16) | copy-start | bytes 786436
  33.9 5.9 %copy-start.2 = (bf16[1,1024,128]{2,1,0:T(8,128)(2,1)S(1)}, bf16[1,1024,128]{2,1,0:T(8,128)(2,1)}, u32[]{:S(2)}) copy-start(bf16[1,1024,128]{2,1,0:T(8,128)(2,1)} %param.17) | copy-start | bytes 786436

commit v10 on v9

--- a/solution.py
+++ b/solution.py
@@ -55,33 +55,39 @@
         )
         return st.astype(jnp.bfloat16)
 
+    out_ref[:, 0:rows] = jnp.zeros((nb, rows, HEAD_SIZE), out_ref.dtype)
+    floor = jnp.full((16, rows), NEGATIVE_FLOOR, jnp.float32)
+    empty = split(floor, jnp.zeros((16, rows), jnp.float32))
+    out_ref[:, rows:] = jnp.broadcast_to(empty[None], (nb, 16, rows))
+
+    def attend(b, masked):
+        d = b // 2
+        stored = ((d % nz) * nx + d // nz) * 2 + b % 2
+        scores = lax.dot_general(
+            q_ref[stored], k_ref[...], (((1,), (1,)), ((), ())), preferred_element_type=jnp.float32
+        ) * (1.0 / math.sqrt(HEAD_SIZE))
+        if masked:
+            scores = jnp.where(token <= lim_ref[...], scores, NEGATIVE_FLOOR)
+        maxima = jnp.max(scores, axis=1, keepdims=True)
+        weights = jnp.exp(scores - maxima)
+        totals = jnp.sum(weights, axis=1, keepdims=True)
+        out_ref[b, 0:rows] = jnp.dot(
+            weights.astype(jnp.bfloat16), v_ref[...], preferred_element_type=jnp.float32
+        ).astype(out_ref.dtype)
+        m_row = jnp.transpose(jnp.broadcast_to(maxima, (rows, rows)))[0:16]
+        l_row = jnp.transpose(jnp.broadcast_to(totals, (rows, rows)))[0:16]
+        out_ref[b, rows:] = split(m_row, l_row)
+
     def body(b, carry):
         flag = flags_ref[b]
 
-        @pl.when(flag == 0)
+        @pl.when(flag == 1)
         def _():
-            out_ref[b, 0:rows] = jnp.zeros((rows, HEAD_SIZE), out_ref.dtype)
-            floor = jnp.full((16, rows), NEGATIVE_FLOOR, jnp.float32)
-            out_ref[b, rows:] = split(floor, jnp.zeros((16, rows), jnp.float32))
-
-        @pl.when(flag > 0)
+            attend(b, False)
+
+        @pl.when(flag == 2)
         def _():
-            d = b // 2
-            stored = ((d % nz) * nx + d // nz) * 2 + b % 2
-            scores = lax.dot_general(
-                q_ref[stored], k_ref[...], (((1,), (1,)), ((), ())), preferred_element_type=jnp.float32
-            ) * (1.0 / math.sqrt(HEAD_SIZE))
-            limit = jnp.where(flag == 2, lim_ref[...], keys - 1)
-            scores = jnp.where(token <= limit, scores, NEGATIVE_FLOOR)
-            maxima = jnp.max(scores, axis=1, keepdims=True)
-            weights = jnp.exp(scores - maxima)
-            totals = jnp.sum(weights, axis=1, keepdims=True)
-            out_ref[b, 0:rows] = jnp.dot(
-                weights.astype(jnp.bfloat16), v_ref[...], preferred_element_type=jnp.float32
-            ).astype(out_ref.dtype)
-            m_row = jnp.transpose(jnp.broadcast_to(maxima, (rows, rows)))[0:16]
-            l_row = jnp.transpose(jnp.broadcast_to(totals, (rows, rows)))[0:16]
-            out_ref[b, rows:] = split(m_row, l_row)
+            attend(b, True)
 
         return carry
 

time: 139 us -> 138 us (level)
    pallas_call x1, Pallas kernels: 8.01 us -> 5.63 us  [passage_attention(): pl.pallas_call(functools.partial(passage_kernel, nx, nz), in_specs=[pl.Bl...]
where the time goes in v10:
time: 138 us; the launch traced here: 137 us
  Pallas kernels  103 us (75%)
  other arithmetic  13.1 us (9%)
  matrix products  11.2 us (8%)
  local copies, waits for them, and re-layouts  8.05 us (6%)
  between operations  2.23 us (2%)
    pallas_call x1, Pallas kernels, relay_gather(): pl.pallas_call(functools.partial(relay_gather_kernel, nx, nz), in_specs=[...  33.3 us
    pallas_call x1, Pallas kernels, relay_reduce(): pl.pallas_call(functools.partial(relay_reduce_kernel, nx, nz), in_specs=[...  31.4 us
    pallas_call x1, Pallas kernels, mp_scatter(): pl.pallas_call(functools.partial(mp_scatter_kernel, n), in_specs=[vmem],...  17.9 us
    pallas_call x1, Pallas kernels, mp_gather(): pl.pallas_call(functools.partial(mp_gather_kernel, n), in_specs=[vmem], o...  14.6 us
    pallas_call x1, Pallas kernels, passage_attention(): pl.pallas_call(functools.partial(passage_kernel, nx, nz), in_specs=[pl.Bl...  5.63 us
    dot_general x1, matrix products, local(): projected = jnp.dot(attention, w_out, preferred_element_type=jnp.float32)  3.86 us
    dot_general x1, matrix products, local(): jnp.dot(normalized_hidden, w_query, preferred_element_type=jnp.float32)  3.29 us

profile of v10, /device:TPU:1, one launch (start us, length us, event | category | flops | bytes accessed | tf_op | source)
XLA Modules:
  0.0 137.3 jit_solution(8711228402838561032)
XLA Ops:
  0.6 0.0 copy-start
  0.6 0.0 copy-start.3
  0.7 1.3 dynamic_slice.21
  2.0 1.2 dynamic_slice.20
  3.2 1.3 dynamic_slice.19
  4.5 1.3 iota_compare_fusion.3
  5.9 1.3 fusion.45
  7.2 0.1 pad_add_fusion
  7.3 0.9 select_reduce_fusion.1
  8.2 0.6 dynamic_slice.23
  9.5 0.6 dynamic_slice.22
  10.7 0.7 broadcast_add_fusion
  11.4 0.1 add_convert_fusion.2
  11.5 0.1 fusion.11
  11.6 0.1 fusion.37
  11.7 0.1 copy.48
  11.8 0.6 reshape.316.flags_ref
  12.4 0.1 broadcast_in_dim.118
  12.5 0.7 reshape_reshape.4.lim_ref
  13.2 1.4 %pad_maximum_fusion.x_ref = bf16[64,512]{1,0:T(8,128)(2,1)} fusion(bf16[32,512]{1,0:T(8,128)(2,1)} %param.15, bf16[32,512]{1,0:T(8,128)(2,1)} %param.14), kind=kLoop, calls=%fused_computation.30 | loop fusion | flops 131072 | bytes 131072 | tf_op jit(solution)/shard_map/concatenate | solution.py:535
  14.6 0.2 multiply_cosine_fusion.1
  14.8 14.6 %shard_map.149 = bf16[64,4096]{1,0:T(8,128)(2,1)} custom-call(bf16[64,512]{1,0:T(8,128)(2,1)} %pad_maximum_fusion.x_ref), custom_call_target="tpu_custom_call" | custom-call | tf_op jit(solution)/shard_map/pallas_call | solution.py:140
  29.4 1.2 fusion.1
  30.7 0.0 copy-done
  30.7 1.4 %convolution_convert_fusion.2 = bf16[64,128]{1,0:T(8,128)(2,1)S(1)} fusion(bf16[4096,128]{1,0:T(8,128)(2,1)S(1)} %copy-done, bf16[64,4096]{1,0:T(8,128)(2,1)} %shard_map.149, f32[4096]{0:T(1024)} %param.18, f32[64]{0:T(128)S(1)} %add_rsqrt_fusion), kind=kOutput, calls=%fused_computation.7 | convolution fusion | flops 68165632 | bytes 1605888 | tf_op jit(solution)/shard_map/dot_general | solution.py:558
  32.1 1.7 %convolution_bitcast_fusion = f32[64,1,128]{2,0,1:T(8,128)S(1)} fusion(bf16[4096,128]{1,0:T(8,128)(2,1)} %param.20, bf16[64,4096]{1,0:T(8,128)(2,1)} %shard_map.149, f32[4096]{0:T(1024)} %param.18, f32[64]{0:T(128)S(1)} %add_rsqrt_fusion), kind=kOutput, calls=%fused_computation.6 | convolution fusion | flops 68157440 | bytes 1622272 | tf_op jit(solution)/shard_map/dot_general | solution.py:550
  33.9 0.0 copy-done.3
  33.9 0.0 copy-start.1
  33.9 0.0 copy-start.2
  33.9 3.3 %fusion.52 = f32[64,512]{1,0:T(8,128)S(1)} fusion(bf16[4096,512]{1,0:T(8,128)(2,1)} %param.19, bf16[64,4096]{1,0:T(8,128)(2,1)} %shard_map.149, f32[4096]{0:T(1024)S(1)} %copy-done.3, f32[64]{0:T(128)S(1)} %add_rsqrt_fusion), kind=kOutput, calls=%fused_computation.102 | convolution fusion | flops 269484032 | bytes 4866304 | tf_op jit(solution)/shard_map/dot_general | solution.py:541
  37.2 0.2 fusion.26
  37.4 0.1 fusion.39
  37.5 0.1 fusion.55
  37.7 0.3 fusion.57
  38.0 0.1 copy.51
  38.0 0.1 copy.52
  38.1 0.7 pad_maximum_fusion.1.x_ref
  38.8 0.2 fusion.27
  39.0 0.4 convolution_convert_fusion.1
  39.5 0.0 copy-done.1
  39.5 0.2 fusion.4
  39.7 0.0 copy-done.2
  39.8 1.1 slice_select_fusion
  40.9 33.3 %shard_map.150 = bf16[32,2,128,128]{3,2,1,0:T(8,128)(2,1)} custom-call(bf16[2,128,128]{2,1,0:T(8,128)(2,1)} %pad_maximum_fusion.1.x_ref), custom_call_target="tpu_custom_call" | custom-call | tf_op jit(solution)/shard_map/pallas_call | solution.py:337
  74.2 5.6 %shard_map.151 = bf16[64,144,128]{2,1,0:T(8,128)(2,1)} custom-call(s32[64]{0:T(128)} %reshape.316.flags_ref, bf16[64,128,128]{2,1,0:T(8,128)(2,1)} %bitcast.55, bf16[1024,128]{1,0:T(8,128)(2,1)} %get-tuple-element.11.k_ref, bf16[1024,128]{1,0:T(8,128)(2,1)} %get-tuple-element.10.v_ref, s32[128,1]{1,0:T(8,128)} %reshape_reshape.4.lim_ref), custom_call_target="tpu_custom_call" | custom-call | tf_op jit(solution)/shard_map/pallas_call | solution.py:100
  79.8 31.4 %shard_map.152 = bf16[4,2,144,128]{3,2,1,0:T(8,128)(2,1)} custom-call(bf16[32,2,144,128]{3,2,1,0:T(8,128)(2,1)} %bitcast.54), custom_call_target="tpu_custom_call" | custom-call | tf_op jit(solution)/shard_map/pallas_call | solution.py:463
  111.2 0.7 slice_convert_fusion
  111.9 0.1 reduce_max.21
  112.0 0.1 copy.54
  112.1 0.1 copy.55
  112.2 0.1 sub.42
  112.4 1.2 multiply_reduce_fusion
  113.6 0.1 reduce_sum.76
  113.7 0.1 copy.58
  113.8 3.9 %convolution_convert_fusion.x_ref = bf16[64,4096]{1,0:T(8,128)(2,1)} fusion(bf16[512,4096]{1,0:T(8,128)(2,1)} %param.22, f32[64,4]{0,1:T(4,128)S(1)} %get-tuple-element.4, f32[64,4]{0,1:T(4,128)S(1)} %get-tuple-element.5, f32[32,4,128]{2,0,1:T(8,128)S(1)} %fusion.27, f32[64,4,128]{2,1,0:T(4,128)S(1)} %bitcast.56, pred[64]{0:T(512)(128)(4,1)S(1)} %pad_add_fusion), kind=kOutput, calls=%fused_computation | convolution fusion | flops 268861440 | bytes 4917312 | tf_op jit(solution)/shard_map/dot_general | solution.py:637
  117.6 17.9 %shard_map.153 = bf16[8,64,512]{2,1,0:T(8,128)(2,1)} custom-call(bf16[64,4096]{1,0:T(8,128)(2,1)} %convolution_convert_fusion.x_ref), custom_call_target="tpu_custom_call" | custom-call | tf_op jit(solution)/shard_map/pallas_call | solution.py:187
  135.5 1.1 reduce_sum.78
  136.6 0.6 fusion.56
  (15 shorter events, 0.3 us)
Async XLA Ops:
  0.6 30.1 %copy-start = (bf16[4096,128]{1,0:T(8,128)(2,1)S(1)}, bf16[4096,128]{1,0:T(8,128)(2,1)}, u32[]{:S(2)}) copy-start(bf16[4096,128]{1,0:T(8,128)(2,1)} %param.21) | copy-start | bytes 3145732
  0.6 33.2 %copy-start.3 = (f32[4096]{0:T(1024)S(1)}, f32[4096]{0:T(1024)}, u32[]{:S(2)}) copy-start(f32[4096]{0:T(1024)} %param.18) | copy-start | bytes 49156
  33.9 5.6 %copy-start.1 = (bf16[1,1024,128]{2,1,0:T(8,128)(2,1)S(1)}, bf16[1,1024,128]{2,1,0:T(8,128)(2,1)}, u32[]{:S(2)}) copy-start(bf16[1,1024,128]{2,1,0:T(8,128)(2,1)} %param.16) | copy-start | bytes 786436
  33.9 5.9 %copy-start.2 = (bf16[1,1024,128]{2,1,0:T(8,128)(2,1)S(1)}, bf16[1,1024,128]{2,1,0:T(8,128)(2,1)}, u32[]{:S(2)}) copy-start(bf16[1,1024,128]{2,1,0:T(8,128)(2,1)} %param.17) | copy-start | bytes 786436

commit v11 on v10

--- a/solution.py
+++ b/solution.py
@@ -79,7 +79,7 @@
         out_ref[b, rows:] = split(m_row, l_row)
 
     def body(b, carry):
-        flag = flags_ref[b]
+        flag = flags_ref[b % 2, b // 2]
 
         @pl.when(flag == 1)
         def _():
@@ -105,10 +105,11 @@
     )(flags, q_blocks, keys, values, lim)
 
 
-def mp_gather_kernel(n, x_ref, y_ref, send_sem, recv_sem, local_sem):
+def mp_gather_kernel(n, span, p_ref, r_ref, owner_ref, slot_ref, plen_ref, count_ref, index_ref,
+                     y_ref, meta_ref, send_sem, recv_sem, local_sem):
     me = lax.axis_index("mp")
     row = lax.axis_index("seq")
-    width = x_ref.shape[1]
+    rows, width = p_ref.shape
     barrier = pltpu.get_barrier_semaphore()
     for k in range(1, n):
         peer = lax.rem(me + k, n)
@@ -118,37 +119,79 @@
     copies = []
     for k in range(1, n):
         peer = lax.rem(me + k, n)
-        c = pltpu.make_async_remote_copy(
-            src_ref=x_ref,
-            dst_ref=y_ref.at[:, cols],
-            send_sem=send_sem.at[k],
-            recv_sem=recv_sem.at[k],
-            device_id=(row, peer),
-            device_id_type=MESH,
-        )
+        for part, src in enumerate((p_ref, r_ref)):
+            c = pltpu.make_async_remote_copy(
+                src_ref=src,
+                dst_ref=y_ref.at[pl.ds(part * rows, rows), cols],
+                send_sem=send_sem.at[part, k],
+                recv_sem=recv_sem.at[part, k],
+                device_id=(row, peer),
+                device_id_type=MESH,
+            )
+            c.start()
+            copies.append(c)
+    own = [
+        pltpu.make_async_copy(src, y_ref.at[pl.ds(part * rows, rows), cols], local_sem.at[part])
+        for part, src in enumerate((p_ref, r_ref))
+    ]
+    for c in own:
         c.start()
-        copies.append(c)
-    own = pltpu.make_async_copy(x_ref, y_ref.at[:, cols], local_sem)
-    own.start()
+
+    f32 = jnp.float32
+    owner = owner_ref[...].astype(f32)
+    slot = slot_ref[...].astype(f32)
+    lane = lax.broadcasted_iota(jnp.int32, owner.shape, 1)
+    mine = lane == row
+
+    def pick(v):
+        return jnp.sum(jnp.where(mine, v, 0.0), axis=1, keepdims=True)
+
+    own_owner = pick(owner)
+    own_slot = pick(slot)
+    rank = jnp.sum(jnp.where((owner == own_owner) & (lane < row), 1.0, 0.0), axis=1, keepdims=True)
+    held = jnp.sum(jnp.where(owner == own_slot, 1.0, 0.0), axis=1, keepdims=True)
+    length = pick(plen_ref[...].astype(f32))
+    count = pick(count_ref[...].astype(f32))
+    index = index_ref[pl.ds(row, 1), :].astype(f32)
+    lanef = lane.astype(f32)
+    quantities = [
+        held * span + lanef,
+        rank * span + index,
+        jnp.where(lanef < length, 1.0, 0.0),
+        jnp.where(lanef < count, 1.0, 0.0),
+        jnp.where(slot == own_owner, 1.0, 0.0),
+        jnp.where(mine, 2.0, jnp.where((owner == own_owner) & (lane > row), 1.0, 0.0)),
+        index,
+        rank * span + 0.0 * lanef,
+    ]
+    for q, value in enumerate(quantities):
+        meta_ref[q : q + 1, :] = value.astype(jnp.int32)
+
     for c in copies:
         c.wait()
-    own.wait()
-
-
-def mp_gather(x, n):
+    for c in own:
+        c.wait()
+
+
+def mp_gather(prompt_part, recompute_part, owner, slot, plen, count, index, n, span):
     vmem = pl.BlockSpec(memory_space=pltpu.VMEM)
+    rows, width = prompt_part.shape
+    small = [v.reshape(1, -1) for v in (owner, slot, plen, count)]
     return pl.pallas_call(
-        functools.partial(mp_gather_kernel, n),
-        in_specs=[vmem],
-        out_specs=vmem,
-        out_shape=jax.ShapeDtypeStruct((x.shape[0], x.shape[1] * n), x.dtype),
+        functools.partial(mp_gather_kernel, n, span),
+        in_specs=[vmem] * 7,
+        out_specs=[vmem, vmem],
+        out_shape=[
+            jax.ShapeDtypeStruct((2 * rows, width * n), prompt_part.dtype),
+            jax.ShapeDtypeStruct((8, owner.shape[0]), jnp.int32),
+        ],
         scratch_shapes=[
-            pltpu.SemaphoreType.DMA((n,)),
-            pltpu.SemaphoreType.DMA((n,)),
-            pltpu.SemaphoreType.DMA(()),
+            pltpu.SemaphoreType.DMA((2, n)),
+            pltpu.SemaphoreType.DMA((2, n)),
+            pltpu.SemaphoreType.DMA((2,)),
         ],
         compiler_params=pltpu.CompilerParams(collective_id=0, has_side_effects=True),
-    )(x)
+    )(prompt_part, recompute_part, *small, index)
 
 
 def mp_scatter_kernel(n, x_ref, y_ref, send_sem, recv_sem, local_sem):
@@ -507,34 +550,17 @@
     me = lax.axis_index("seq")
     scale = 1.0 / math.sqrt(HEAD_SIZE)
 
-    seq_ids = jnp.arange(n_seq, dtype=jnp.int32)
-    same_owner = passage_owner[:, None] == passage_owner[None, :]
-    passage_rank = jnp.sum(
-        jnp.where(same_owner & (seq_ids[None, :] < seq_ids[:, None]), 1, 0), axis=1
-    ).astype(jnp.int32)
-    held_count = jnp.sum(
-        jnp.where(passage_owner[None, :] == prompt_slot[:, None], 1, 0), axis=1
-    ).astype(jnp.int32)
-    own_rank = passage_rank[me]
-    own_owner = passage_owner[me]
-    own_held = held_count[me]
-    own_index = lax.dynamic_index_in_dim(recompute_index, me, 0, keepdims=False)
-    own_length = prompt_length[me]
-    own_count = recompute_count[me]
-
-    prompt_pos = own_held * passage_length + jnp.arange(prompt_rows, dtype=jnp.int32)
-    recompute_pos = own_rank * passage_length + own_index
-    own_pos = jnp.concatenate([prompt_pos, recompute_pos])
-    own_live = jnp.concatenate(
-        [
-            jnp.arange(prompt_rows, dtype=jnp.int32) < own_length,
-            jnp.arange(recompute_rows, dtype=jnp.int32) < own_count,
-        ]
-    )
-
-    rows_local = jnp.concatenate([prompt_hidden, recompute_hidden], axis=0)
-    n_mp = w_out.shape[1] // rows_local.shape[1]
-    full_rows = mp_gather(rows_local, n_mp)
+    n_mp = w_out.shape[1] // prompt_hidden.shape[1]
+    full_rows, meta = mp_gather(
+        prompt_hidden, recompute_hidden, passage_owner, prompt_slot, prompt_length,
+        recompute_count, recompute_index, n_mp, passage_length,
+    )
+    own_pos = jnp.concatenate([meta[0], meta[1]])
+    own_live = jnp.concatenate([meta[2], meta[3]]) > 0
+    own_index = meta[6]
+    own_shift = meta[7, 0]
+    prompt_live = meta[2] > 0
+    recompute_live = meta[3] > 0
     normalized_hidden = normalize(full_rows, norm_gain)
     queries = (
         apply_rotation(
@@ -559,7 +585,7 @@
         normalized_hidden, value_weight, preferred_element_type=jnp.float32
     ).astype(jnp.bfloat16)
 
-    position_shift = jnp.full((passage_length,), own_rank * passage_length, jnp.int32)
+    position_shift = jnp.full((passage_length,), own_shift, jnp.int32)
     shifted_keys = (
         apply_rotation(
             key_cache[0].astype(jnp.float32).reshape(passage_length, 1, HEAD_SIZE),
@@ -569,7 +595,7 @@
         .reshape(passage_length, HEAD_SIZE)
     )
     chosen = (own_index[:, None] == jnp.arange(passage_length, dtype=jnp.int32)[None, :]) & (
-        jnp.arange(recompute_rows, dtype=jnp.int32)[:, None] < own_count
+        recompute_live[:, None]
     )
     replaced = jnp.any(chosen, axis=0)[:, None]
     fresh_pair = jnp.concatenate([fresh_keys[prompt_rows:], fresh_values[prompt_rows:]], axis=1)
@@ -587,13 +613,8 @@
         queries.reshape(2, prompt_rows * local_heads, HEAD_SIZE), nx, nz
     )
     q_blocks = all_queries.reshape(n_seq * 2, prompt_rows * local_heads, HEAD_SIZE)
-    prompt_flag = jnp.where(prompt_slot == own_owner, 1, 0)
-    recompute_flag = jnp.where(
-        seq_ids == me, 2, jnp.where((passage_owner == own_owner) & (seq_ids > me), 1, 0)
-    )
-    flags = jnp.stack([prompt_flag, recompute_flag], axis=1).reshape(-1).astype(jnp.int32)
     lim = jnp.repeat(own_index, local_heads).reshape(-1, 1).astype(jnp.int32)
-    packed = passage_attention(nx, nz, flags, q_blocks, passage_keys, passage_values, lim)
+    packed = passage_attention(nx, nz, meta[4:6], q_blocks, passage_keys, passage_values, lim)
     block_rows = packed.shape[1]
 
     back = relay_reduce(packed.reshape(n_seq, 2, block_rows, HEAD_SIZE), nx, nz)
@@ -611,7 +632,7 @@
     pv = fresh_values[:prompt_rows].astype(jnp.float32)
     ps = jnp.einsum("qhd,kd->qhk", pq, pk) * scale
     jj = jnp.arange(prompt_rows, dtype=jnp.int32)
-    pvis = (jj[None, :] <= jj[:, None]) & (jj[None, :] < own_length)
+    pvis = (jj[None, :] <= jj[:, None]) & prompt_live[None, :]
     ps = jnp.where(pvis[:, None, :], ps, NEGATIVE_FLOOR)
     pmax = jnp.max(ps, axis=-1)
     pw = jnp.where(pvis[:, None, :], jnp.exp(ps - pmax[..., None]), 0.0)

time: 138 us -> 130 us (0.942)
  other arithmetic: 13.1 us -> 9.86 us
  matrix products: 11.2 us -> 8.4 us
  local copies, waits for them, and re-layouts: 8.05 us -> 5.75 us
    dynamic_slice x5 -> x0, local copies, waits for them, and re-layouts: 5.06 us -> none  [the longest x1 1.33 us: local(): own_owner = passage_owner[me]]
    slice x0 -> x2, local copies, waits for them, and re-layouts: none -> 2.59 us  [the longest x1 1.35 us: local(): own_shift = meta[7, 0]]
    dot_general x1, matrix products: 3.29 us -> 0.89 us  [local(): jnp.dot(normalized_hidden, w_query, preferred_element_type=jnp.float32)]
    concatenate x2 -> x0, other arithmetic: 1.48 us -> none  [the longest x1 1.4 us: local(): rows_local = jnp.concatenate([prompt_hidden, recompute_hidden], axis=0)]
where the time goes in v11:
time: 130 us
  Pallas kernels  104 us (80%)
  other arithmetic  9.86 us (8%)
  matrix products  8.4 us (6%)
  local copies, waits for them, and re-layouts  5.75 us (4%)
  between operations  1.62 us (1%)
    pallas_call x1, Pallas kernels, relay_gather(): pl.pallas_call(functools.partial(relay_gather_kernel, nx, nz), in_specs=[...  33.3 us
    pallas_call x1, Pallas kernels, relay_reduce(): pl.pallas_call(functools.partial(relay_reduce_kernel, nx, nz), in_specs=[...  31.6 us
    pallas_call x1, Pallas kernels, mp_scatter(): pl.pallas_call(functools.partial(mp_scatter_kernel, n), in_specs=[vmem],...  17.6 us
    pallas_call x1, Pallas kernels, mp_gather(): pl.pallas_call(functools.partial(mp_gather_kernel, n, span), in_specs=[vm...  14.8 us
    pallas_call x1, Pallas kernels, passage_attention(): pl.pallas_call(functools.partial(passage_kernel, nx, nz), in_specs=[pl.Bl...  6.69 us
    dot_general x1, matrix products, local(): projected = jnp.dot(attention, w_out, preferred_element_type=jnp.float32)  3.86 us

profile of v11, /device:TPU:1, one launch (start us, length us, event | category | flops | bytes accessed | tf_op | source)
XLA Modules:
  0.0 129.6 jit_solution(13887032727387860359)
XLA Ops:
  0.6 0.0 copy-start
  0.6 0.0 copy-start.5
  0.7 0.0 copy-start.3
  0.7 1.1 bitcast_convert_fusion
  1.8 14.8 %shard_map.149 = (bf16[64,4096]{1,0:T(8,128)(2,1)}, s32[8,32]{1,0:T(8,128)}) custom-call(bf16[32,512]{1,0:T(8,128)(2,1)} %p_ref.1, bf16[32,512]{1,0:T(8,128)(2,1)} %r_ref.1, s32[1,32]{1,0:T(1,128)} %bitcast.69, s32[1,32]{1,0:T(1,128)} %bitcast.70, s32[1,32]{1,0:T(1,128)} %bitcast.71, s32[1,32]{1,0:T(1,128)} %bitcast.72, s32[32,32]{1,0:T(8,128)} %index_ref.1), custom_call_target="tpu_custom_call" | custom-call | tf_op jit(solution)/shard_map/pallas_call | solution.py:180
  16.6 0.0 copy-start.1
  16.6 0.0 copy-start.2
  16.6 1.3 %slice.107 = s32[1,1]{1,0:T(1,128)} slice(s32[8,32]{1,0:T(8,128)} %get-tuple-element.4), slice={[7:8], [0:1]} | slice | bytes 8 | tf_op jit(solution)/shard_map/slice | solution.py:561
  18.7 0.7 broadcast_compare_fusion
  19.3 1.2 fusion.1
  20.6 0.7 compare_bitcast_fusion
  21.4 0.2 fusion.4
  21.6 1.2 slice.94.flags_ref
  22.8 0.9 slice_bitcast_fusion.6
  23.7 0.1 add_compare_fusion
  23.8 0.1 add_convert_fusion.2
  23.9 0.1 fusion.11
  24.0 0.1 fusion.36
  24.0 0.0 copy-done
  24.0 1.4 %convolution_convert_fusion.2 = bf16[64,128]{1,0:T(8,128)(2,1)S(1)} fusion(bf16[4096,128]{1,0:T(8,128)(2,1)S(1)} %copy-done, bf16[64,4096]{1,0:T(8,128)(2,1)} %get-tuple-element.5, f32[4096]{0:T(1024)} %param.18, f32[64]{0:T(128)S(1)} %add_rsqrt_fusion), kind=kOutput, calls=%fused_computation.7 | convolution fusion | flops 68165632 | bytes 1605888 | tf_op jit(solution)/shard_map/dot_general | solution.py:584
  25.4 0.1 broadcast_in_dim.44
  25.5 0.0 copy-done.5
  25.5 0.0 copy-done.3
  25.5 1.4 %convolution_bitcast_fusion = f32[64,1,128]{2,0,1:T(8,128)S(1)} fusion(bf16[4096,128]{1,0:T(8,128)(2,1)S(1)} %copy-done.3, bf16[64,4096]{1,0:T(8,128)(2,1)} %get-tuple-element.5, f32[4096]{0:T(1024)S(1)} %copy-done.5, f32[64]{0:T(128)S(1)} %add_rsqrt_fusion), kind=kOutput, calls=%fused_computation.6 | convolution fusion | flops 68157440 | bytes 1622272 | tf_op jit(solution)/shard_map/dot_general | solution.py:576
  26.9 0.0 copy-done.1
  26.9 0.0 copy-done.2
  26.9 0.0 copy-start.4
  26.9 0.9 fusion.49
  27.9 0.2 fusion.26
  28.1 0.1 fusion.38
  28.2 0.7 reshape_reshape.4.lim_ref
  28.9 0.2 multiply_cosine_fusion.1
  29.1 0.1 fusion.52
  29.3 0.3 fusion.54
  29.5 0.1 copy.47
  29.6 0.1 copy.48
  29.6 0.7 pad_maximum_fusion.x_ref
  30.4 0.2 fusion.27
  30.6 0.4 convolution_convert_fusion.1
  31.0 0.0 copy-done.4
  31.0 1.1 slice_select_fusion
  32.2 33.3 %shard_map.150 = bf16[32,2,128,128]{3,2,1,0:T(8,128)(2,1)} custom-call(bf16[2,128,128]{2,1,0:T(8,128)(2,1)} %pad_maximum_fusion.x_ref), custom_call_target="tpu_custom_call" | custom-call | tf_op jit(solution)/shard_map/pallas_call | solution.py:380
  65.5 6.7 %shard_map.151 = bf16[64,144,128]{2,1,0:T(8,128)(2,1)} custom-call(s32[2,32]{1,0:T(2,128)} %slice.94.flags_ref, bf16[64,128,128]{2,1,0:T(8,128)(2,1)} %bitcast.62, bf16[1024,128]{1,0:T(8,128)(2,1)} %get-tuple-element.11.k_ref, bf16[1024,128]{1,0:T(8,128)(2,1)} %get-tuple-element.10.v_ref, s32[128,1]{1,0:T(8,128)} %reshape_reshape.4.lim_ref), custom_call_target="tpu_custom_call" | custom-call | tf_op jit(solution)/shard_map/pallas_call | solution.py:100
  72.1 31.6 %shard_map.152 = bf16[4,2,144,128]{3,2,1,0:T(8,128)(2,1)} custom-call(bf16[32,2,144,128]{3,2,1,0:T(8,128)(2,1)} %bitcast.61), custom_call_target="tpu_custom_call" | custom-call | tf_op jit(solution)/shard_map/pallas_call | solution.py:506
  103.8 0.7 slice_convert_fusion
  104.5 0.1 reduce_max.21
  104.6 0.1 copy.50
  104.7 0.1 copy.51
  104.8 0.1 sub.42
  105.0 1.2 multiply_reduce_fusion
  106.2 0.1 reduce_sum.56
  106.3 0.1 copy.54
  106.4 3.9 %convolution_convert_fusion.x_ref = bf16[64,4096]{1,0:T(8,128)(2,1)} fusion(bf16[512,4096]{1,0:T(8,128)(2,1)} %param.22, f32[64,4]{0,1:T(4,128)S(1)} %get-tuple-element.6, f32[64,4]{0,1:T(4,128)S(1)} %get-tuple-element.7, f32[32,4,128]{2,0,1:T(8,128)S(1)} %fusion.27, f32[64,4,128]{2,1,0:T(4,128)S(1)} %bitcast.63, pred[64]{0:T(512)(128)(4,1)S(1)} %add_compare_fusion), kind=kOutput, calls=%fused_computation | convolution fusion | flops 268861440 | bytes 4917312 | tf_op jit(solution)/shard_map/dot_general | solution.py:658
  110.2 17.6 %shard_map.153 = bf16[8,64,512]{2,1,0:T(8,128)(2,1)} custom-call(bf16[64,4096]{1,0:T(8,128)(2,1)} %convolution_convert_fusion.x_ref), custom_call_target="tpu_custom_call" | custom-call | tf_op jit(solution)/shard_map/pallas_call | solution.py:230
  127.9 1.1 reduce_sum.58
  129.0 0.6 fusion.53
  (13 shorter events, 0.3 us)
Async XLA Ops:
  0.6 23.4 %copy-start = (bf16[4096,128]{1,0:T(8,128)(2,1)S(1)}, bf16[4096,128]{1,0:T(8,128)(2,1)}, u32[]{:S(2)}) copy-start(bf16[4096,128]{1,0:T(8,128)(2,1)} %param.21) | copy-start | bytes 3145732
  0.6 24.9 %copy-start.5 = (f32[4096]{0:T(1024)S(1)}, f32[4096]{0:T(1024)}, u32[]{:S(2)}) copy-start(f32[4096]{0:T(1024)} %param.18) | copy-start | bytes 49156
  0.7 24.9 %copy-start.3 = (bf16[4096,128]{1,0:T(8,128)(2,1)S(1)}, bf16[4096,128]{1,0:T(8,128)(2,1)}, u32[]{:S(2)}) copy-start(bf16[4096,128]{1,0:T(8,128)(2,1)} %param.20) | copy-start | bytes 3145732
  16.6 10.3 %copy-start.1 = (bf16[64,4096]{1,0:T(8,128)(2,1)S(1)}, bf16[64,4096]{1,0:T(8,128)(2,1)}, u32[]{:S(2)}) copy-start(bf16[64,4096]{1,0:T(8,128)(2,1)} %get-tuple-element.5) | copy-start | bytes 1572868
  16.6 10.3 %copy-start.2 = (bf16[4096,512]{1,0:T(8,128)(2,1)S(1)}, bf16[4096,512]{1,0:T(8,128)(2,1)}, u32[]{:S(2)}) copy-start(bf16[4096,512]{1,0:T(8,128)(2,1)} %param.19) | copy-start | bytes 12582916
  26.9 4.1 %copy-start.4 = (bf16[1,1024,128]{2,1,0:T(8,128)(2,1)S(1)}, bf16[1,1024,128]{2,1,0:T(8,128)(2,1)}, u32[]{:S(2)}) copy-start(bf16[1,1024,128]{2,1,0:T(8,128)(2,1)} %param.17) | copy-start | bytes 786436

commit v12 on v11

--- a/solution.py
+++ b/solution.py
@@ -79,7 +79,7 @@
         out_ref[b, rows:] = split(m_row, l_row)
 
     def body(b, carry):
-        flag = flags_ref[b % 2, b // 2]
+        flag = flags_ref[4 + b % 2, b // 2]
 
         @pl.when(flag == 1)
         def _():
@@ -106,7 +106,7 @@
 
 
 def mp_gather_kernel(n, span, p_ref, r_ref, owner_ref, slot_ref, plen_ref, count_ref, index_ref,
-                     y_ref, meta_ref, send_sem, recv_sem, local_sem):
+                     y_ref, meta_ref, lim_ref, send_sem, recv_sem, local_sem):
     me = lax.axis_index("mp")
     row = lax.axis_index("seq")
     rows, width = p_ref.shape
@@ -166,6 +166,11 @@
     ]
     for q, value in enumerate(quantities):
         meta_ref[q : q + 1, :] = value.astype(jnp.int32)
+    heads = lim_ref.shape[0] // index.shape[1]
+    wide = jnp.broadcast_to(index, (lim_ref.shape[0], index.shape[1]))
+    which = lax.broadcasted_iota(jnp.int32, wide.shape, 0) // heads
+    pick_lane = lax.broadcasted_iota(jnp.int32, wide.shape, 1)
+    lim_ref[...] = jnp.sum(jnp.where(which == pick_lane, wide, 0.0), axis=1, keepdims=True).astype(jnp.int32)
 
     for c in copies:
         c.wait()
@@ -173,17 +178,18 @@
         c.wait()
 
 
-def mp_gather(prompt_part, recompute_part, owner, slot, plen, count, index, n, span):
+def mp_gather(prompt_part, recompute_part, owner, slot, plen, count, index, n, span, heads):
     vmem = pl.BlockSpec(memory_space=pltpu.VMEM)
     rows, width = prompt_part.shape
     small = [v.reshape(1, -1) for v in (owner, slot, plen, count)]
     return pl.pallas_call(
         functools.partial(mp_gather_kernel, n, span),
         in_specs=[vmem] * 7,
-        out_specs=[vmem, vmem],
+        out_specs=[vmem, vmem, vmem],
         out_shape=[
             jax.ShapeDtypeStruct((2 * rows, width * n), prompt_part.dtype),
             jax.ShapeDtypeStruct((8, owner.shape[0]), jnp.int32),
+            jax.ShapeDtypeStruct((index.shape[1] * heads, 1), jnp.int32),
         ],
         scratch_shapes=[
             pltpu.SemaphoreType.DMA((2, n)),
@@ -551,9 +557,9 @@
     scale = 1.0 / math.sqrt(HEAD_SIZE)
 
     n_mp = w_out.shape[1] // prompt_hidden.shape[1]
-    full_rows, meta = mp_gather(
+    full_rows, meta, lim = mp_gather(
         prompt_hidden, recompute_hidden, passage_owner, prompt_slot, prompt_length,
-        recompute_count, recompute_index, n_mp, passage_length,
+        recompute_count, recompute_index, n_mp, passage_length, local_heads,
     )
     own_pos = jnp.concatenate([meta[0], meta[1]])
     own_live = jnp.concatenate([meta[2], meta[3]]) > 0
@@ -613,8 +619,7 @@
         queries.reshape(2, prompt_rows * local_heads, HEAD_SIZE), nx, nz
     )
     q_blocks = all_queries.reshape(n_seq * 2, prompt_rows * local_heads, HEAD_SIZE)
-    lim = jnp.repeat(own_index, local_heads).reshape(-1, 1).astype(jnp.int32)
-    packed = passage_attention(nx, nz, meta[4:6], q_blocks, passage_keys, passage_values, lim)
+    packed = passage_attention(nx, nz, meta, q_blocks, passage_keys, passage_values, lim)
     block_rows = packed.shape[1]
 
     back = relay_reduce(packed.reshape(n_seq, 2, block_rows, HEAD_SIZE), nx, nz)

time: 130 us -> 132 us (1.015)
  Pallas kernels: 104 us -> 107 us
  local copies, waits for them, and re-layouts: 5.75 us -> 3.73 us
    pallas_call x1, Pallas kernels: 6.69 us -> 12.4 us  [passage_attention(): pl.pallas_call(functools.partial(passage_kernel, nx, nz), in_specs=[pl.Bl...]
    pallas_call x1, Pallas kernels: 31.6 us -> 29.3 us  [relay_reduce(): pl.pallas_call(functools.partial(relay_reduce_kernel, nx, nz), in_specs=[...]
where the time goes in v12:
time: 132 us; the launch traced here: 131 us
  Pallas kernels  107 us (81%)
  other arithmetic  9.86 us (7%)
  matrix products  8.39 us (6%)
  local copies, waits for them, and re-layouts  3.73 us (3%)
  between operations  1.64 us (1%)
    pallas_call x1, Pallas kernels, relay_gather(): pl.pallas_call(functools.partial(relay_gather_kernel, nx, nz), in_specs=[...  33.3 us
    pallas_call x1, Pallas kernels, relay_reduce(): pl.pallas_call(functools.partial(relay_reduce_kernel, nx, nz), in_specs=[...  29.3 us
    pallas_call x1, Pallas kernels, mp_scatter(): pl.pallas_call(functools.partial(mp_scatter_kernel, n), in_specs=[vmem],...  17.4 us
    pallas_call x1, Pallas kernels, mp_gather(): pl.pallas_call(functools.partial(mp_gather_kernel, n, span), in_specs=[vm...  14.8 us
    pallas_call x1, Pallas kernels, passage_attention(): pl.pallas_call(functools.partial(passage_kernel, nx, nz), in_specs=[pl.Bl...  12.4 us
    dot_general x1, matrix products, local(): projected = jnp.dot(attention, w_out, preferred_element_type=jnp.float32)  3.86 us

profile of v12, /device:TPU:1, one launch (start us, length us, event | category | flops | bytes accessed | tf_op | source)
XLA Modules:
  0.0 130.8 jit_solution(973153860055492764)
XLA Ops:
  0.6 0.0 copy-start
  0.6 0.0 copy-start.5
  0.7 0.0 copy-start.3
  0.7 1.1 bitcast_convert_fusion
  1.8 14.8 %shard_map.149 = (bf16[64,4096]{1,0:T(8,128)(2,1)}, s32[8,32]{1,0:T(8,128)}, s32[128,1]{1,0:T(8,128)}) custom-call(bf16[32,512]{1,0:T(8,128)(2,1)} %p_ref.1, bf16[32,512]{1,0:T(8,128)(2,1)} %r_ref.1, s32[1,32]{1,0:T(1,128)} %bitcast.69, s32[1,32]{1,0:T(1,128)} %bitcast.70, s32[1,32]{1,0:T(1,128)} %bitcast.71, s32[1,32]{1,0:T(1,128)} %bitcast.72, ...), custom_call_target="tpu_custom_call" | custom-call | tf_op jit(solution)/shard_map/pallas_call | solution.py:185
  16.6 0.0 copy-start.1
  16.6 0.0 copy-start.2
  16.6 1.3 %slice.103 = s32[1,1]{1,0:T(1,128)} slice(s32[8,32]{1,0:T(8,128)} %get-tuple-element.5.flags_ref), slice={[7:8], [0:1]} | slice | bytes 8 | tf_op jit(solution)/shard_map/slice | solution.py:567
  18.7 0.7 broadcast_compare_fusion
  19.4 1.2 fusion.1
  20.6 0.7 compare_bitcast_fusion
  21.4 0.2 fusion.4
  21.6 0.9 slice_bitcast_fusion.6
  22.5 0.1 add_compare_fusion
  22.6 0.1 add_convert_fusion.2
  22.6 0.1 fusion.11
  22.7 0.1 fusion.36
  22.8 0.0 copy-done
  22.8 1.4 %convolution_convert_fusion.2 = bf16[64,128]{1,0:T(8,128)(2,1)S(1)} fusion(bf16[4096,128]{1,0:T(8,128)(2,1)S(1)} %copy-done, bf16[64,4096]{1,0:T(8,128)(2,1)} %get-tuple-element.6, f32[4096]{0:T(1024)} %param.18, f32[64]{0:T(128)S(1)} %add_rsqrt_fusion), kind=kOutput, calls=%fused_computation.7 | convolution fusion | flops 68165632 | bytes 1605888 | tf_op jit(solution)/shard_map/dot_general | solution.py:590
  24.2 0.0 copy-done.5
  24.2 0.0 copy-done.3
  24.3 1.4 %convolution_bitcast_fusion = f32[64,1,128]{2,0,1:T(8,128)S(1)} fusion(bf16[4096,128]{1,0:T(8,128)(2,1)S(1)} %copy-done.3, bf16[64,4096]{1,0:T(8,128)(2,1)} %get-tuple-element.6, f32[4096]{0:T(1024)S(1)} %copy-done.5, f32[64]{0:T(128)S(1)} %add_rsqrt_fusion), kind=kOutput, calls=%fused_computation.6 | convolution fusion | flops 68157440 | bytes 1622272 | tf_op jit(solution)/shard_map/dot_general | solution.py:582
  25.6 0.0 copy-done.1
  25.7 0.0 copy-done.2
  25.7 0.0 copy-start.4
  25.7 0.9 fusion.49
  26.6 0.2 fusion.26
  26.8 0.1 fusion.38
  26.9 0.2 multiply_cosine_fusion.1
  27.1 0.1 fusion.52
  27.3 0.3 fusion.54
  27.6 0.1 copy.44
  27.6 0.1 copy.45
  27.7 0.7 pad_maximum_fusion.x_ref
  28.4 0.2 fusion.27
  28.6 0.4 convolution_convert_fusion.1
  29.0 0.0 copy-done.4
  29.1 1.1 slice_select_fusion
  30.2 33.3 %shard_map.150 = bf16[32,2,128,128]{3,2,1,0:T(8,128)(2,1)} custom-call(bf16[2,128,128]{2,1,0:T(8,128)(2,1)} %pad_maximum_fusion.x_ref), custom_call_target="tpu_custom_call" | custom-call | tf_op jit(solution)/shard_map/pallas_call | solution.py:386
  63.5 12.4 %shard_map.151 = bf16[64,144,128]{2,1,0:T(8,128)(2,1)} custom-call(s32[8,32]{1,0:T(8,128)} %get-tuple-element.5.flags_ref, bf16[64,128,128]{2,1,0:T(8,128)(2,1)} %bitcast.62, bf16[1024,128]{1,0:T(8,128)(2,1)} %get-tuple-element.13.k_ref, bf16[1024,128]{1,0:T(8,128)(2,1)} %get-tuple-element.12.v_ref, s32[128,1]{1,0:T(8,128)} %get-tuple-element.7.lim_ref), custom_call_target="tpu_custom_call" | custom-call | tf_op jit(solution)/shard_map/pallas_call | solution.py:100
  75.9 29.3 %shard_map.152 = bf16[4,2,144,128]{3,2,1,0:T(8,128)(2,1)} custom-call(bf16[32,2,144,128]{3,2,1,0:T(8,128)(2,1)} %bitcast.61), custom_call_target="tpu_custom_call" | custom-call | tf_op jit(solution)/shard_map/pallas_call | solution.py:512
  105.2 0.7 slice_convert_fusion
  105.9 0.1 reduce_max.21
  106.0 0.1 copy.46
  106.1 0.1 copy.47
  106.2 0.1 sub.42
  106.4 1.2 multiply_reduce_fusion
  107.6 0.1 reduce_sum.56
  107.7 0.1 copy.50
  107.8 3.9 %convolution_convert_fusion.x_ref = bf16[64,4096]{1,0:T(8,128)(2,1)} fusion(bf16[512,4096]{1,0:T(8,128)(2,1)} %param.22, f32[64,4]{0,1:T(4,128)S(1)} %get-tuple-element.8, f32[64,4]{0,1:T(4,128)S(1)} %get-tuple-element.9, f32[32,4,128]{2,0,1:T(8,128)S(1)} %fusion.27, f32[64,4,128]{2,1,0:T(4,128)S(1)} %bitcast.63, pred[64]{0:T(512)(128)(4,1)S(1)} %add_compare_fusion), kind=kOutput, calls=%fused_computation | convolution fusion | flops 268861440 | bytes 4917312 | tf_op jit(solution)/shard_map/dot_general | solution.py:663
  111.6 17.4 %shard_map.153 = bf16[8,64,512]{2,1,0:T(8,128)(2,1)} custom-call(bf16[64,4096]{1,0:T(8,128)(2,1)} %convolution_convert_fusion.x_ref), custom_call_target="tpu_custom_call" | custom-call | tf_op jit(solution)/shard_map/pallas_call | solution.py:236
  129.1 1.1 reduce_sum.58
  130.2 0.6 fusion.53
  (13 shorter events, 0.3 us)
Async XLA Ops:
  0.6 22.2 %copy-start = (bf16[4096,128]{1,0:T(8,128)(2,1)S(1)}, bf16[4096,128]{1,0:T(8,128)(2,1)}, u32[]{:S(2)}) copy-start(bf16[4096,128]{1,0:T(8,128)(2,1)} %param.21) | copy-start | bytes 3145732
  0.6 23.6 %copy-start.5 = (f32[4096]{0:T(1024)S(1)}, f32[4096]{0:T(1024)}, u32[]{:S(2)}) copy-start(f32[4096]{0:T(1024)} %param.18) | copy-start | bytes 49156
  0.7 23.6 %copy-start.3 = (bf16[4096,128]{1,0:T(8,128)(2,1)S(1)}, bf16[4096,128]{1,0:T(8,128)(2,1)}, u32[]{:S(2)}) copy-start(bf16[4096,128]{1,0:T(8,128)(2,1)} %param.20) | copy-start | bytes 3145732
  16.6 9.0 %copy-start.1 = (bf16[64,4096]{1,0:T(8,128)(2,1)S(1)}, bf16[64,4096]{1,0:T(8,128)(2,1)}, u32[]{:S(2)}) copy-start(bf16[64,4096]{1,0:T(8,128)(2,1)} %get-tuple-element.6) | copy-start | bytes 1572868
  16.6 9.0 %copy-start.2 = (bf16[4096,512]{1,0:T(8,128)(2,1)S(1)}, bf16[4096,512]{1,0:T(8,128)(2,1)}, u32[]{:S(2)}) copy-start(bf16[4096,512]{1,0:T(8,128)(2,1)} %param.19) | copy-start | bytes 12582916
  25.7 3.4 %copy-start.4 = (bf16[1,1024,128]{2,1,0:T(8,128)(2,1)S(1)}, bf16[1,1024,128]{2,1,0:T(8,128)(2,1)}, u32[]{:S(2)}) copy-start(bf16[1,1024,128]{2,1,0:T(8,128)(2,1)} %param.17) | copy-start | bytes 786436

commit v13 on v12

--- a/solution.py
+++ b/solution.py
@@ -200,7 +200,7 @@
     )(prompt_part, recompute_part, *small, index)
 
 
-def mp_scatter_kernel(n, x_ref, y_ref, send_sem, recv_sem, local_sem):
+def mp_scatter_kernel(n, a_ref, w_ref, y_ref, buf, send_sem, recv_sem):
     me = lax.axis_index("mp")
     row = lax.axis_index("seq")
     width = y_ref.shape[2]
@@ -209,11 +209,19 @@
         peer = lax.rem(me + k, n)
         pl.semaphore_signal(barrier, inc=1, device_id=(row, peer), device_id_type=MESH)
     pl.semaphore_wait(barrier, n - 1)
+
+    def block(d):
+        cols = pl.ds(pl.multiple_of(d * width, width), width)
+        return jnp.dot(a_ref[...], w_ref[:, cols], preferred_element_type=jnp.float32).astype(
+            y_ref.dtype
+        )
+
     copies = []
     for k in range(1, n):
         peer = lax.rem(me + k, n)
+        buf[k] = block(peer)
         c = pltpu.make_async_remote_copy(
-            src_ref=x_ref.at[:, pl.ds(pl.multiple_of(peer * width, width), width)],
+            src_ref=buf.at[k],
             dst_ref=y_ref.at[me],
             send_sem=send_sem.at[k],
             recv_sem=recv_sem.at[k],
@@ -222,29 +230,27 @@
         )
         c.start()
         copies.append(c)
-    own = pltpu.make_async_copy(
-        x_ref.at[:, pl.ds(pl.multiple_of(me * width, width), width)], y_ref.at[me], local_sem
-    )
-    own.start()
+    y_ref[me] = block(me)
     for c in copies:
         c.wait()
-    own.wait()
-
-
-def mp_scatter(x, n):
+
+
+def mp_scatter(attention, w_out, n):
     vmem = pl.BlockSpec(memory_space=pltpu.VMEM)
+    rows = attention.shape[0]
+    width = w_out.shape[1] // n
     return pl.pallas_call(
         functools.partial(mp_scatter_kernel, n),
-        in_specs=[vmem],
+        in_specs=[vmem, vmem],
         out_specs=vmem,
-        out_shape=jax.ShapeDtypeStruct((n, x.shape[0], x.shape[1] // n), x.dtype),
+        out_shape=jax.ShapeDtypeStruct((n, rows, width), jnp.bfloat16),
         scratch_shapes=[
+            pltpu.VMEM((n, rows, width), jnp.bfloat16),
             pltpu.SemaphoreType.DMA((n,)),
             pltpu.SemaphoreType.DMA((n,)),
-            pltpu.SemaphoreType.DMA(()),
         ],
         compiler_params=pltpu.CompilerParams(collective_id=1, has_side_effects=True),
-    )(x)
+    )(attention, w_out)
 
 
 def relay_gather_kernel(nx, nz, x_ref, y_ref, *sems):
@@ -660,8 +666,7 @@
     attention = jnp.where(
         own_live[:, None, None], accumulated / safe_totals[..., None], 0.0
     ).astype(jnp.bfloat16).reshape(query_rows, local_heads * HEAD_SIZE)
-    projected = jnp.dot(attention, w_out, preferred_element_type=jnp.float32)
-    shares = mp_scatter(projected.astype(jnp.bfloat16), n_mp)
+    shares = mp_scatter(attention, w_out, n_mp)
     combined = jnp.sum(shares.astype(jnp.float32), axis=0).astype(jnp.bfloat16)
     return (combined[:prompt_rows], combined[prompt_rows:])
 

time: 132 us -> 128 us (0.970)
  matrix products: 8.39 us -> 4.53 us
    pallas_call x1, Pallas kernels: 12.4 us -> 6.17 us  [passage_attention(): pl.pallas_call(functools.partial(passage_kernel, nx, nz), in_specs=[pl.Bl...]
    pallas_call x1, Pallas kernels: 29.3 us -> 33.8 us  [relay_reduce(): pl.pallas_call(functools.partial(relay_reduce_kernel, nx, nz), in_specs=[...]
    dot_general x1 -> x0, matrix products: 3.86 us -> none  [local(): projected = jnp.dot(attention, w_out, preferred_element_type=jnp.float32)]
where the time goes in v13:
time: 128 us; the launch traced here: 127 us
  Pallas kernels  106 us (83%)
  other arithmetic  10.6 us (8%)
  matrix products  4.53 us (4%)
  local copies, waits for them, and re-layouts  3.73 us (3%)
  between operations  1.64 us (1%)
    pallas_call x1, Pallas kernels, relay_reduce(): pl.pallas_call(functools.partial(relay_reduce_kernel, nx, nz), in_specs=[...  33.8 us
    pallas_call x1, Pallas kernels, relay_gather(): pl.pallas_call(functools.partial(relay_gather_kernel, nx, nz), in_specs=[...  33.3 us
    pallas_call x1, Pallas kernels, mp_scatter(): pl.pallas_call(functools.partial(mp_scatter_kernel, n), in_specs=[vmem, v...  18.4 us
    pallas_call x1, Pallas kernels, mp_gather(): pl.pallas_call(functools.partial(mp_gather_kernel, n, span), in_specs=[vm...  14.8 us
    pallas_call x1, Pallas kernels, passage_attention(): pl.pallas_call(functools.partial(passage_kernel, nx, nz), in_specs=[pl.Bl...  6.17 us

profile of v13, /device:TPU:1, one launch (start us, length us, event | category | flops | bytes accessed | tf_op | source)
XLA Modules:
  0.0 126.9 jit_solution(14753870707644935289)
XLA Ops:
  0.6 0.0 copy-start
  0.6 0.0 copy-start.5
  0.7 0.0 copy-start.3
  0.7 1.1 bitcast_convert_fusion
  1.8 14.8 %shard_map.149 = (bf16[64,4096]{1,0:T(8,128)(2,1)}, s32[8,32]{1,0:T(8,128)}, s32[128,1]{1,0:T(8,128)}) custom-call(bf16[32,512]{1,0:T(8,128)(2,1)} %p_ref.1, bf16[32,512]{1,0:T(8,128)(2,1)} %r_ref.1, s32[1,32]{1,0:T(1,128)} %bitcast.66, s32[1,32]{1,0:T(1,128)} %bitcast.67, s32[1,32]{1,0:T(1,128)} %bitcast.68, s32[1,32]{1,0:T(1,128)} %bitcast.69, ...), custom_call_target="tpu_custom_call" | custom-call | tf_op jit(solution)/shard_map/pallas_call | solution.py:185
  16.6 0.0 copy-start.1
  16.6 0.0 copy-start.2
  16.6 1.3 %slice.103 = s32[1,1]{1,0:T(1,128)} slice(s32[8,32]{1,0:T(8,128)} %get-tuple-element.5.flags_ref), slice={[7:8], [0:1]} | slice | bytes 8 | tf_op jit(solution)/shard_map/slice | solution.py:573
  18.7 0.7 broadcast_compare_fusion
  19.4 1.2 fusion.1
  20.6 0.7 compare_bitcast_fusion
  21.4 0.2 fusion.4
  21.6 0.9 slice_bitcast_fusion.6
  22.5 0.1 add_compare_fusion
  22.6 0.1 add_convert_fusion.2
  22.6 0.1 fusion.11
  22.7 0.1 fusion.34
  22.8 0.0 copy-done
  22.8 1.4 %convolution_convert_fusion.1 = bf16[64,128]{1,0:T(8,128)(2,1)S(1)} fusion(bf16[4096,128]{1,0:T(8,128)(2,1)S(1)} %copy-done, bf16[64,4096]{1,0:T(8,128)(2,1)} %get-tuple-element.6, f32[4096]{0:T(1024)} %param.18, f32[64]{0:T(128)S(1)} %add_rsqrt_fusion), kind=kOutput, calls=%fused_computation.6 | convolution fusion | flops 68165632 | bytes 1605888 | tf_op jit(solution)/shard_map/dot_general | solution.py:596
  24.2 0.0 copy-done.5
  24.2 0.0 copy-done.3
  24.3 1.4 %convolution_bitcast_fusion = f32[64,1,128]{2,0,1:T(8,128)S(1)} fusion(bf16[4096,128]{1,0:T(8,128)(2,1)S(1)} %copy-done.3, bf16[64,4096]{1,0:T(8,128)(2,1)} %get-tuple-element.6, f32[4096]{0:T(1024)S(1)} %copy-done.5, f32[64]{0:T(128)S(1)} %add_rsqrt_fusion), kind=kOutput, calls=%fused_computation.5 | convolution fusion | flops 68157440 | bytes 1622272 | tf_op jit(solution)/shard_map/dot_general | solution.py:588
  25.6 0.0 copy-done.1
  25.7 0.0 copy-done.2
  25.7 0.0 copy-start.4
  25.7 0.9 fusion.47
  26.6 0.2 fusion.24
  26.8 0.1 fusion.36
  26.9 0.2 multiply_cosine_fusion.1
  27.1 0.1 fusion.50
  27.3 0.3 fusion.52
  27.6 0.1 copy.45
  27.6 0.1 copy.46
  27.7 0.7 pad_maximum_fusion.x_ref
  28.4 0.2 fusion.25
  28.6 0.4 convolution_convert_fusion
  29.0 0.0 copy-done.4
  29.1 1.1 slice_select_fusion
  30.2 33.3 %shard_map.150 = bf16[32,2,128,128]{3,2,1,0:T(8,128)(2,1)} custom-call(bf16[2,128,128]{2,1,0:T(8,128)(2,1)} %pad_maximum_fusion.x_ref), custom_call_target="tpu_custom_call" | custom-call | tf_op jit(solution)/shard_map/pallas_call | solution.py:392
  63.5 6.2 %shard_map.151 = bf16[64,144,128]{2,1,0:T(8,128)(2,1)} custom-call(s32[8,32]{1,0:T(8,128)} %get-tuple-element.5.flags_ref, bf16[64,128,128]{2,1,0:T(8,128)(2,1)} %bitcast.59, bf16[1024,128]{1,0:T(8,128)(2,1)} %get-tuple-element.13.k_ref, bf16[1024,128]{1,0:T(8,128)(2,1)} %get-tuple-element.12.v_ref, s32[128,1]{1,0:T(8,128)} %get-tuple-element.7.lim_ref), custom_call_target="tpu_custom_call" | custom-call | tf_op jit(solution)/shard_map/pallas_call | solution.py:100
  69.7 33.8 %shard_map.152 = bf16[4,2,144,128]{3,2,1,0:T(8,128)(2,1)} custom-call(bf16[32,2,144,128]{3,2,1,0:T(8,128)(2,1)} %bitcast.58), custom_call_target="tpu_custom_call" | custom-call | tf_op jit(solution)/shard_map/pallas_call | solution.py:518
  103.5 0.7 slice_convert_fusion
  104.2 0.1 reduce_max.21
  104.3 0.1 copy.47
  104.4 0.1 copy.48
  104.5 0.1 sub.42
  104.7 1.2 multiply_reduce_fusion
  105.8 0.1 reduce_sum.56
  106.0 0.1 copy.51
  106.0 0.8 copy_bitcast_fusion.a_ref
  106.8 18.4 %shard_map.153 = bf16[8,64,512]{2,1,0:T(8,128)(2,1)} custom-call(bf16[64,512]{1,0:T(8,128)(2,1)} %copy_bitcast_fusion.a_ref, bf16[512,4096]{1,0:T(8,128)(2,1)} %w_ref.1), custom_call_target="tpu_custom_call" | custom-call | tf_op jit(solution)/shard_map/pallas_call | solution.py:242
  125.2 1.1 reduce_sum.58
  126.3 0.6 fusion.51
  (13 shorter events, 0.3 us)
Async XLA Ops:
  0.6 22.2 %copy-start = (bf16[4096,128]{1,0:T(8,128)(2,1)S(1)}, bf16[4096,128]{1,0:T(8,128)(2,1)}, u32[]{:S(2)}) copy-start(bf16[4096,128]{1,0:T(8,128)(2,1)} %param.21) | copy-start | bytes 3145732
  0.6 23.6 %copy-start.5 = (f32[4096]{0:T(1024)S(1)}, f32[4096]{0:T(1024)}, u32[]{:S(2)}) copy-start(f32[4096]{0:T(1024)} %param.18) | copy-start | bytes 49156
  0.7 23.6 %copy-start.3 = (bf16[4096,128]{1,0:T(8,128)(2,1)S(1)}, bf16[4096,128]{1,0:T(8,128)(2,1)}, u32[]{:S(2)}) copy-start(bf16[4096,128]{1,0:T(8,128)(2,1)} %param.20) | copy-start | bytes 3145732
  16.6 9.0 %copy-start.1 = (bf16[64,4096]{1,0:T(8,128)(2,1)S(1)}, bf16[64,4096]{1,0:T(8,128)(2,1)}, u32[]{:S(2)}) copy-start(bf16[64,4096]{1,0:T(8,128)(2,1)} %get-tuple-element.6) | copy-start | bytes 1572868
  16.6 9.0 %copy-start.2 = (bf16[4096,512]{1,0:T(8,128)(2,1)S(1)}, bf16[4096,512]{1,0:T(8,128)(2,1)}, u32[]{:S(2)}) copy-start(bf16[4096,512]{1,0:T(8,128)(2,1)} %param.19) | copy-start | bytes 12582916
  25.7 3.4 %copy-start.4 = (bf16[1,1024,128]{2,1,0:T(8,128)(2,1)S(1)}, bf16[1,1024,128]{2,1,0:T(8,128)(2,1)}, u32[]{:S(2)}) copy-start(bf16[1,1024,128]{2,1,0:T(8,128)(2,1)} %param.17) | copy-start | bytes 786436

commit v14 on v13

--- a/solution.py
+++ b/solution.py
@@ -253,7 +253,8 @@
     )(attention, w_out)
 
 
-def relay_gather_kernel(nx, nz, x_ref, y_ref, *sems):
+def relay_gather_kernel(nx, nz, x_ref, kc_ref, vc_ref, fresh_ref, meta_ref, rot_ref,
+                        y_ref, pk_ref, pv_ref, *sems):
     (sx_send, sx_recv, zp_send, zp_recv, zm_send, zm_recv, own_sem,
      bp_send, bp_recv, bm_send, bm_recv, xp_send, xp_recv, xm_send, xm_recv,
      fp_send, fp_recv, fm_send, fm_recv) = sems
@@ -292,6 +293,19 @@
     ]
     own = pltpu.make_async_copy(x_ref, y_ref.at[slot], own_sem)
     own.start()
+
+    width = kc_ref.shape[1]
+    cached = kc_ref[...].astype(jnp.float32)
+    turned = pltpu.roll(cached, width // 2, 1)
+    shifted = (cached * rot_ref[0:1, :] + turned * rot_ref[1:2, :]).astype(pk_ref.dtype)
+    token = lax.broadcasted_iota(jnp.int32, (kc_ref.shape[0], meta_ref.shape[1]), 0)
+    chosen = (token == meta_ref[6:7, :]) & (meta_ref[3:4, :] > 0)
+    placed = jnp.dot(
+        chosen.astype(jnp.bfloat16), fresh_ref[...], preferred_element_type=jnp.float32
+    ).astype(pk_ref.dtype)
+    replaced = jnp.max(jnp.where(chosen, 1.0, 0.0), axis=1, keepdims=True) > 0.0
+    pk_ref[...] = jnp.where(replaced, placed[:, :width], shifted)
+    pv_ref[...] = jnp.where(replaced, placed[:, width:], vc_ref[...])
 
     def x_out(column):
         a = copy(
@@ -384,16 +398,20 @@
         c.wait_send()
 
 
-def relay_gather(x, nx, nz):
+def relay_gather(x, kc, vc, fresh, meta, rot, nx, nz):
     assert nx == 4 and nz % 2 == 0
     vmem = pl.BlockSpec(memory_space=pltpu.VMEM)
     steps = nz // 2
     dma = pltpu.SemaphoreType.DMA
     return pl.pallas_call(
         functools.partial(relay_gather_kernel, nx, nz),
-        in_specs=[vmem],
-        out_specs=vmem,
-        out_shape=jax.ShapeDtypeStruct((nx * nz,) + x.shape, x.dtype),
+        in_specs=[vmem] * 6,
+        out_specs=[vmem, vmem, vmem],
+        out_shape=[
+            jax.ShapeDtypeStruct((nx * nz,) + x.shape, x.dtype),
+            jax.ShapeDtypeStruct(kc.shape, kc.dtype),
+            jax.ShapeDtypeStruct(vc.shape, vc.dtype),
+        ],
         scratch_shapes=[
             dma((nx,)), dma((nx,)),
             dma((steps + 1, nx)), dma((steps + 1, nx)), dma((steps + 1, nx)), dma((steps + 1, nx)),
@@ -403,7 +421,7 @@
             dma((nz,)), dma((nz,)), dma((nz,)), dma((nz,)),
         ],
         compiler_params=pltpu.CompilerParams(collective_id=2, has_side_effects=True),
-    )(x)
+    )(x, kc, vc, fresh, meta, rot)
 
 
 def merge_piece(a, b, rows):
@@ -597,32 +615,28 @@
         normalized_hidden, value_weight, preferred_element_type=jnp.float32
     ).astype(jnp.bfloat16)
 
-    position_shift = jnp.full((passage_length,), own_shift, jnp.int32)
-    shifted_keys = (
-        apply_rotation(
-            key_cache[0].astype(jnp.float32).reshape(passage_length, 1, HEAD_SIZE),
-            position_shift,
-        )
-        .astype(jnp.bfloat16)
-        .reshape(passage_length, HEAD_SIZE)
-    )
-    chosen = (own_index[:, None] == jnp.arange(passage_length, dtype=jnp.int32)[None, :]) & (
-        recompute_live[:, None]
-    )
-    replaced = jnp.any(chosen, axis=0)[:, None]
+    half_width = HEAD_SIZE // 2
+    exponent = jnp.arange(half_width).astype(jnp.float32) * (2.0 / HEAD_SIZE)
+    frequency = jnp.exp(-exponent * math.log(500000.0))
+    angle = own_shift.astype(jnp.float32) * frequency
+    rot = jnp.stack(
+        [
+            jnp.concatenate([jnp.cos(angle), jnp.cos(angle)]),
+            jnp.concatenate([-jnp.sin(angle), jnp.sin(angle)]),
+        ]
+    )
     fresh_pair = jnp.concatenate([fresh_keys[prompt_rows:], fresh_values[prompt_rows:]], axis=1)
-    placed = lax.dot_general(
-        chosen.astype(jnp.bfloat16),
+
+    nx, nz = SEQ_SHAPE
+    all_queries, passage_keys, passage_values = relay_gather(
+        queries.reshape(2, prompt_rows * local_heads, HEAD_SIZE),
+        key_cache[0],
+        value_cache[0],
         fresh_pair,
-        (((0,), (0,)), ((), ())),
-        preferred_element_type=jnp.float32,
-    ).astype(jnp.bfloat16)
-    passage_keys = jnp.where(replaced, placed[:, :HEAD_SIZE], shifted_keys)
-    passage_values = jnp.where(replaced, placed[:, HEAD_SIZE:], value_cache[0])
-
-    nx, nz = SEQ_SHAPE
-    all_queries = relay_gather(
-        queries.reshape(2, prompt_rows * local_heads, HEAD_SIZE), nx, nz
+        meta,
+        rot,
+        nx,
+        nz,
     )
     q_blocks = all_queries.reshape(n_seq * 2, prompt_rows * local_heads, HEAD_SIZE)
     packed = passage_attention(nx, nz, meta, q_blocks, passage_keys, passage_values, lim)

time: 128 us -> 127 us (level)
  matrix products: 4.53 us -> 6.68 us
  other arithmetic: 10.6 us -> 8.76 us
    pallas_call x1, Pallas kernels: 33.8 us -> 30.1 us  [relay_reduce(): pl.pallas_call(functools.partial(relay_reduce_kernel, nx, nz), in_specs=[...]
    dot_general x1, matrix products: 0.89 us -> 3.1 us  [local(): jnp.dot(normalized_hidden, w_query, preferred_element_type=jnp.float32)]
where the time goes in v14:
time: 127 us; the launch traced here: 126 us
  Pallas kernels  106 us (83%)
  other arithmetic  8.76 us (7%)
  matrix products  6.68 us (5%)
  local copies, waits for them, and re-layouts  3.58 us (3%)
  between operations  1.5 us (1%)
    pallas_call x1, Pallas kernels, relay_gather(): pl.pallas_call(functools.partial(relay_gather_kernel, nx, nz), in_specs=[...  33.8 us
    pallas_call x1, Pallas kernels, relay_reduce(): pl.pallas_call(functools.partial(relay_reduce_kernel, nx, nz), in_specs=[...  30.1 us
    pallas_call x1, Pallas kernels, mp_scatter(): pl.pallas_call(functools.partial(mp_scatter_kernel, n), in_specs=[vmem, v...  19.6 us
    pallas_call x1, Pallas kernels, mp_gather(): pl.pallas_call(functools.partial(mp_gather_kernel, n, span), in_specs=[vm...  14.9 us
    pallas_call x1, Pallas kernels, passage_attention(): pl.pallas_call(functools.partial(passage_kernel, nx, nz), in_specs=[pl.Bl...  7.21 us
    dot_general x1, matrix products, local(): jnp.dot(normalized_hidden, w_query, preferred_element_type=jnp.float32)  3.1 us

profile of v14, /device:TPU:1, one launch (start us, length us, event | category | flops | bytes accessed | tf_op | source)
XLA Modules:
  0.0 126.0 jit_solution(8665695168248101894)
XLA Ops:
  0.6 0.0 copy-start
  0.7 14.9 %shard_map.149 = (bf16[64,4096]{1,0:T(8,128)(2,1)}, s32[8,32]{1,0:T(8,128)}, s32[128,1]{1,0:T(8,128)}) custom-call(bf16[32,512]{1,0:T(8,128)(2,1)} %p_ref.1, bf16[32,512]{1,0:T(8,128)(2,1)} %r_ref.1, s32[1,32]{1,0:T(1,128)} %bitcast.61, s32[1,32]{1,0:T(1,128)} %bitcast.62, s32[1,32]{1,0:T(1,128)} %bitcast.63, s32[1,32]{1,0:T(1,128)} %bitcast.64, ...), custom_call_target="tpu_custom_call" | custom-call | tf_op jit(solution)/shard_map/pallas_call | solution.py:185
  15.6 0.0 copy-start.1
  15.6 1.3 slice.84
  17.5 1.2 fusion.1
  18.7 0.1 fusion.34
  18.8 0.7 compare_bitcast_fusion
  19.5 0.1 maximum_bitcast_fusion.1
  19.6 0.1 maximum_bitcast_fusion
  19.7 0.6 pad_maximum_fusion.6.rot_ref
  20.3 0.8 slice_bitcast_fusion.5
  21.1 0.1 add_compare_fusion
  21.2 0.1 add_convert_fusion.1
  21.3 0.1 fusion.24
  21.3 0.0 copy-done
  21.3 1.4 %convolution_convert_fusion = bf16[64,128]{1,0:T(8,128)(2,1)S(1)} fusion(bf16[4096,128]{1,0:T(8,128)(2,1)S(1)} %copy-done, bf16[64,4096]{1,0:T(8,128)(2,1)} %get-tuple-element.9, f32[4096]{0:T(1024)} %param.18, f32[64]{0:T(128)S(1)} %add_rsqrt_fusion), kind=kOutput, calls=%fused_computation.5 | convolution fusion | flops 68165632 | bytes 1605888 | tf_op jit(solution)/shard_map/dot_general | solution.py:614
  22.7 1.7 %convolution_bitcast_fusion = f32[64,1,128]{2,0,1:T(8,128)S(1)} fusion(bf16[4096,128]{1,0:T(8,128)(2,1)} %param.20, bf16[64,4096]{1,0:T(8,128)(2,1)} %get-tuple-element.9, f32[4096]{0:T(1024)} %param.18, f32[64]{0:T(128)S(1)} %add_rsqrt_fusion), kind=kOutput, calls=%fused_computation.4 | convolution fusion | flops 68157440 | bytes 1622272 | tf_op jit(solution)/shard_map/dot_general | solution.py:606
  24.5 0.0 copy-done.1
  24.5 3.1 %fusion.37 = f32[64,512]{1,0:T(8,128)S(1)} fusion(bf16[4096,512]{1,0:T(8,128)(2,1)} %param.19, bf16[64,4096]{1,0:T(8,128)(2,1)S(1)} %copy-done.1, f32[4096]{0:T(1024)} %param.18, f32[64]{0:T(128)S(1)} %add_rsqrt_fusion), kind=kOutput, calls=%fused_computation.77 | convolution fusion | flops 269484032 | bytes 4866304 | tf_op jit(solution)/shard_map/dot_general | solution.py:597
  27.7 0.2 fusion.17
  27.9 0.1 fusion.26
  27.9 0.6 pad_maximum_fusion.3.fresh_ref
  28.6 0.2 multiply_cosine_fusion.1
  28.8 0.1 fusion.40
  28.9 0.3 fusion.42
  29.2 0.1 copy.35
  29.3 0.1 copy.36
  29.3 0.7 pad_maximum_fusion.x_ref
  30.1 0.2 fusion.18
  30.3 33.8 %shard_map.150 = (bf16[32,2,128,128]{3,2,1,0:T(8,128)(2,1)}, bf16[1024,128]{1,0:T(8,128)(2,1)}, bf16[1024,128]{1,0:T(8,128)(2,1)}) custom-call(bf16[2,128,128]{2,1,0:T(8,128)(2,1)} %pad_maximum_fusion.x_ref, bf16[1024,128]{1,0:T(8,128)(2,1)} %bitcast.54, bf16[1024,128]{1,0:T(8,128)(2,1)} %bitcast.55, bf16[32,256]{1,0:T(8,128)(2,1)} %pad_maximum_fusion.3.fresh_ref, ...), custom_call_target="tpu_custom_call" | custom-call | tf_op jit(solution)/shard_map/pallas_call | solution.py:406
  64.0 7.2 %shard_map.151 = bf16[64,144,128]{2,1,0:T(8,128)(2,1)} custom-call(s32[8,32]{1,0:T(8,128)} %get-tuple-element.8.meta_ref.flags_ref, bf16[64,128,128]{2,1,0:T(8,128)(2,1)} %bitcast.52, bf16[1024,128]{1,0:T(8,128)(2,1)} %get-tuple-element.11.k_ref, bf16[1024,128]{1,0:T(8,128)(2,1)} %get-tuple-element.12.v_ref, s32[128,1]{1,0:T(8,128)} %get-tuple-element.13.lim_ref), custom_call_target="tpu_custom_call" | custom-call | tf_op jit(solution)/shard_map/pallas_call | solution.py:100
  71.2 30.1 %shard_map.152 = bf16[4,2,144,128]{3,2,1,0:T(8,128)(2,1)} custom-call(bf16[32,2,144,128]{3,2,1,0:T(8,128)(2,1)} %bitcast.51), custom_call_target="tpu_custom_call" | custom-call | tf_op jit(solution)/shard_map/pallas_call | solution.py:536
  101.3 0.7 slice_convert_fusion
  102.1 0.1 reduce_max.21
  102.2 0.1 copy.37
  102.3 0.1 copy.38
  102.4 0.1 sub.38
  102.5 1.2 multiply_reduce_fusion
  103.7 0.1 reduce_sum.56
  103.8 0.1 copy.41
  103.9 0.8 copy_bitcast_fusion.a_ref
  104.7 19.6 %shard_map.153 = bf16[8,64,512]{2,1,0:T(8,128)(2,1)} custom-call(bf16[64,512]{1,0:T(8,128)(2,1)} %copy_bitcast_fusion.a_ref, bf16[512,4096]{1,0:T(8,128)(2,1)} %w_ref.1), custom_call_target="tpu_custom_call" | custom-call | tf_op jit(solution)/shard_map/pallas_call | solution.py:242
  124.3 1.1 reduce_sum.58
  125.4 0.6 fusion.41
  (13 shorter events, 0.3 us)
Async XLA Ops:
  0.6 20.7 %copy-start = (bf16[4096,128]{1,0:T(8,128)(2,1)S(1)}, bf16[4096,128]{1,0:T(8,128)(2,1)}, u32[]{:S(2)}) copy-start(bf16[4096,128]{1,0:T(8,128)(2,1)} %param.21) | copy-start | bytes 3145732
  15.6 8.9 %copy-start.1 = (bf16[64,4096]{1,0:T(8,128)(2,1)S(1)}, bf16[64,4096]{1,0:T(8,128)(2,1)}, u32[]{:S(2)}) copy-start(bf16[64,4096]{1,0:T(8,128)(2,1)} %get-tuple-element.9) | copy-start | bytes 1572868

commit v15 on v14

--- a/solution.py
+++ b/solution.py
@@ -200,7 +200,7 @@
     )(prompt_part, recompute_part, *small, index)
 
 
-def mp_scatter_kernel(n, a_ref, w_ref, y_ref, buf, send_sem, recv_sem):
+def mp_scatter_kernel(n, a_ref, w_ref, p_ref, r_ref, y_ref, buf, send_sem, recv_sem):
     me = lax.axis_index("mp")
     row = lax.axis_index("seq")
     width = y_ref.shape[2]
@@ -233,18 +233,28 @@
     y_ref[me] = block(me)
     for c in copies:
         c.wait()
-
-
-def mp_scatter(attention, w_out, n):
+    total = y_ref[0].astype(jnp.float32)
+    for k in range(1, n):
+        total = total + y_ref[k].astype(jnp.float32)
+    rows = p_ref.shape[0]
+    p_ref[...] = total[:rows].astype(p_ref.dtype)
+    r_ref[...] = total[rows:].astype(r_ref.dtype)
+
+
+def mp_scatter(attention, w_out, n, split):
     vmem = pl.BlockSpec(memory_space=pltpu.VMEM)
     rows = attention.shape[0]
     width = w_out.shape[1] // n
     return pl.pallas_call(
         functools.partial(mp_scatter_kernel, n),
         in_specs=[vmem, vmem],
-        out_specs=vmem,
-        out_shape=jax.ShapeDtypeStruct((n, rows, width), jnp.bfloat16),
+        out_specs=[vmem, vmem],
+        out_shape=[
+            jax.ShapeDtypeStruct((split, width), jnp.bfloat16),
+            jax.ShapeDtypeStruct((rows - split, width), jnp.bfloat16),
+        ],
         scratch_shapes=[
+            pltpu.VMEM((n, rows, width), jnp.bfloat16),
             pltpu.VMEM((n, rows, width), jnp.bfloat16),
             pltpu.SemaphoreType.DMA((n,)),
             pltpu.SemaphoreType.DMA((n,)),
@@ -680,9 +690,8 @@
     attention = jnp.where(
         own_live[:, None, None], accumulated / safe_totals[..., None], 0.0
     ).astype(jnp.bfloat16).reshape(query_rows, local_heads * HEAD_SIZE)
-    shares = mp_scatter(attention, w_out, n_mp)
-    combined = jnp.sum(shares.astype(jnp.float32), axis=0).astype(jnp.bfloat16)
-    return (combined[:prompt_rows], combined[prompt_rows:])
+    prompt_out, recompute_out = mp_scatter(attention, w_out, n_mp, prompt_rows)
+    return (prompt_out, recompute_out)
 
 
 def solution(mesh):

time: 127 us -> 128 us (level)
  local copies, waits for them, and re-layouts: 3.58 us -> 5.69 us
    unnamed x5 -> x7, local copies, waits for them, and re-layouts: 0.02 us -> 2.76 us
where the time goes in v15:
time: 128 us; the launch traced here: 127 us
  Pallas kernels  106 us (83%)
  other arithmetic  7.64 us (6%)
  matrix products  6.68 us (5%)
  local copies, waits for them, and re-layouts  5.69 us (4%)
  between operations  1.5 us (1%)
    pallas_call x1, Pallas kernels, relay_gather(): pl.pallas_call(functools.partial(relay_gather_kernel, nx, nz), in_specs=[...  33.8 us
    pallas_call x1, Pallas kernels, relay_reduce(): pl.pallas_call(functools.partial(relay_reduce_kernel, nx, nz), in_specs=[...  31.4 us
    pallas_call x1, Pallas kernels, mp_scatter(): pl.pallas_call(functools.partial(mp_scatter_kernel, n), in_specs=[vmem, v...  18.8 us
    pallas_call x1, Pallas kernels, mp_gather(): pl.pallas_call(functools.partial(mp_gather_kernel, n, span), in_specs=[vm...  14.9 us
    pallas_call x1, Pallas kernels, passage_attention(): pl.pallas_call(functools.partial(passage_kernel, nx, nz), in_specs=[pl.Bl...  6.69 us
    dot_general x1, matrix products, local(): jnp.dot(normalized_hidden, w_query, preferred_element_type=jnp.float32)  3.1 us
    unnamed x7, local copies, waits for them, and re-layouts  2.76 us

profile of v15, /device:TPU:1, one launch (start us, length us, event | category | flops | bytes accessed | tf_op | source)
XLA Modules:
  0.0 127.0 jit_solution(6578357915269550147)
XLA Ops:
  0.6 0.0 copy-start
  0.7 14.9 %shard_map.149 = (bf16[64,4096]{1,0:T(8,128)(2,1)}, s32[8,32]{1,0:T(8,128)}, s32[128,1]{1,0:T(8,128)}) custom-call(bf16[32,512]{1,0:T(8,128)(2,1)} %p_ref.1, bf16[32,512]{1,0:T(8,128)(2,1)} %r_ref.1, s32[1,32]{1,0:T(1,128)} %bitcast.61, s32[1,32]{1,0:T(1,128)} %bitcast.62, s32[1,32]{1,0:T(1,128)} %bitcast.63, s32[1,32]{1,0:T(1,128)} %bitcast.64, ...), custom_call_target="tpu_custom_call" | custom-call | tf_op jit(solution)/shard_map/pallas_call | solution.py:185
  15.6 0.0 copy-start.1
  15.6 1.3 slice.78
  17.5 1.2 fusion.1
  18.7 0.1 fusion.34
  18.8 0.7 compare_bitcast_fusion
  19.5 0.1 maximum_bitcast_fusion.1
  19.6 0.1 maximum_bitcast_fusion
  19.7 0.6 pad_maximum_fusion.6.rot_ref
  20.3 0.8 slice_bitcast_fusion.5
  21.1 0.1 add_compare_fusion
  21.2 0.1 add_convert_fusion.1
  21.3 0.1 fusion.24
  21.3 0.0 copy-done
  21.3 1.4 %convolution_convert_fusion = bf16[64,128]{1,0:T(8,128)(2,1)S(1)} fusion(bf16[4096,128]{1,0:T(8,128)(2,1)S(1)} %copy-done, bf16[64,4096]{1,0:T(8,128)(2,1)} %get-tuple-element.9, f32[4096]{0:T(1024)} %param.18, f32[64]{0:T(128)S(1)} %add_rsqrt_fusion), kind=kOutput, calls=%fused_computation.5 | convolution fusion | flops 68165632 | bytes 1605888 | tf_op jit(solution)/shard_map/dot_general | solution.py:624
  22.7 1.7 %convolution_bitcast_fusion = f32[64,1,128]{2,0,1:T(8,128)S(1)} fusion(bf16[4096,128]{1,0:T(8,128)(2,1)} %param.20, bf16[64,4096]{1,0:T(8,128)(2,1)} %get-tuple-element.9, f32[4096]{0:T(1024)} %param.18, f32[64]{0:T(128)S(1)} %add_rsqrt_fusion), kind=kOutput, calls=%fused_computation.4 | convolution fusion | flops 68157440 | bytes 1622272 | tf_op jit(solution)/shard_map/dot_general | solution.py:616
  24.5 0.0 copy-done.1
  24.5 3.1 %fusion.37 = f32[64,512]{1,0:T(8,128)S(1)} fusion(bf16[4096,512]{1,0:T(8,128)(2,1)} %param.19, bf16[64,4096]{1,0:T(8,128)(2,1)S(1)} %copy-done.1, f32[4096]{0:T(1024)} %param.18, f32[64]{0:T(128)S(1)} %add_rsqrt_fusion), kind=kOutput, calls=%fused_computation.77 | convolution fusion | flops 269484032 | bytes 4866304 | tf_op jit(solution)/shard_map/dot_general | solution.py:607
  27.7 0.2 fusion.17
  27.9 0.1 fusion.26
  27.9 0.6 pad_maximum_fusion.3.fresh_ref
  28.6 0.2 multiply_cosine_fusion.1
  28.8 0.1 fusion.40
  28.9 0.3 fusion.41
  29.2 0.1 copy.35
  29.3 0.1 copy.36
  29.3 0.7 pad_maximum_fusion.x_ref
  30.1 0.2 fusion.18
  30.3 33.8 %shard_map.150 = (bf16[32,2,128,128]{3,2,1,0:T(8,128)(2,1)}, bf16[1024,128]{1,0:T(8,128)(2,1)}, bf16[1024,128]{1,0:T(8,128)(2,1)}) custom-call(bf16[2,128,128]{2,1,0:T(8,128)(2,1)} %pad_maximum_fusion.x_ref, bf16[1024,128]{1,0:T(8,128)(2,1)} %bitcast.54, bf16[1024,128]{1,0:T(8,128)(2,1)} %bitcast.55, bf16[32,256]{1,0:T(8,128)(2,1)} %pad_maximum_fusion.3.fresh_ref, ...), custom_call_target="tpu_custom_call" | custom-call | tf_op jit(solution)/shard_map/pallas_call | solution.py:416
  64.0 6.7 %shard_map.151 = bf16[64,144,128]{2,1,0:T(8,128)(2,1)} custom-call(s32[8,32]{1,0:T(8,128)} %get-tuple-element.8.meta_ref.flags_ref, bf16[64,128,128]{2,1,0:T(8,128)(2,1)} %bitcast.52, bf16[1024,128]{1,0:T(8,128)(2,1)} %get-tuple-element.11.k_ref, bf16[1024,128]{1,0:T(8,128)(2,1)} %get-tuple-element.12.v_ref, s32[128,1]{1,0:T(8,128)} %get-tuple-element.13.lim_ref), custom_call_target="tpu_custom_call" | custom-call | tf_op jit(solution)/shard_map/pallas_call | solution.py:100
  70.7 31.4 %shard_map.152 = bf16[4,2,144,128]{3,2,1,0:T(8,128)(2,1)} custom-call(bf16[32,2,144,128]{3,2,1,0:T(8,128)(2,1)} %bitcast.51), custom_call_target="tpu_custom_call" | custom-call | tf_op jit(solution)/shard_map/pallas_call | solution.py:546
  102.1 0.7 slice_convert_fusion
  102.8 0.1 reduce_max.21
  102.9 0.1 copy.37
  103.0 0.1 copy.38
  103.1 0.1 sub.38
  103.3 1.2 multiply_reduce_fusion
  104.5 0.1 reduce_sum.44
  104.6 0.1 copy.41
  104.7 0.8 copy_bitcast_fusion.a_ref
  105.4 18.8 %shard_map.153 = (bf16[32,512]{1,0:T(8,128)(2,1)}, bf16[32,512]{1,0:T(8,128)(2,1)}) custom-call(bf16[64,512]{1,0:T(8,128)(2,1)} %copy_bitcast_fusion.a_ref, bf16[512,4096]{1,0:T(8,128)(2,1)} %w_ref.1), custom_call_target="tpu_custom_call" | custom-call | tf_op jit(solution)/shard_map/pallas_call | solution.py:248
  124.3 1.4 %copy.64 = bf16[32,512]{1,0:T(8,128)(2,1)} copy(bf16[32,512]{1,0:T(8,128)(2,1)} %get-tuple-element.36) | data formatting | bytes 65536
  125.6 1.4 %copy.65 = bf16[32,512]{1,0:T(8,128)(2,1)} copy(bf16[32,512]{1,0:T(8,128)(2,1)} %get-tuple-element.37) | data formatting | bytes 65536
  (13 shorter events, 0.3 us)
Async XLA Ops:
  0.6 20.7 %copy-start = (bf16[4096,128]{1,0:T(8,128)(2,1)S(1)}, bf16[4096,128]{1,0:T(8,128)(2,1)}, u32[]{:S(2)}) copy-start(bf16[4096,128]{1,0:T(8,128)(2,1)} %param.21) | copy-start | bytes 3145732
  15.6 8.9 %copy-start.1 = (bf16[64,4096]{1,0:T(8,128)(2,1)S(1)}, bf16[64,4096]{1,0:T(8,128)(2,1)}, u32[]{:S(2)}) copy-start(bf16[64,4096]{1,0:T(8,128)(2,1)} %get-tuple-element.9) | copy-start | bytes 1572868

commit v16 on v14

--- a/solution.py
+++ b/solution.py
@@ -508,10 +508,12 @@
     for i in range(nx):
         last[(1, i)].wait_recv()
         last[(-1, i)].wait_recv()
-        merge_into(col.at[i], x_ref.at[i * nz + z], rp.at[steps, i])
-        merge_into(col.at[i], col.at[i], rm.at[steps, i])
-    for k in range(1, nx):
+    for k in list(range(1, nx)) + [0]:
         target = lax.rem(x + k, nx)
+        merge_into(col.at[target], x_ref.at[target * nz + z], rp.at[steps, target])
+        merge_into(col.at[target], col.at[target], rm.at[steps, target])
+        if k == 0:
+            continue
         c = pltpu.make_async_remote_copy(
             src_ref=col.at[target],
             dst_ref=y_ref.at[x],

time: 127 us -> 126 us (level)
    pallas_call x1, Pallas kernels: 30.1 us -> 31.9 us  [relay_reduce(): pl.pallas_call(functools.partial(relay_reduce_kernel, nx, nz), in_specs=[...]
    pallas_call x1, Pallas kernels: 19.6 us -> 18.2 us  [mp_scatter(): pl.pallas_call(functools.partial(mp_scatter_kernel, n), in_specs=[vmem, v...]
where the time goes in v16:
time: 126 us; the launch traced here: 125 us
  Pallas kernels  105 us (83%)
  other arithmetic  8.76 us (7%)
  matrix products  6.68 us (5%)
  local copies, waits for them, and re-layouts  3.58 us (3%)
  between operations  1.5 us (1%)
    pallas_call x1, Pallas kernels, relay_gather(): pl.pallas_call(functools.partial(relay_gather_kernel, nx, nz), in_specs=[...  33.8 us
    pallas_call x1, Pallas kernels, relay_reduce(): pl.pallas_call(functools.partial(relay_reduce_kernel, nx, nz), in_specs=[...  31.9 us
    pallas_call x1, Pallas kernels, mp_scatter(): pl.pallas_call(functools.partial(mp_scatter_kernel, n), in_specs=[vmem, v...  18.2 us
    pallas_call x1, Pallas kernels, mp_gather(): pl.pallas_call(functools.partial(mp_gather_kernel, n, span), in_specs=[vm...  14.9 us
    pallas_call x1, Pallas kernels, passage_attention(): pl.pallas_call(functools.partial(passage_kernel, nx, nz), in_specs=[pl.Bl...  6.17 us
    dot_general x1, matrix products, local(): jnp.dot(normalized_hidden, w_query, preferred_element_type=jnp.float32)  3.1 us

profile of v16, /device:TPU:1, one launch (start us, length us, event | category | flops | bytes accessed | tf_op | source)
XLA Modules:
  0.0 125.5 jit_solution(12303088004494721134)
XLA Ops:
  0.6 0.0 copy-start
  0.7 14.9 %shard_map.149 = (bf16[64,4096]{1,0:T(8,128)(2,1)}, s32[8,32]{1,0:T(8,128)}, s32[128,1]{1,0:T(8,128)}) custom-call(bf16[32,512]{1,0:T(8,128)(2,1)} %p_ref.1, bf16[32,512]{1,0:T(8,128)(2,1)} %r_ref.1, s32[1,32]{1,0:T(1,128)} %bitcast.61, s32[1,32]{1,0:T(1,128)} %bitcast.62, s32[1,32]{1,0:T(1,128)} %bitcast.63, s32[1,32]{1,0:T(1,128)} %bitcast.64, ...), custom_call_target="tpu_custom_call" | custom-call | tf_op jit(solution)/shard_map/pallas_call | solution.py:185
  15.6 0.0 copy-start.1
  15.6 1.3 slice.84
  17.5 1.2 fusion.1
  18.7 0.1 fusion.34
  18.8 0.7 compare_bitcast_fusion
  19.5 0.1 maximum_bitcast_fusion.1
  19.6 0.1 maximum_bitcast_fusion
  19.7 0.6 pad_maximum_fusion.6.rot_ref
  20.3 0.8 slice_bitcast_fusion.5
  21.1 0.1 add_compare_fusion
  21.2 0.1 add_convert_fusion.1
  21.3 0.1 fusion.24
  21.3 0.0 copy-done
  21.3 1.4 %convolution_convert_fusion = bf16[64,128]{1,0:T(8,128)(2,1)S(1)} fusion(bf16[4096,128]{1,0:T(8,128)(2,1)S(1)} %copy-done, bf16[64,4096]{1,0:T(8,128)(2,1)} %get-tuple-element.9, f32[4096]{0:T(1024)} %param.18, f32[64]{0:T(128)S(1)} %add_rsqrt_fusion), kind=kOutput, calls=%fused_computation.5 | convolution fusion | flops 68165632 | bytes 1605888 | tf_op jit(solution)/shard_map/dot_general | solution.py:616
  22.7 1.7 %convolution_bitcast_fusion = f32[64,1,128]{2,0,1:T(8,128)S(1)} fusion(bf16[4096,128]{1,0:T(8,128)(2,1)} %param.20, bf16[64,4096]{1,0:T(8,128)(2,1)} %get-tuple-element.9, f32[4096]{0:T(1024)} %param.18, f32[64]{0:T(128)S(1)} %add_rsqrt_fusion), kind=kOutput, calls=%fused_computation.4 | convolution fusion | flops 68157440 | bytes 1622272 | tf_op jit(solution)/shard_map/dot_general | solution.py:608
  24.5 0.0 copy-done.1
  24.5 3.1 %fusion.37 = f32[64,512]{1,0:T(8,128)S(1)} fusion(bf16[4096,512]{1,0:T(8,128)(2,1)} %param.19, bf16[64,4096]{1,0:T(8,128)(2,1)S(1)} %copy-done.1, f32[4096]{0:T(1024)} %param.18, f32[64]{0:T(128)S(1)} %add_rsqrt_fusion), kind=kOutput, calls=%fused_computation.77 | convolution fusion | flops 269484032 | bytes 4866304 | tf_op jit(solution)/shard_map/dot_general | solution.py:599
  27.7 0.2 fusion.17
  27.9 0.1 fusion.26
  27.9 0.6 pad_maximum_fusion.3.fresh_ref
  28.6 0.2 multiply_cosine_fusion.1
  28.8 0.1 fusion.40
  28.9 0.3 fusion.42
  29.2 0.1 copy.35
  29.3 0.1 copy.36
  29.3 0.7 pad_maximum_fusion.x_ref
  30.1 0.2 fusion.18
  30.3 33.8 %shard_map.150 = (bf16[32,2,128,128]{3,2,1,0:T(8,128)(2,1)}, bf16[1024,128]{1,0:T(8,128)(2,1)}, bf16[1024,128]{1,0:T(8,128)(2,1)}) custom-call(bf16[2,128,128]{2,1,0:T(8,128)(2,1)} %pad_maximum_fusion.x_ref, bf16[1024,128]{1,0:T(8,128)(2,1)} %bitcast.54, bf16[1024,128]{1,0:T(8,128)(2,1)} %bitcast.55, bf16[32,256]{1,0:T(8,128)(2,1)} %pad_maximum_fusion.3.fresh_ref, ...), custom_call_target="tpu_custom_call" | custom-call | tf_op jit(solution)/shard_map/pallas_call | solution.py:406
  64.0 6.2 %shard_map.151 = bf16[64,144,128]{2,1,0:T(8,128)(2,1)} custom-call(s32[8,32]{1,0:T(8,128)} %get-tuple-element.8.meta_ref.flags_ref, bf16[64,128,128]{2,1,0:T(8,128)(2,1)} %bitcast.52, bf16[1024,128]{1,0:T(8,128)(2,1)} %get-tuple-element.11.k_ref, bf16[1024,128]{1,0:T(8,128)(2,1)} %get-tuple-element.12.v_ref, s32[128,1]{1,0:T(8,128)} %get-tuple-element.13.lim_ref), custom_call_target="tpu_custom_call" | custom-call | tf_op jit(solution)/shard_map/pallas_call | solution.py:100
  70.2 31.9 %shard_map.152 = bf16[4,2,144,128]{3,2,1,0:T(8,128)(2,1)} custom-call(bf16[32,2,144,128]{3,2,1,0:T(8,128)(2,1)} %bitcast.51), custom_call_target="tpu_custom_call" | custom-call | tf_op jit(solution)/shard_map/pallas_call | solution.py:538
  102.1 0.7 slice_convert_fusion
  102.9 0.1 reduce_max.21
  103.0 0.1 copy.37
  103.1 0.1 copy.38
  103.2 0.1 sub.38
  103.3 1.2 multiply_reduce_fusion
  104.5 0.1 reduce_sum.56
  104.6 0.1 copy.41
  104.7 0.8 copy_bitcast_fusion.a_ref
  105.5 18.2 %shard_map.153 = bf16[8,64,512]{2,1,0:T(8,128)(2,1)} custom-call(bf16[64,512]{1,0:T(8,128)(2,1)} %copy_bitcast_fusion.a_ref, bf16[512,4096]{1,0:T(8,128)(2,1)} %w_ref.1), custom_call_target="tpu_custom_call" | custom-call | tf_op jit(solution)/shard_map/pallas_call | solution.py:242
  123.7 1.1 reduce_sum.58
  124.8 0.6 fusion.41
  (13 shorter events, 0.3 us)
Async XLA Ops:
  0.6 20.7 %copy-start = (bf16[4096,128]{1,0:T(8,128)(2,1)S(1)}, bf16[4096,128]{1,0:T(8,128)(2,1)}, u32[]{:S(2)}) copy-start(bf16[4096,128]{1,0:T(8,128)(2,1)} %param.21) | copy-start | bytes 3145732
  15.6 8.9 %copy-start.1 = (bf16[64,4096]{1,0:T(8,128)(2,1)S(1)}, bf16[64,4096]{1,0:T(8,128)(2,1)}, u32[]{:S(2)}) copy-start(bf16[64,4096]{1,0:T(8,128)(2,1)} %get-tuple-element.9) | copy-start | bytes 1572868

commit v17 on v16

--- a/solution.py
+++ b/solution.py
@@ -63,20 +63,21 @@
     def attend(b, masked):
         d = b // 2
         stored = ((d % nz) * nx + d // nz) * 2 + b % 2
-        scores = lax.dot_general(
+        scale = 1.0 / math.sqrt(HEAD_SIZE)
+        raw = lax.dot_general(
             q_ref[stored], k_ref[...], (((1,), (1,)), ((), ())), preferred_element_type=jnp.float32
-        ) * (1.0 / math.sqrt(HEAD_SIZE))
+        )
         if masked:
-            scores = jnp.where(token <= lim_ref[...], scores, NEGATIVE_FLOOR)
-        maxima = jnp.max(scores, axis=1, keepdims=True)
-        weights = jnp.exp(scores - maxima)
+            raw = jnp.where(token <= lim_ref[...], raw, NEGATIVE_FLOOR)
+        raw_max = jnp.max(raw, axis=1, keepdims=True)
+        weights = jnp.exp((raw - raw_max) * scale)
         totals = jnp.sum(weights, axis=1, keepdims=True)
         out_ref[b, 0:rows] = jnp.dot(
             weights.astype(jnp.bfloat16), v_ref[...], preferred_element_type=jnp.float32
         ).astype(out_ref.dtype)
-        m_row = jnp.transpose(jnp.broadcast_to(maxima, (rows, rows)))[0:16]
-        l_row = jnp.transpose(jnp.broadcast_to(totals, (rows, rows)))[0:16]
-        out_ref[b, rows:] = split(m_row, l_row)
+        lane = lax.broadcasted_iota(jnp.int32, (rows, rows), 1)
+        both = jnp.transpose(jnp.where(lane < rows // 2, raw_max * scale, totals))
+        out_ref[b, rows:] = split(both[0:16], both[rows // 2 : rows // 2 + 16])
 
     def body(b, carry):
         flag = flags_ref[4 + b % 2, b // 2]

time: 126 us -> 128 us (1.016)
  Pallas kernels: 105 us -> 107 us
where the time goes in v17:
time: 128 us; the launch traced here: 127 us
  Pallas kernels  107 us (84%)
  other arithmetic  8.76 us (7%)
  matrix products  6.68 us (5%)
  local copies, waits for them, and re-layouts  3.58 us (3%)
  between operations  1.5 us (1%)
    pallas_call x1, Pallas kernels, relay_gather(): pl.pallas_call(functools.partial(relay_gather_kernel, nx, nz), in_specs=[...  33.8 us
    pallas_call x1, Pallas kernels, relay_reduce(): pl.pallas_call(functools.partial(relay_reduce_kernel, nx, nz), in_specs=[...  31.9 us
    pallas_call x1, Pallas kernels, mp_scatter(): pl.pallas_call(functools.partial(mp_scatter_kernel, n), in_specs=[vmem, v...  18.7 us
    pallas_call x1, Pallas kernels, mp_gather(): pl.pallas_call(functools.partial(mp_gather_kernel, n, span), in_specs=[vm...  14.9 us
    pallas_call x1, Pallas kernels, passage_attention(): pl.pallas_call(functools.partial(passage_kernel, nx, nz), in_specs=[pl.Bl...  7.24 us
    dot_general x1, matrix products, local(): jnp.dot(normalized_hidden, w_query, preferred_element_type=jnp.float32)  3.1 us

profile of v17, /device:TPU:1, one launch (start us, length us, event | category | flops | bytes accessed | tf_op | source)
XLA Modules:
  0.0 127.0 jit_solution(2548024283747298624)
XLA Ops:
  0.6 0.0 copy-start
  0.7 14.9 %shard_map.149 = (bf16[64,4096]{1,0:T(8,128)(2,1)}, s32[8,32]{1,0:T(8,128)}, s32[128,1]{1,0:T(8,128)}) custom-call(bf16[32,512]{1,0:T(8,128)(2,1)} %p_ref.1, bf16[32,512]{1,0:T(8,128)(2,1)} %r_ref.1, s32[1,32]{1,0:T(1,128)} %bitcast.61, s32[1,32]{1,0:T(1,128)} %bitcast.62, s32[1,32]{1,0:T(1,128)} %bitcast.63, s32[1,32]{1,0:T(1,128)} %bitcast.64, ...), custom_call_target="tpu_custom_call" | custom-call | tf_op jit(solution)/shard_map/pallas_call | solution.py:186
  15.6 0.0 copy-start.1
  15.6 1.3 slice.84
  17.5 1.2 fusion.1
  18.7 0.1 fusion.34
  18.8 0.7 compare_bitcast_fusion
  19.5 0.1 maximum_bitcast_fusion.1
  19.6 0.1 maximum_bitcast_fusion
  19.7 0.6 pad_maximum_fusion.6.rot_ref
  20.3 0.8 slice_bitcast_fusion.5
  21.1 0.1 add_compare_fusion
  21.2 0.1 add_convert_fusion.1
  21.3 0.1 fusion.24
  21.3 0.0 copy-done
  21.3 1.4 %convolution_convert_fusion = bf16[64,128]{1,0:T(8,128)(2,1)S(1)} fusion(bf16[4096,128]{1,0:T(8,128)(2,1)S(1)} %copy-done, bf16[64,4096]{1,0:T(8,128)(2,1)} %get-tuple-element.9, f32[4096]{0:T(1024)} %param.18, f32[64]{0:T(128)S(1)} %add_rsqrt_fusion), kind=kOutput, calls=%fused_computation.5 | convolution fusion | flops 68165632 | bytes 1605888 | tf_op jit(solution)/shard_map/dot_general | solution.py:617
  22.7 1.7 %convolution_bitcast_fusion = f32[64,1,128]{2,0,1:T(8,128)S(1)} fusion(bf16[4096,128]{1,0:T(8,128)(2,1)} %param.20, bf16[64,4096]{1,0:T(8,128)(2,1)} %get-tuple-element.9, f32[4096]{0:T(1024)} %param.18, f32[64]{0:T(128)S(1)} %add_rsqrt_fusion), kind=kOutput, calls=%fused_computation.4 | convolution fusion | flops 68157440 | bytes 1622272 | tf_op jit(solution)/shard_map/dot_general | solution.py:609
  24.5 0.0 copy-done.1
  24.5 3.1 %fusion.37 = f32[64,512]{1,0:T(8,128)S(1)} fusion(bf16[4096,512]{1,0:T(8,128)(2,1)} %param.19, bf16[64,4096]{1,0:T(8,128)(2,1)S(1)} %copy-done.1, f32[4096]{0:T(1024)} %param.18, f32[64]{0:T(128)S(1)} %add_rsqrt_fusion), kind=kOutput, calls=%fused_computation.77 | convolution fusion | flops 269484032 | bytes 4866304 | tf_op jit(solution)/shard_map/dot_general | solution.py:600
  27.7 0.2 fusion.17
  27.9 0.1 fusion.26
  27.9 0.6 pad_maximum_fusion.3.fresh_ref
  28.6 0.2 multiply_cosine_fusion.1
  28.8 0.1 fusion.40
  28.9 0.3 fusion.42
  29.2 0.1 copy.35
  29.3 0.1 copy.36
  29.3 0.7 pad_maximum_fusion.x_ref
  30.1 0.2 fusion.18
  30.3 33.8 %shard_map.150 = (bf16[32,2,128,128]{3,2,1,0:T(8,128)(2,1)}, bf16[1024,128]{1,0:T(8,128)(2,1)}, bf16[1024,128]{1,0:T(8,128)(2,1)}) custom-call(bf16[2,128,128]{2,1,0:T(8,128)(2,1)} %pad_maximum_fusion.x_ref, bf16[1024,128]{1,0:T(8,128)(2,1)} %bitcast.54, bf16[1024,128]{1,0:T(8,128)(2,1)} %bitcast.55, bf16[32,256]{1,0:T(8,128)(2,1)} %pad_maximum_fusion.3.fresh_ref, ...), custom_call_target="tpu_custom_call" | custom-call | tf_op jit(solution)/shard_map/pallas_call | solution.py:407
  64.0 7.2 %shard_map.151 = bf16[64,144,128]{2,1,0:T(8,128)(2,1)} custom-call(s32[8,32]{1,0:T(8,128)} %get-tuple-element.8.meta_ref.flags_ref, bf16[64,128,128]{2,1,0:T(8,128)(2,1)} %bitcast.52, bf16[1024,128]{1,0:T(8,128)(2,1)} %get-tuple-element.11.k_ref, bf16[1024,128]{1,0:T(8,128)(2,1)} %get-tuple-element.12.v_ref, s32[128,1]{1,0:T(8,128)} %get-tuple-element.13.lim_ref), custom_call_target="tpu_custom_call" | custom-call | tf_op jit(solution)/shard_map/pallas_call | solution.py:101
  71.3 31.9 %shard_map.152 = bf16[4,2,144,128]{3,2,1,0:T(8,128)(2,1)} custom-call(bf16[32,2,144,128]{3,2,1,0:T(8,128)(2,1)} %bitcast.51), custom_call_target="tpu_custom_call" | custom-call | tf_op jit(solution)/shard_map/pallas_call | solution.py:539
  103.2 0.7 slice_convert_fusion
  103.9 0.1 reduce_max.21
  104.0 0.1 copy.37
  104.1 0.1 copy.38
  104.2 0.1 sub.38
  104.4 1.2 multiply_reduce_fusion
  105.5 0.1 reduce_sum.56
  105.7 0.1 copy.41
  105.8 0.8 copy_bitcast_fusion.a_ref
  106.5 18.7 %shard_map.153 = bf16[8,64,512]{2,1,0:T(8,128)(2,1)} custom-call(bf16[64,512]{1,0:T(8,128)(2,1)} %copy_bitcast_fusion.a_ref, bf16[512,4096]{1,0:T(8,128)(2,1)} %w_ref.1), custom_call_target="tpu_custom_call" | custom-call | tf_op jit(solution)/shard_map/pallas_call | solution.py:243
  125.3 1.1 reduce_sum.58
  126.4 0.6 fusion.41
  (13 shorter events, 0.3 us)
Async XLA Ops:
  0.6 20.7 %copy-start = (bf16[4096,128]{1,0:T(8,128)(2,1)S(1)}, bf16[4096,128]{1,0:T(8,128)(2,1)}, u32[]{:S(2)}) copy-start(bf16[4096,128]{1,0:T(8,128)(2,1)} %param.21) | copy-start | bytes 3145732
  15.6 8.9 %copy-start.1 = (bf16[64,4096]{1,0:T(8,128)(2,1)S(1)}, bf16[64,4096]{1,0:T(8,128)(2,1)}, u32[]{:S(2)}) copy-start(bf16[64,4096]{1,0:T(8,128)(2,1)} %get-tuple-element.9) | copy-start | bytes 1572868

commit v18 on v17

--- a/solution.py
+++ b/solution.py
@@ -294,19 +294,6 @@
     ]
     own = pltpu.make_async_copy(x_ref, y_ref.at[slot], own_sem)
     own.start()
-
-    width = kc_ref.shape[1]
-    cached = kc_ref[...].astype(jnp.float32)
-    turned = pltpu.roll(cached, width // 2, 1)
-    shifted = (cached * rot_ref[0:1, :] + turned * rot_ref[1:2, :]).astype(pk_ref.dtype)
-    token = lax.broadcasted_iota(jnp.int32, (kc_ref.shape[0], meta_ref.shape[1]), 0)
-    chosen = (token == meta_ref[6:7, :]) & (meta_ref[3:4, :] > 0)
-    placed = jnp.dot(
-        chosen.astype(jnp.bfloat16), fresh_ref[...], preferred_element_type=jnp.float32
-    ).astype(pk_ref.dtype)
-    replaced = jnp.max(jnp.where(chosen, 1.0, 0.0), axis=1, keepdims=True) > 0.0
-    pk_ref[...] = jnp.where(replaced, placed[:, :width], shifted)
-    pv_ref[...] = jnp.where(replaced, placed[:, width:], vc_ref[...])
 
     def x_out(column):
         a = copy(
@@ -389,6 +376,19 @@
                     fm_send.at[zc], fm_recv.at[zc], (left * nz + z, mp),
                 )
             )
+    width = kc_ref.shape[1]
+    cached = kc_ref[...].astype(jnp.float32)
+    turned = pltpu.roll(cached, width // 2, 1)
+    shifted = (cached * rot_ref[0:1, :] + turned * rot_ref[1:2, :]).astype(pk_ref.dtype)
+    token = lax.broadcasted_iota(jnp.int32, (kc_ref.shape[0], meta_ref.shape[1]), 0)
+    chosen = (token == meta_ref[6:7, :]) & (meta_ref[3:4, :] > 0)
+    placed = jnp.dot(
+        chosen.astype(jnp.bfloat16), fresh_ref[...], preferred_element_type=jnp.float32
+    ).astype(pk_ref.dtype)
+    replaced = jnp.max(jnp.where(chosen, 1.0, 0.0), axis=1, keepdims=True) > 0.0
+    pk_ref[...] = jnp.where(replaced, placed[:, :width], shifted)
+    pv_ref[...] = jnp.where(replaced, placed[:, width:], vc_ref[...])
+
     for c in zlast.values():
         c.wait_recv()
     for c in forwards:

time: 128 us -> 128 us (level)
    pallas_call x1, Pallas kernels: 7.24 us -> 10.4 us  [passage_attention(): pl.pallas_call(functools.partial(passage_kernel, nx, nz), in_specs=[pl.Bl...]
    pallas_call x1, Pallas kernels: 31.9 us -> 30 us  [relay_reduce(): pl.pallas_call(functools.partial(relay_reduce_kernel, nx, nz), in_specs=[...]
where the time goes in v18:
time: 128 us
  Pallas kernels  107 us (84%)
  other arithmetic  8.76 us (7%)
  matrix products  6.68 us (5%)
  local copies, waits for them, and re-layouts  3.58 us (3%)
  between operations  1.5 us (1%)
    pallas_call x1, Pallas kernels, relay_gather(): pl.pallas_call(functools.partial(relay_gather_kernel, nx, nz), in_specs=[...  33.8 us
    pallas_call x1, Pallas kernels, relay_reduce(): pl.pallas_call(functools.partial(relay_reduce_kernel, nx, nz), in_specs=[...  30 us
    pallas_call x1, Pallas kernels, mp_scatter(): pl.pallas_call(functools.partial(mp_scatter_kernel, n), in_specs=[vmem, v...  18.4 us
    pallas_call x1, Pallas kernels, mp_gather(): pl.pallas_call(functools.partial(mp_gather_kernel, n, span), in_specs=[vm...  14.9 us
    pallas_call x1, Pallas kernels, passage_attention(): pl.pallas_call(functools.partial(passage_kernel, nx, nz), in_specs=[pl.Bl...  10.4 us
    dot_general x1, matrix products, local(): jnp.dot(normalized_hidden, w_query, preferred_element_type=jnp.float32)  3.1 us

profile of v18, /device:TPU:1, one launch (start us, length us, event | category | flops | bytes accessed | tf_op | source)
XLA Modules:
  0.0 127.9 jit_solution(14718886016820228651)
XLA Ops:
  0.6 0.0 copy-start
  0.7 14.9 %shard_map.149 = (bf16[64,4096]{1,0:T(8,128)(2,1)}, s32[8,32]{1,0:T(8,128)}, s32[128,1]{1,0:T(8,128)}) custom-call(bf16[32,512]{1,0:T(8,128)(2,1)} %p_ref.1, bf16[32,512]{1,0:T(8,128)(2,1)} %r_ref.1, s32[1,32]{1,0:T(1,128)} %bitcast.61, s32[1,32]{1,0:T(1,128)} %bitcast.62, s32[1,32]{1,0:T(1,128)} %bitcast.63, s32[1,32]{1,0:T(1,128)} %bitcast.64, ...), custom_call_target="tpu_custom_call" | custom-call | tf_op jit(solution)/shard_map/pallas_call | solution.py:186
  15.6 0.0 copy-start.1
  15.6 1.3 slice.84
  17.5 1.2 fusion.1
  18.7 0.1 fusion.34
  18.8 0.7 compare_bitcast_fusion
  19.5 0.1 maximum_bitcast_fusion.1
  19.6 0.1 maximum_bitcast_fusion
  19.7 0.6 pad_maximum_fusion.6.rot_ref
  20.3 0.8 slice_bitcast_fusion.5
  21.1 0.1 add_compare_fusion
  21.2 0.1 add_convert_fusion.1
  21.3 0.1 fusion.24
  21.3 0.0 copy-done
  21.3 1.4 %convolution_convert_fusion = bf16[64,128]{1,0:T(8,128)(2,1)S(1)} fusion(bf16[4096,128]{1,0:T(8,128)(2,1)S(1)} %copy-done, bf16[64,4096]{1,0:T(8,128)(2,1)} %get-tuple-element.9, f32[4096]{0:T(1024)} %param.18, f32[64]{0:T(128)S(1)} %add_rsqrt_fusion), kind=kOutput, calls=%fused_computation.5 | convolution fusion | flops 68165632 | bytes 1605888 | tf_op jit(solution)/shard_map/dot_general | solution.py:617
  22.7 1.7 %convolution_bitcast_fusion = f32[64,1,128]{2,0,1:T(8,128)S(1)} fusion(bf16[4096,128]{1,0:T(8,128)(2,1)} %param.20, bf16[64,4096]{1,0:T(8,128)(2,1)} %get-tuple-element.9, f32[4096]{0:T(1024)} %param.18, f32[64]{0:T(128)S(1)} %add_rsqrt_fusion), kind=kOutput, calls=%fused_computation.4 | convolution fusion | flops 68157440 | bytes 1622272 | tf_op jit(solution)/shard_map/dot_general | solution.py:609
  24.5 0.0 copy-done.1
  24.5 3.1 %fusion.37 = f32[64,512]{1,0:T(8,128)S(1)} fusion(bf16[4096,512]{1,0:T(8,128)(2,1)} %param.19, bf16[64,4096]{1,0:T(8,128)(2,1)S(1)} %copy-done.1, f32[4096]{0:T(1024)} %param.18, f32[64]{0:T(128)S(1)} %add_rsqrt_fusion), kind=kOutput, calls=%fused_computation.77 | convolution fusion | flops 269484032 | bytes 4866304 | tf_op jit(solution)/shard_map/dot_general | solution.py:600
  27.7 0.2 fusion.17
  27.9 0.1 fusion.26
  27.9 0.6 pad_maximum_fusion.3.fresh_ref
  28.6 0.2 multiply_cosine_fusion.1
  28.8 0.1 fusion.40
  28.9 0.3 fusion.42
  29.2 0.1 copy.35
  29.3 0.1 copy.36
  29.3 0.7 pad_maximum_fusion.x_ref
  30.1 0.2 fusion.18
  30.3 33.8 %shard_map.150 = (bf16[32,2,128,128]{3,2,1,0:T(8,128)(2,1)}, bf16[1024,128]{1,0:T(8,128)(2,1)}, bf16[1024,128]{1,0:T(8,128)(2,1)}) custom-call(bf16[2,128,128]{2,1,0:T(8,128)(2,1)} %pad_maximum_fusion.x_ref, bf16[1024,128]{1,0:T(8,128)(2,1)} %bitcast.54, bf16[1024,128]{1,0:T(8,128)(2,1)} %bitcast.55, bf16[32,256]{1,0:T(8,128)(2,1)} %pad_maximum_fusion.3.fresh_ref, ...), custom_call_target="tpu_custom_call" | custom-call | tf_op jit(solution)/shard_map/pallas_call | solution.py:407
  64.0 10.4 %shard_map.151 = bf16[64,144,128]{2,1,0:T(8,128)(2,1)} custom-call(s32[8,32]{1,0:T(8,128)} %get-tuple-element.8.meta_ref.flags_ref, bf16[64,128,128]{2,1,0:T(8,128)(2,1)} %bitcast.52, bf16[1024,128]{1,0:T(8,128)(2,1)} %get-tuple-element.11.k_ref, bf16[1024,128]{1,0:T(8,128)(2,1)} %get-tuple-element.12.v_ref, s32[128,1]{1,0:T(8,128)} %get-tuple-element.13.lim_ref), custom_call_target="tpu_custom_call" | custom-call | tf_op jit(solution)/shard_map/pallas_call | solution.py:101
  74.4 30.0 %shard_map.152 = bf16[4,2,144,128]{3,2,1,0:T(8,128)(2,1)} custom-call(bf16[32,2,144,128]{3,2,1,0:T(8,128)(2,1)} %bitcast.51), custom_call_target="tpu_custom_call" | custom-call | tf_op jit(solution)/shard_map/pallas_call | solution.py:539
  104.4 0.7 slice_convert_fusion
  105.1 0.1 reduce_max.21
  105.3 0.1 copy.37
  105.3 0.1 copy.38
  105.4 0.1 sub.38
  105.6 1.2 multiply_reduce_fusion
  106.8 0.1 reduce_sum.56
  106.9 0.1 copy.41
  107.0 0.8 copy_bitcast_fusion.a_ref
  107.8 18.4 %shard_map.153 = bf16[8,64,512]{2,1,0:T(8,128)(2,1)} custom-call(bf16[64,512]{1,0:T(8,128)(2,1)} %copy_bitcast_fusion.a_ref, bf16[512,4096]{1,0:T(8,128)(2,1)} %w_ref.1), custom_call_target="tpu_custom_call" | custom-call | tf_op jit(solution)/shard_map/pallas_call | solution.py:243
  126.1 1.1 reduce_sum.58
  127.2 0.6 fusion.41
  (13 shorter events, 0.3 us)
Async XLA Ops:
  0.6 20.7 %copy-start = (bf16[4096,128]{1,0:T(8,128)(2,1)S(1)}, bf16[4096,128]{1,0:T(8,128)(2,1)}, u32[]{:S(2)}) copy-start(bf16[4096,128]{1,0:T(8,128)(2,1)} %param.21) | copy-start | bytes 3145732
  15.6 8.9 %copy-start.1 = (bf16[64,4096]{1,0:T(8,128)(2,1)S(1)}, bf16[64,4096]{1,0:T(8,128)(2,1)}, u32[]{:S(2)}) copy-start(bf16[64,4096]{1,0:T(8,128)(2,1)} %get-tuple-element.9) | copy-start | bytes 1572868

commit v19 on v14

--- a/solution.py
+++ b/solution.py
@@ -435,8 +435,10 @@
     s1 = jnp.exp(m1 - top)
     s2 = jnp.exp(m2 - top)
     total = l1 * s1 + l2 * s2
-    c1 = jnp.transpose(jnp.broadcast_to(s1, (rows, rows)))
-    c2 = jnp.transpose(jnp.broadcast_to(s2, (rows, rows)))
+    upper = lax.broadcasted_iota(jnp.int32, (rows, rows), 0) < rows // 2
+    both = jnp.transpose(jnp.where(upper, s1, s2))
+    c1 = both[:, 0:1]
+    c2 = both[:, rows // 2 : rows // 2 + 1]
     acc = af[0:rows] * c1 + bf[0:rows] * c2
     sub = lax.broadcasted_iota(jnp.int32, (16, rows), 0)
     top_hi = top.astype(jnp.bfloat16).astype(jnp.float32)

time: 127 us -> 127 us (level)
    pallas_call x1, Pallas kernels: 30.1 us -> 31.5 us  [relay_reduce(): pl.pallas_call(functools.partial(relay_reduce_kernel, nx, nz), in_specs=[...]
where the time goes in v19:
time: 127 us; the launch traced here: 126 us
  Pallas kernels  106 us (83%)
  other arithmetic  8.76 us (7%)
  matrix products  6.68 us (5%)
  local copies, waits for them, and re-layouts  3.58 us (3%)
  between operations  1.5 us (1%)
    pallas_call x1, Pallas kernels, relay_gather(): pl.pallas_call(functools.partial(relay_gather_kernel, nx, nz), in_specs=[...  33.8 us
    pallas_call x1, Pallas kernels, relay_reduce(): pl.pallas_call(functools.partial(relay_reduce_kernel, nx, nz), in_specs=[...  31.5 us
    pallas_call x1, Pallas kernels, mp_scatter(): pl.pallas_call(functools.partial(mp_scatter_kernel, n), in_specs=[vmem, v...  19 us
    pallas_call x1, Pallas kernels, mp_gather(): pl.pallas_call(functools.partial(mp_gather_kernel, n, span), in_specs=[vm...  14.9 us
    pallas_call x1, Pallas kernels, passage_attention(): pl.pallas_call(functools.partial(passage_kernel, nx, nz), in_specs=[pl.Bl...  6.69 us
    dot_general x1, matrix products, local(): jnp.dot(normalized_hidden, w_query, preferred_element_type=jnp.float32)  3.1 us

profile of v19, /device:TPU:1, one launch (start us, length us, event | category | flops | bytes accessed | tf_op | source)
XLA Modules:
  0.0 126.4 jit_solution(17596315762735903877)
XLA Ops:
  0.6 0.0 copy-start
  0.7 14.9 %shard_map.149 = (bf16[64,4096]{1,0:T(8,128)(2,1)}, s32[8,32]{1,0:T(8,128)}, s32[128,1]{1,0:T(8,128)}) custom-call(bf16[32,512]{1,0:T(8,128)(2,1)} %p_ref.1, bf16[32,512]{1,0:T(8,128)(2,1)} %r_ref.1, s32[1,32]{1,0:T(1,128)} %bitcast.61, s32[1,32]{1,0:T(1,128)} %bitcast.62, s32[1,32]{1,0:T(1,128)} %bitcast.63, s32[1,32]{1,0:T(1,128)} %bitcast.64, ...), custom_call_target="tpu_custom_call" | custom-call | tf_op jit(solution)/shard_map/pallas_call | solution.py:185
  15.6 0.0 copy-start.1
  15.6 1.3 slice.84
  17.5 1.2 fusion.1
  18.7 0.1 fusion.34
  18.8 0.7 compare_bitcast_fusion
  19.5 0.1 maximum_bitcast_fusion.1
  19.6 0.1 maximum_bitcast_fusion
  19.7 0.6 pad_maximum_fusion.6.rot_ref
  20.3 0.8 slice_bitcast_fusion.5
  21.1 0.1 add_compare_fusion
  21.2 0.1 add_convert_fusion.1
  21.3 0.1 fusion.24
  21.3 0.0 copy-done
  21.3 1.4 %convolution_convert_fusion = bf16[64,128]{1,0:T(8,128)(2,1)S(1)} fusion(bf16[4096,128]{1,0:T(8,128)(2,1)S(1)} %copy-done, bf16[64,4096]{1,0:T(8,128)(2,1)} %get-tuple-element.9, f32[4096]{0:T(1024)} %param.18, f32[64]{0:T(128)S(1)} %add_rsqrt_fusion), kind=kOutput, calls=%fused_computation.5 | convolution fusion | flops 68165632 | bytes 1605888 | tf_op jit(solution)/shard_map/dot_general | solution.py:616
  22.7 1.7 %convolution_bitcast_fusion = f32[64,1,128]{2,0,1:T(8,128)S(1)} fusion(bf16[4096,128]{1,0:T(8,128)(2,1)} %param.20, bf16[64,4096]{1,0:T(8,128)(2,1)} %get-tuple-element.9, f32[4096]{0:T(1024)} %param.18, f32[64]{0:T(128)S(1)} %add_rsqrt_fusion), kind=kOutput, calls=%fused_computation.4 | convolution fusion | flops 68157440 | bytes 1622272 | tf_op jit(solution)/shard_map/dot_general | solution.py:608
  24.5 0.0 copy-done.1
  24.5 3.1 %fusion.37 = f32[64,512]{1,0:T(8,128)S(1)} fusion(bf16[4096,512]{1,0:T(8,128)(2,1)} %param.19, bf16[64,4096]{1,0:T(8,128)(2,1)S(1)} %copy-done.1, f32[4096]{0:T(1024)} %param.18, f32[64]{0:T(128)S(1)} %add_rsqrt_fusion), kind=kOutput, calls=%fused_computation.77 | convolution fusion | flops 269484032 | bytes 4866304 | tf_op jit(solution)/shard_map/dot_general | solution.py:599
  27.7 0.2 fusion.17
  27.9 0.1 fusion.26
  27.9 0.6 pad_maximum_fusion.3.fresh_ref
  28.6 0.2 multiply_cosine_fusion.1
  28.8 0.1 fusion.40
  28.9 0.3 fusion.42
  29.2 0.1 copy.35
  29.3 0.1 copy.36
  29.3 0.7 pad_maximum_fusion.x_ref
  30.1 0.2 fusion.18
  30.3 33.8 %shard_map.150 = (bf16[32,2,128,128]{3,2,1,0:T(8,128)(2,1)}, bf16[1024,128]{1,0:T(8,128)(2,1)}, bf16[1024,128]{1,0:T(8,128)(2,1)}) custom-call(bf16[2,128,128]{2,1,0:T(8,128)(2,1)} %pad_maximum_fusion.x_ref, bf16[1024,128]{1,0:T(8,128)(2,1)} %bitcast.54, bf16[1024,128]{1,0:T(8,128)(2,1)} %bitcast.55, bf16[32,256]{1,0:T(8,128)(2,1)} %pad_maximum_fusion.3.fresh_ref, ...), custom_call_target="tpu_custom_call" | custom-call | tf_op jit(solution)/shard_map/pallas_call | solution.py:406
  64.0 6.7 %shard_map.151 = bf16[64,144,128]{2,1,0:T(8,128)(2,1)} custom-call(s32[8,32]{1,0:T(8,128)} %get-tuple-element.8.meta_ref.flags_ref, bf16[64,128,128]{2,1,0:T(8,128)(2,1)} %bitcast.52, bf16[1024,128]{1,0:T(8,128)(2,1)} %get-tuple-element.11.k_ref, bf16[1024,128]{1,0:T(8,128)(2,1)} %get-tuple-element.12.v_ref, s32[128,1]{1,0:T(8,128)} %get-tuple-element.13.lim_ref), custom_call_target="tpu_custom_call" | custom-call | tf_op jit(solution)/shard_map/pallas_call | solution.py:100
  70.7 31.5 %shard_map.152 = bf16[4,2,144,128]{3,2,1,0:T(8,128)(2,1)} custom-call(bf16[32,2,144,128]{3,2,1,0:T(8,128)(2,1)} %bitcast.51), custom_call_target="tpu_custom_call" | custom-call | tf_op jit(solution)/shard_map/pallas_call | solution.py:538
  102.2 0.7 slice_convert_fusion
  103.0 0.1 reduce_max.21
  103.1 0.1 copy.37
  103.2 0.1 copy.38
  103.3 0.1 sub.38
  103.4 1.2 multiply_reduce_fusion
  104.6 0.1 reduce_sum.56
  104.7 0.1 copy.41
  104.8 0.8 copy_bitcast_fusion.a_ref
  105.6 19.0 %shard_map.153 = bf16[8,64,512]{2,1,0:T(8,128)(2,1)} custom-call(bf16[64,512]{1,0:T(8,128)(2,1)} %copy_bitcast_fusion.a_ref, bf16[512,4096]{1,0:T(8,128)(2,1)} %w_ref.1), custom_call_target="tpu_custom_call" | custom-call | tf_op jit(solution)/shard_map/pallas_call | solution.py:242
  124.6 1.1 reduce_sum.58
  125.7 0.6 fusion.41
  (13 shorter events, 0.3 us)
Async XLA Ops:
  0.6 20.7 %copy-start = (bf16[4096,128]{1,0:T(8,128)(2,1)S(1)}, bf16[4096,128]{1,0:T(8,128)(2,1)}, u32[]{:S(2)}) copy-start(bf16[4096,128]{1,0:T(8,128)(2,1)} %param.21) | copy-start | bytes 3145732
  15.6 8.9 %copy-start.1 = (bf16[64,4096]{1,0:T(8,128)(2,1)S(1)}, bf16[64,4096]{1,0:T(8,128)(2,1)}, u32[]{:S(2)}) copy-start(bf16[64,4096]{1,0:T(8,128)(2,1)} %get-tuple-element.9) | copy-start | bytes 1572868

commit v20 on v19

--- a/solution.py
+++ b/solution.py
@@ -453,6 +453,36 @@
     return acc.astype(jnp.bfloat16), st.astype(jnp.bfloat16)
 
 
+def merge_three(a, b, c, rows):
+    parts = [p.astype(jnp.float32) for p in (a, b, c)]
+    maxima = [p[rows : rows + 1] + p[rows + 1 : rows + 2] for p in parts]
+    totals = [p[rows + 2 : rows + 3] + p[rows + 3 : rows + 4] for p in parts]
+    top = jnp.maximum(jnp.maximum(maxima[0], maxima[1]), maxima[2])
+    scales = [jnp.exp(m - top) for m in maxima]
+    total = totals[0] * scales[0] + totals[1] * scales[1] + totals[2] * scales[2]
+    third = rows // 3
+    sub_all = lax.broadcasted_iota(jnp.int32, (rows, rows), 0)
+    cols = jnp.transpose(
+        jnp.where(sub_all < third, scales[0], jnp.where(sub_all < 2 * third, scales[1], scales[2]))
+    )
+    acc = (
+        parts[0][0:rows] * cols[:, 0:1]
+        + parts[1][0:rows] * cols[:, third : third + 1]
+        + parts[2][0:rows] * cols[:, 2 * third : 2 * third + 1]
+    )
+    sub = lax.broadcasted_iota(jnp.int32, (16, rows), 0)
+    top_hi = top.astype(jnp.bfloat16).astype(jnp.float32)
+    tot_hi = total.astype(jnp.bfloat16).astype(jnp.float32)
+    st = jnp.where(
+        sub == 0,
+        top,
+        jnp.where(
+            sub == 1, top - top_hi, jnp.where(sub == 2, total, jnp.where(sub == 3, total - tot_hi, 0.0))
+        ),
+    )
+    return acc.astype(jnp.bfloat16), st.astype(jnp.bfloat16)
+
+
 def relay_reduce_kernel(
     nx, nz, x_ref, y_ref, rp, rm, bp, bm, col, sp_send, sp_recv, sm_send, sm_recv, sx_send, sx_recv
 ):
@@ -510,8 +540,12 @@
     for i in range(nx):
         last[(1, i)].wait_recv()
         last[(-1, i)].wait_recv()
-        merge_into(col.at[i], x_ref.at[i * nz + z], rp.at[steps, i])
-        merge_into(col.at[i], col.at[i], rm.at[steps, i])
+        for h in range(2):
+            acc, st = merge_three(
+                x_ref.at[i * nz + z][h], rp.at[steps, i][h], rm.at[steps, i][h], rows
+            )
+            col[i, h, 0:rows] = acc
+            col[i, h, rows:] = st
     for k in range(1, nx):
         target = lax.rem(x + k, nx)
         c = pltpu.make_async_remote_copy(

time: 127 us -> 128 us (level)
  no operation moved by 1% of the time
where the time goes in v20:
time: 128 us; the launch traced here: 127 us
  Pallas kernels  107 us (84%)
  other arithmetic  8.76 us (7%)
  matrix products  6.68 us (5%)
  local copies, waits for them, and re-layouts  3.58 us (3%)
  between operations  1.5 us (1%)
    pallas_call x1, Pallas kernels, relay_gather(): pl.pallas_call(functools.partial(relay_gather_kernel, nx, nz), in_specs=[...  33.8 us
    pallas_call x1, Pallas kernels, relay_reduce(): pl.pallas_call(functools.partial(relay_reduce_kernel, nx, nz), in_specs=[...  32.1 us
    pallas_call x1, Pallas kernels, mp_scatter(): pl.pallas_call(functools.partial(mp_scatter_kernel, n), in_specs=[vmem, v...  18.9 us
    pallas_call x1, Pallas kernels, mp_gather(): pl.pallas_call(functools.partial(mp_gather_kernel, n, span), in_specs=[vm...  14.9 us
    pallas_call x1, Pallas kernels, passage_attention(): pl.pallas_call(functools.partial(passage_kernel, nx, nz), in_specs=[pl.Bl...  7.2 us
    dot_general x1, matrix products, local(): jnp.dot(normalized_hidden, w_query, preferred_element_type=jnp.float32)  3.1 us

profile of v20, /device:TPU:1, one launch (start us, length us, event | category | flops | bytes accessed | tf_op | source)
XLA Modules:
  0.0 127.4 jit_solution(2753915096010905886)
XLA Ops:
  0.6 0.0 copy-start
  0.7 14.9 %shard_map.149 = (bf16[64,4096]{1,0:T(8,128)(2,1)}, s32[8,32]{1,0:T(8,128)}, s32[128,1]{1,0:T(8,128)}) custom-call(bf16[32,512]{1,0:T(8,128)(2,1)} %p_ref.1, bf16[32,512]{1,0:T(8,128)(2,1)} %r_ref.1, s32[1,32]{1,0:T(1,128)} %bitcast.61, s32[1,32]{1,0:T(1,128)} %bitcast.62, s32[1,32]{1,0:T(1,128)} %bitcast.63, s32[1,32]{1,0:T(1,128)} %bitcast.64, ...), custom_call_target="tpu_custom_call" | custom-call | tf_op jit(solution)/shard_map/pallas_call | solution.py:185
  15.6 0.0 copy-start.1
  15.6 1.3 slice.84
  17.5 1.2 fusion.1
  18.7 0.1 fusion.34
  18.8 0.7 compare_bitcast_fusion
  19.5 0.1 maximum_bitcast_fusion.1
  19.6 0.1 maximum_bitcast_fusion
  19.7 0.6 pad_maximum_fusion.6.rot_ref
  20.3 0.8 slice_bitcast_fusion.5
  21.1 0.1 add_compare_fusion
  21.2 0.1 add_convert_fusion.1
  21.3 0.1 fusion.24
  21.3 0.0 copy-done
  21.3 1.4 %convolution_convert_fusion = bf16[64,128]{1,0:T(8,128)(2,1)S(1)} fusion(bf16[4096,128]{1,0:T(8,128)(2,1)S(1)} %copy-done, bf16[64,4096]{1,0:T(8,128)(2,1)} %get-tuple-element.9, f32[4096]{0:T(1024)} %param.18, f32[64]{0:T(128)S(1)} %add_rsqrt_fusion), kind=kOutput, calls=%fused_computation.5 | convolution fusion | flops 68165632 | bytes 1605888 | tf_op jit(solution)/shard_map/dot_general | solution.py:650
  22.7 1.7 %convolution_bitcast_fusion = f32[64,1,128]{2,0,1:T(8,128)S(1)} fusion(bf16[4096,128]{1,0:T(8,128)(2,1)} %param.20, bf16[64,4096]{1,0:T(8,128)(2,1)} %get-tuple-element.9, f32[4096]{0:T(1024)} %param.18, f32[64]{0:T(128)S(1)} %add_rsqrt_fusion), kind=kOutput, calls=%fused_computation.4 | convolution fusion | flops 68157440 | bytes 1622272 | tf_op jit(solution)/shard_map/dot_general | solution.py:642
  24.5 0.0 copy-done.1
  24.5 3.1 %fusion.37 = f32[64,512]{1,0:T(8,128)S(1)} fusion(bf16[4096,512]{1,0:T(8,128)(2,1)} %param.19, bf16[64,4096]{1,0:T(8,128)(2,1)S(1)} %copy-done.1, f32[4096]{0:T(1024)} %param.18, f32[64]{0:T(128)S(1)} %add_rsqrt_fusion), kind=kOutput, calls=%fused_computation.77 | convolution fusion | flops 269484032 | bytes 4866304 | tf_op jit(solution)/shard_map/dot_general | solution.py:633
  27.7 0.2 fusion.17
  27.9 0.1 fusion.26
  27.9 0.6 pad_maximum_fusion.3.fresh_ref
  28.6 0.2 multiply_cosine_fusion.1
  28.8 0.1 fusion.40
  28.9 0.3 fusion.42
  29.2 0.1 copy.35
  29.3 0.1 copy.36
  29.3 0.7 pad_maximum_fusion.x_ref
  30.1 0.2 fusion.18
  30.3 33.8 %shard_map.150 = (bf16[32,2,128,128]{3,2,1,0:T(8,128)(2,1)}, bf16[1024,128]{1,0:T(8,128)(2,1)}, bf16[1024,128]{1,0:T(8,128)(2,1)}) custom-call(bf16[2,128,128]{2,1,0:T(8,128)(2,1)} %pad_maximum_fusion.x_ref, bf16[1024,128]{1,0:T(8,128)(2,1)} %bitcast.54, bf16[1024,128]{1,0:T(8,128)(2,1)} %bitcast.55, bf16[32,256]{1,0:T(8,128)(2,1)} %pad_maximum_fusion.3.fresh_ref, ...), custom_call_target="tpu_custom_call" | custom-call | tf_op jit(solution)/shard_map/pallas_call | solution.py:406
  64.0 7.2 %shard_map.151 = bf16[64,144,128]{2,1,0:T(8,128)(2,1)} custom-call(s32[8,32]{1,0:T(8,128)} %get-tuple-element.8.meta_ref.flags_ref, bf16[64,128,128]{2,1,0:T(8,128)(2,1)} %bitcast.52, bf16[1024,128]{1,0:T(8,128)(2,1)} %get-tuple-element.11.k_ref, bf16[1024,128]{1,0:T(8,128)(2,1)} %get-tuple-element.12.v_ref, s32[128,1]{1,0:T(8,128)} %get-tuple-element.13.lim_ref), custom_call_target="tpu_custom_call" | custom-call | tf_op jit(solution)/shard_map/pallas_call | solution.py:100
  71.2 32.1 %shard_map.152 = bf16[4,2,144,128]{3,2,1,0:T(8,128)(2,1)} custom-call(bf16[32,2,144,128]{3,2,1,0:T(8,128)(2,1)} %bitcast.51), custom_call_target="tpu_custom_call" | custom-call | tf_op jit(solution)/shard_map/pallas_call | solution.py:572
  103.4 0.7 slice_convert_fusion
  104.1 0.1 reduce_max.21
  104.2 0.1 copy.37
  104.3 0.1 copy.38
  104.4 0.1 sub.38
  104.6 1.2 multiply_reduce_fusion
  105.7 0.1 reduce_sum.56
  105.8 0.1 copy.41
  105.9 0.8 copy_bitcast_fusion.a_ref
  106.7 18.9 %shard_map.153 = bf16[8,64,512]{2,1,0:T(8,128)(2,1)} custom-call(bf16[64,512]{1,0:T(8,128)(2,1)} %copy_bitcast_fusion.a_ref, bf16[512,4096]{1,0:T(8,128)(2,1)} %w_ref.1), custom_call_target="tpu_custom_call" | custom-call | tf_op jit(solution)/shard_map/pallas_call | solution.py:242
  125.6 1.1 reduce_sum.58
  126.8 0.6 fusion.41
  (13 shorter events, 0.3 us)
Async XLA Ops:
  0.6 20.7 %copy-start = (bf16[4096,128]{1,0:T(8,128)(2,1)S(1)}, bf16[4096,128]{1,0:T(8,128)(2,1)}, u32[]{:S(2)}) copy-start(bf16[4096,128]{1,0:T(8,128)(2,1)} %param.21) | copy-start | bytes 3145732
  15.6 8.9 %copy-start.1 = (bf16[64,4096]{1,0:T(8,128)(2,1)S(1)}, bf16[64,4096]{1,0:T(8,128)(2,1)}, u32[]{:S(2)}) copy-start(bf16[64,4096]{1,0:T(8,128)(2,1)} %get-tuple-element.9) | copy-start | bytes 1572868

commit v21 on v19

--- a/solution.py
+++ b/solution.py
@@ -74,9 +74,9 @@
         out_ref[b, 0:rows] = jnp.dot(
             weights.astype(jnp.bfloat16), v_ref[...], preferred_element_type=jnp.float32
         ).astype(out_ref.dtype)
-        m_row = jnp.transpose(jnp.broadcast_to(maxima, (rows, rows)))[0:16]
-        l_row = jnp.transpose(jnp.broadcast_to(totals, (rows, rows)))[0:16]
-        out_ref[b, rows:] = split(m_row, l_row)
+        lane = lax.broadcasted_iota(jnp.int32, (rows, rows), 1)
+        both = jnp.transpose(jnp.where(lane < rows // 2, maxima, totals))
+        out_ref[b, rows:] = split(both[0:16], both[rows // 2 : rows // 2 + 16])
 
     def body(b, carry):
         flag = flags_ref[4 + b % 2, b // 2]

time: 127 us -> 128 us (level)
    pallas_call x1, Pallas kernels: 31.5 us -> 32.8 us  [relay_reduce(): pl.pallas_call(functools.partial(relay_reduce_kernel, nx, nz), in_specs=[...]
where the time goes in v21:
time: 128 us
  Pallas kernels  107 us (84%)
  other arithmetic  8.76 us (7%)
  matrix products  6.68 us (5%)
  local copies, waits for them, and re-layouts  3.58 us (3%)
  between operations  1.5 us (1%)
    pallas_call x1, Pallas kernels, relay_gather(): pl.pallas_call(functools.partial(relay_gather_kernel, nx, nz), in_specs=[...  33.8 us
    pallas_call x1, Pallas kernels, relay_reduce(): pl.pallas_call(functools.partial(relay_reduce_kernel, nx, nz), in_specs=[...  32.8 us
    pallas_call x1, Pallas kernels, mp_scatter(): pl.pallas_call(functools.partial(mp_scatter_kernel, n), in_specs=[vmem, v...  19.5 us
    pallas_call x1, Pallas kernels, mp_gather(): pl.pallas_call(functools.partial(mp_gather_kernel, n, span), in_specs=[vm...  14.9 us
    pallas_call x1, Pallas kernels, passage_attention(): pl.pallas_call(functools.partial(passage_kernel, nx, nz), in_specs=[pl.Bl...  6.17 us
    dot_general x1, matrix products, local(): jnp.dot(normalized_hidden, w_query, preferred_element_type=jnp.float32)  3.1 us

profile of v21, /device:TPU:1, one launch (start us, length us, event | category | flops | bytes accessed | tf_op | source)
XLA Modules:
  0.0 127.7 jit_solution(2782450870817412975)
XLA Ops:
  0.6 0.0 copy-start
  0.7 14.9 %shard_map.149 = (bf16[64,4096]{1,0:T(8,128)(2,1)}, s32[8,32]{1,0:T(8,128)}, s32[128,1]{1,0:T(8,128)}) custom-call(bf16[32,512]{1,0:T(8,128)(2,1)} %p_ref.1, bf16[32,512]{1,0:T(8,128)(2,1)} %r_ref.1, s32[1,32]{1,0:T(1,128)} %bitcast.61, s32[1,32]{1,0:T(1,128)} %bitcast.62, s32[1,32]{1,0:T(1,128)} %bitcast.63, s32[1,32]{1,0:T(1,128)} %bitcast.64, ...), custom_call_target="tpu_custom_call" | custom-call | tf_op jit(solution)/shard_map/pallas_call | solution.py:185
  15.6 0.0 copy-start.1
  15.6 1.3 slice.84
  17.5 1.2 fusion.1
  18.7 0.1 fusion.34
  18.8 0.7 compare_bitcast_fusion
  19.5 0.1 maximum_bitcast_fusion.1
  19.6 0.1 maximum_bitcast_fusion
  19.7 0.6 pad_maximum_fusion.6.rot_ref
  20.3 0.8 slice_bitcast_fusion.5
  21.1 0.1 add_compare_fusion
  21.2 0.1 add_convert_fusion.1
  21.3 0.1 fusion.24
  21.3 0.0 copy-done
  21.3 1.4 %convolution_convert_fusion = bf16[64,128]{1,0:T(8,128)(2,1)S(1)} fusion(bf16[4096,128]{1,0:T(8,128)(2,1)S(1)} %copy-done, bf16[64,4096]{1,0:T(8,128)(2,1)} %get-tuple-element.9, f32[4096]{0:T(1024)} %param.18, f32[64]{0:T(128)S(1)} %add_rsqrt_fusion), kind=kOutput, calls=%fused_computation.5 | convolution fusion | flops 68165632 | bytes 1605888 | tf_op jit(solution)/shard_map/dot_general | solution.py:616
  22.7 1.7 %convolution_bitcast_fusion = f32[64,1,128]{2,0,1:T(8,128)S(1)} fusion(bf16[4096,128]{1,0:T(8,128)(2,1)} %param.20, bf16[64,4096]{1,0:T(8,128)(2,1)} %get-tuple-element.9, f32[4096]{0:T(1024)} %param.18, f32[64]{0:T(128)S(1)} %add_rsqrt_fusion), kind=kOutput, calls=%fused_computation.4 | convolution fusion | flops 68157440 | bytes 1622272 | tf_op jit(solution)/shard_map/dot_general | solution.py:608
  24.5 0.0 copy-done.1
  24.5 3.1 %fusion.37 = f32[64,512]{1,0:T(8,128)S(1)} fusion(bf16[4096,512]{1,0:T(8,128)(2,1)} %param.19, bf16[64,4096]{1,0:T(8,128)(2,1)S(1)} %copy-done.1, f32[4096]{0:T(1024)} %param.18, f32[64]{0:T(128)S(1)} %add_rsqrt_fusion), kind=kOutput, calls=%fused_computation.77 | convolution fusion | flops 269484032 | bytes 4866304 | tf_op jit(solution)/shard_map/dot_general | solution.py:599
  27.7 0.2 fusion.17
  27.9 0.1 fusion.26
  27.9 0.6 pad_maximum_fusion.3.fresh_ref
  28.6 0.2 multiply_cosine_fusion.1
  28.8 0.1 fusion.40
  28.9 0.3 fusion.42
  29.2 0.1 copy.35
  29.3 0.1 copy.36
  29.3 0.7 pad_maximum_fusion.x_ref
  30.1 0.2 fusion.18
  30.3 33.8 %shard_map.150 = (bf16[32,2,128,128]{3,2,1,0:T(8,128)(2,1)}, bf16[1024,128]{1,0:T(8,128)(2,1)}, bf16[1024,128]{1,0:T(8,128)(2,1)}) custom-call(bf16[2,128,128]{2,1,0:T(8,128)(2,1)} %pad_maximum_fusion.x_ref, bf16[1024,128]{1,0:T(8,128)(2,1)} %bitcast.54, bf16[1024,128]{1,0:T(8,128)(2,1)} %bitcast.55, bf16[32,256]{1,0:T(8,128)(2,1)} %pad_maximum_fusion.3.fresh_ref, ...), custom_call_target="tpu_custom_call" | custom-call | tf_op jit(solution)/shard_map/pallas_call | solution.py:406
  64.0 6.2 %shard_map.151 = bf16[64,144,128]{2,1,0:T(8,128)(2,1)} custom-call(s32[8,32]{1,0:T(8,128)} %get-tuple-element.8.meta_ref.flags_ref, bf16[64,128,128]{2,1,0:T(8,128)(2,1)} %bitcast.52, bf16[1024,128]{1,0:T(8,128)(2,1)} %get-tuple-element.11.k_ref, bf16[1024,128]{1,0:T(8,128)(2,1)} %get-tuple-element.12.v_ref, s32[128,1]{1,0:T(8,128)} %get-tuple-element.13.lim_ref), custom_call_target="tpu_custom_call" | custom-call | tf_op jit(solution)/shard_map/pallas_call | solution.py:100
  70.2 32.8 %shard_map.152 = bf16[4,2,144,128]{3,2,1,0:T(8,128)(2,1)} custom-call(bf16[32,2,144,128]{3,2,1,0:T(8,128)(2,1)} %bitcast.51), custom_call_target="tpu_custom_call" | custom-call | tf_op jit(solution)/shard_map/pallas_call | solution.py:538
  103.0 0.7 slice_convert_fusion
  103.8 0.1 reduce_max.21
  103.9 0.1 copy.37
  104.0 0.1 copy.38
  104.1 0.1 sub.38
  104.3 1.2 multiply_reduce_fusion
  105.4 0.1 reduce_sum.56
  105.5 0.1 copy.41
  105.6 0.8 copy_bitcast_fusion.a_ref
  106.4 19.5 %shard_map.153 = bf16[8,64,512]{2,1,0:T(8,128)(2,1)} custom-call(bf16[64,512]{1,0:T(8,128)(2,1)} %copy_bitcast_fusion.a_ref, bf16[512,4096]{1,0:T(8,128)(2,1)} %w_ref.1), custom_call_target="tpu_custom_call" | custom-call | tf_op jit(solution)/shard_map/pallas_call | solution.py:242
  125.9 1.1 reduce_sum.58
  127.0 0.6 fusion.41
  (13 shorter events, 0.3 us)
Async XLA Ops:
  0.6 20.7 %copy-start = (bf16[4096,128]{1,0:T(8,128)(2,1)S(1)}, bf16[4096,128]{1,0:T(8,128)(2,1)}, u32[]{:S(2)}) copy-start(bf16[4096,128]{1,0:T(8,128)(2,1)} %param.21) | copy-start | bytes 3145732
  15.6 8.9 %copy-start.1 = (bf16[64,4096]{1,0:T(8,128)(2,1)S(1)}, bf16[64,4096]{1,0:T(8,128)(2,1)}, u32[]{:S(2)}) copy-start(bf16[64,4096]{1,0:T(8,128)(2,1)} %get-tuple-element.9) | copy-start | bytes 1572868
